TPU v7x, 512 devices: a whole 4x8x8 slice. The times are simulated.
512 devices in a mesh: sec: 4 (over x), dom: 128 (over z, y, core).
Axes of the slice: x: 4, y: 8, z: 8, core: 2. Of those that a mesh axis runs over, the one named last changes fastest.
Arguments:
- fields: float32 [4, 64, 131072], P(None, None, ('sec', 'dom')), may hold values from -6 to 6
- source_map: int32 [131072], P(('sec', 'dom')), may hold values from 0 to 255
- new_owner: int32 [32768], P(('sec', 'dom')), may hold values from 0 to 127, as said below
- send_list: int32 [49152], P(('sec', 'dom')), may hold values from -1 to 1535, as said below
- face_slot: int32 [6, 131072], P(None, ('sec', 'dom')), may hold values from -1 to 1631, as said below
Outputs:
- advanced: float32 [4, 64, 131072], P(None, None, ('sec', 'dom'))
Inputs may be any that keep to these rules, and one draw needn't show every extreme that they name: source_map names a cell block of the flow device with the same dom index. new_owner names a device of the same section within 2 dom indices; two devices trade as many blocks each way, at most 4; in every section some device trades exactly 4 with each of its 4 nearby devices. send_list holds, for each device, 4 lists of 24 entries for the offsets -2 to -1 and 1 to 2; an entry f * 256 + e names face f of local element e; a list for a device inside the section is full, one for a device outside it is -1. face_slot names for every element face the touching face: the opposite end along the same direction, nodes in the same order, on the same device or in the lists of a device within 2; -1 marks the outer boundary.
All inputs are finite; a program needn't handle non-finite values.
Results may differ from a plain program's by a relative error of at most 0.0003.
Values sent between devices are 32-bit elements; how exact they have to be, the bound alone decides.
No kernel may reach another device: no remote copies, remote signals or barrier semaphores. Data moves between devices by JAX's collectives and lax.ppermute only.
A program may use at most 64 MiB of HBM per device.

v0:
```python
import functools

import jax
import jax.numpy as jnp
import numpy as np
from jax import lax
from jax.experimental import pallas as pl
from jax.experimental.pallas import tpu as pltpu
from jax.sharding import PartitionSpec as P


FACE_CAP = 24
PIECES = 3
LANES = 128
ELEMENTS = 256
ROWS = 256
TRACE_ROWS = 48
LIFT = 3.0
TIME_STEP = 0.12
SEGMENT_CARRY = [
    0.0,
    -567301805773.0 / 1357537059087.0,
    -2404267990393.0 / 2016746695238.0,
    -3550918686646.0 / 2091501179385.0,
    -1275806237668.0 / 842570457699.0,
]
SEGMENT_WEIGHTS = [
    1432997174477.0 / 9575080441755.0,
    5161836677717.0 / 13612068292357.0,
    1720146321549.0 / 2090206949498.0,
    3134564353537.0 / 4481467310338.0,
    2277821191437.0 / 14882151754819.0,
]
BF = jnp.bfloat16
F32 = jnp.float32


def node_derivative():
    points = np.array([-1.0, -1.0 / np.sqrt(5.0), 1.0 / np.sqrt(5.0), 1.0])
    products = np.array(
        [np.prod([points[row] - points[col] for col in range(4) if col != row]) for row in range(4)]
    )
    matrix = np.zeros((4, 4))
    for row in range(4):
        for col in range(4):
            if row != col:
                matrix[row, col] = products[row] / (products[col] * (points[row] - points[col]))
        matrix[row, row] = -np.sum(matrix[row])
    return matrix


def along(matrix, direction):
    eye = np.eye(4)
    parts = [eye, eye, eye]
    parts[direction] = matrix
    return np.kron(np.kron(parts[0], parts[1]), parts[2])


def face_nodes(face):
    direction, side = divmod(face, 2)
    index = np.arange(64).reshape(4, 4, 4)
    return np.take(index, 3 * side, axis=direction).reshape(-1)


def interior_matrix():
    derivative = node_derivative()
    total = np.zeros((256, 256))
    for a in range(3):
        d = along(derivative, a)
        total[0:64, 64 * (a + 1) : 64 * (a + 2)] -= d
        total[64 * (a + 1) : 64 * (a + 2), 0:64] -= d
    for face in range(6):
        a, side = divmod(face, 2)
        sign = 2.0 * side - 1.0
        nodes = face_nodes(face)
        va = 64 * (a + 1) + nodes
        total[nodes, nodes] -= LIFT
        total[nodes, va] += LIFT * sign
        total[va, va] -= LIFT
        total[va, nodes] += LIFT * sign
        for b in range(3):
            if b != a:
                vb = 64 * (b + 1) + nodes
                total[vb, vb] -= LIFT
    return total


def trace_matrix():
    total = np.zeros((6 * TRACE_ROWS, 256))
    for face in range(6):
        a, side = divmod(face, 2)
        sign = 2.0 * side - 1.0
        nodes = face_nodes(face)
        rows = TRACE_ROWS * face + np.arange(16)
        total[rows, nodes] = 1.0
        total[rows, 64 * (a + 1) + nodes] = sign
        for number, b in enumerate([b for b in range(3) if b != a]):
            total[rows + 16 * (number + 1), 64 * (b + 1) + nodes] = 1.0
    return total


def lift_matrix():
    total = np.zeros((256, 6 * TRACE_ROWS))
    for face in range(6):
        a, side = divmod(face, 2)
        sign = 2.0 * side - 1.0
        nodes = face_nodes(face)
        cols = TRACE_ROWS * face + np.arange(16)
        total[nodes, cols] = 1.0
        total[64 * (a + 1) + nodes, cols] = -sign
        for number, b in enumerate([b for b in range(3) if b != a]):
            total[64 * (b + 1) + nodes, cols + 16 * (number + 1)] = 1.0
    return total


def two_terms(matrix):
    high = matrix.astype(np.float32).astype(BF)
    low = (matrix - high.astype(np.float64)).astype(np.float32).astype(BF)
    return high, low


def mm(a, b):
    return lax.dot_general(a, b, (((1,), (0,)), ((), ())), preferred_element_type=F32)


def mm_nt(a, b):
    return lax.dot_general(a, b, (((1,), (1,)), ((), ())), preferred_element_type=F32)


def split(x):
    high = x.astype(BF)
    return high, (x - high.astype(F32)).astype(BF)


def one_hot(mask):
    return jnp.where(mask, 1.0, 0.0).astype(BF)


def lane_iota(shape):
    return lax.broadcasted_iota(jnp.int32, shape, 1)


def row_iota(shape):
    return lax.broadcasted_iota(jnp.int32, shape, 0)


def picked_traces(state, pick, kinds, trace):
    high, low = split(state)
    chosen = jnp.concatenate([mm(high, pick).astype(BF), mm(low, pick).astype(BF)], axis=1)
    shown = mm(trace, chosen)
    return of_kind(shown[:, :256] + shown[:, 256:], kinds)


def of_kind(shown, kinds):
    total = jnp.zeros((TRACE_ROWS, 256), F32)
    for face in range(6):
        part = shown[TRACE_ROWS * face : TRACE_ROWS * (face + 1)]
        total = total + jnp.where(kinds[face : face + 1] > 0, part, 0.0)
    return total


def arrived(toward, across, back):
    return across, toward + back


def by_kind(came, sent, kinds):
    far = lane_iota((TRACE_ROWS, LANES)) < PIECES * FACE_CAP
    from_left, from_right = sides(*came)
    own_left, own_right = sides(*sent)
    got = jnp.concatenate(
        [jnp.where(far, from_right, own_left), jnp.where(far, from_left, own_right)], axis=1
    )
    masked = jnp.concatenate(
        [jnp.where(kinds[face : face + 1] > 0, got, 0.0) for face in range(6)], axis=0
    )
    return jnp.concatenate(split(masked), axis=0)


def far_rates(stacks, place, lift_two):
    return mm(lift_two, mm(stacks, place).astype(BF))


def sides(first, second):
    odd = ((lax.axis_index("dom") >> 1) & 1) == 1
    return jnp.where(odd, second, first), jnp.where(odd, first, second)


def core_number():
    return lax.axis_index("dom") & 1


def chip_halves(mine, other):
    first = core_number() == 0
    return jnp.where(first, mine, other), jnp.where(first, other, mine)


def difference_along(stride):
    row, col = row_iota((64, 64)), lane_iota((64, 64))
    at, step = (row // stride) & 3, ((col // stride) & 3) - ((row // stride) & 3)
    inner = jnp.where(step == 1, 0.5, jnp.where(step == -1, -0.5, 0.0))
    lower = jnp.where(step == 1, 1.0, jnp.where(step == 0, -1.0, 0.0))
    upper = jnp.where(step == 0, 1.0, jnp.where(step == -1, -1.0, 0.0))
    value = jnp.where(at == 0, lower, jnp.where(at == 3, upper, inner))
    return jnp.where(col - row == step * stride, value, 0.0).astype(BF)


def lamb_kernel(packed, lamb_out):
    slopes = jnp.concatenate([difference_along(stride) for stride in (16, 4, 1)], axis=0)
    v = [packed[64 * a : 64 * (a + 1)] for a in range(3)]
    high, low = split(jnp.concatenate(v, axis=1))
    found = mm(slopes, high) + mm(slopes, low)

    def slope(component, direction):
        return found[64 * direction : 64 * direction + 64, 256 * component : 256 * component + 256]

    w = [
        slope(2, 1) - slope(1, 2),
        slope(0, 2) - slope(2, 0),
        slope(1, 0) - slope(0, 1),
    ]
    rho = packed[192:256]
    lamb_out[0:64] = rho * (w[1] * v[2] - w[2] * v[1])
    lamb_out[64:128] = rho * (w[2] * v[0] - w[0] * v[2])
    lamb_out[128:192] = rho * (w[0] * v[1] - w[1] * v[0])


def depart_kernel(mine, other, first_out, second_out, chip_out, select_out, keep_out, arrive_out):
    low, high = chip_halves(mine[...], other[...])
    chip_out[:, 0:256] = low
    chip_out[:, 256:512] = high
    first = (lax.axis_index("dom") & -2).astype(F32)
    spread = one_hot((lane_iota((64, 256)) >> 2) == row_iota((64, 256)))
    before = one_hot(row_iota((256, 256)) < lane_iota((256, 256)))
    row8 = row_iota((8, 256))
    wanted = jnp.where(row8 == 0, 0, jnp.where(row8 < 3, row8 - 3, row8 - 2)).astype(F32)
    members = []
    for number, half in enumerate((low, high)):
        owner = half[263:264, 0:64] - (first + number)
        owner = jnp.clip(jnp.broadcast_to(owner, (8, 64)), -8.0, 8.0).astype(BF)
        member = (mm(owner, spread) == wanted) & (row8 < 5)
        members.append(jnp.where(member, 1.0, 0.0))
    members = jnp.concatenate(members, axis=0)
    rank = mm(members.astype(BF), before)
    count = jnp.sum(members, axis=1, keepdims=True)

    def group(device, offset):
        return 8 * device + {0: 0, -2: 1, -1: 2, 1: 3, 2: 4}[offset]

    def start(device, offset):
        total = jnp.zeros((1, 1), F32)
        for number in (0, -2, -1, 1, 2):
            if number == offset:
                return total
            at = group(device, number)
            total = total + count[at : at + 1]

    def target(device, moves):
        total = jnp.full((1, 256), -1.0, F32)
        for offset, base in moves:
            at = group(device, offset)
            total = total + members[at : at + 1] * (rank[at : at + 1] + (base + 1.0))
        return total

    low_target = target(0, ((-2, 0.0), (-1, 16.0), (2, 48.0)))
    high_target = target(1, ((-2, 32.0), (1, 64.0), (2, 80.0)))
    number = row_iota((96, 256)).astype(F32)
    select = jnp.concatenate([one_hot(low_target == number), one_hot(high_target == number)], axis=1)
    select_out[...] = select
    cells = jnp.concatenate([low[0:256], high[0:256]], axis=1)
    cells_high, cells_low = split(cells)
    sent = mm_nt(select, cells_high) + mm_nt(select, cells_low)
    first_out[...], second_out[...] = sides(sent[0:48], sent[48:96])

    low_place = target(0, ((0, 0.0), (1, 256.0 + start(1, -1))))
    high_place = target(1, ((0, 256.0), (-1, start(0, 1))))
    number = row_iota((512, 256)).astype(F32)
    keep_out[:, 0:256] = one_hot(low_place == number)
    keep_out[:, 256:512] = one_hot(high_place == number)
    column = lane_iota((16, 512)).astype(F32)
    number = row_iota((16, 512)).astype(F32)
    for piece, (device, offset) in enumerate(((0, -2), (0, -1), (1, -2), (0, 2), (1, 1), (1, 2))):
        at = group(device, offset)
        begin = start(device, offset) + 256.0 * device
        arrive_out[16 * piece : 16 * piece + 16, :] = one_hot(
            (column - begin == number) & (number < count[at : at + 1])
        )


def tables_kernel(
    chip, keep,
    kept_out, local_out, place_out, own_place_out, kinds_out, pick_out, send_kinds_out, meet_out,
):
    high, low = split(chip[0:256])
    kept_out[...] = mm_nt(high, keep[...]) + mm_nt(low, keep[...])
    row = row_iota((256, 256))
    ones = jnp.ones((8, 256), BF)
    kinds = [jnp.zeros((1, 256), F32)] * 6
    places = []
    for device in range(2):
        place = jnp.zeros((256, 256), F32)
        for face in range(6):
            where = chip[256 + face : 257 + face, 256 * device : 256 * (device + 1)].astype(jnp.int32)
            local_out[6 * device + face] = one_hot(where - ELEMENTS * (face ^ 1) == row)
            n = where - 6 * ELEMENTS
            if device == 0:
                entry = jnp.where(n < 48, n + 128, jnp.where(n < 72, n + 24, n - 72))
            else:
                entry = jnp.where(n < 48, n + 176, n - 24)
            hit = jnp.where(jnp.where(n < 0, -1, entry) == row, 1.0, 0.0)
            place = place + hit
            kinds[face] = kinds[face] + mm_nt(ones, hit.astype(BF))[0:1]
        places.append(place)
    own_place_out[...] = jnp.where(core_number() == 0, places[0], places[1]).astype(BF)
    place = jnp.concatenate(places, axis=1).astype(BF)
    place_out[...] = place
    kinds_out[...] = jnp.concatenate(kinds + [jnp.zeros((2, 256), F32)], axis=0)
    lane = lane_iota((8, LANES))
    lists = [
        jnp.broadcast_to(chip[263:264, 256 * device + 128 : 256 * device + 256], (8, LANES))
        for device in range(2)
    ]
    left = jnp.where(lane < 48, lists[0], pltpu.roll(lists[1], 48, 1))
    right = jnp.where(
        lane < 24,
        pltpu.roll(lists[0], LANES - 72, 1),
        jnp.where(lane < 72, pltpu.roll(lists[1], LANES - 24, 1), pltpu.roll(lists[0], 24, 1)),
    )
    names = jnp.concatenate(
        [jnp.where(lane < 96, left, -1.0), jnp.where(lane < 96, right, -1.0)], axis=1
    ).astype(jnp.int32)
    wide = lane_iota((8, 256))
    second = ((wide >= 48) & (wide < 128)) | ((wide >= 152) & (wide < 200))
    column = jnp.where(names < 0, -1, (names & 255) + jnp.where(second, 256, 0))
    pick = one_hot(column[0:1] == row_iota((512, 256)))
    pick_out[...] = pick
    meet_out[...] = mm(place, pick).astype(BF)
    send_kinds_out[...] = jnp.where((names >> 8) == row_iota((8, 256)), 1.0, 0.0)


def arrive_kernel(
    toward, across, back, kept, arrive, pick, send_kinds, trace, state_out, first_out, second_out
):
    got = jnp.concatenate(sides(*arrived(toward[...], across[...], back[...])), axis=0)
    high, low = split(jnp.transpose(got))
    state = kept[...] + (mm(high, arrive[...]) + mm(low, arrive[...]))
    state_out[...] = state
    sent = picked_traces(state, pick[...], send_kinds[...], trace[...])
    first_out[...], second_out[...] = sides(sent[:, :LANES], sent[:, LANES:])


def force_kernel(first, second, third, packed, after, out):
    lamb = first[...] + second[...] + third[...]
    high, low = split(lamb)
    source = one_hot(packed[262:263].astype(jnp.int32) == row_iota((256, 256)))
    out[...] = mm(high, source) + mm(low, source)


def force_depart_kernel(
    mine, other, select, keep, own_first, own_second, first_out, second_out, kept_out
):
    force = jnp.concatenate(chip_halves(mine[...], other[...]), axis=1)
    high, low = split(force)
    sent = mm_nt(select[...], high) + mm_nt(select[...], low)
    pieces = sides(sent[0:48], sent[48:96])
    for out, piece, own in ((first_out, pieces[0], own_first), (second_out, pieces[1], own_second)):
        out[:, 0:192] = piece
        out[:, 192:256] = jnp.zeros((48, 64), F32)
        out[:, 256:384] = own[...]
    kept_out[...] = mm_nt(high, keep[...]) + mm_nt(low, keep[...])


def near_rates(state, near, interior, trace, lift_two):
    high, low = split(state)
    rates = mm(interior, jnp.concatenate([high, low, high], axis=0))
    shown = mm(trace, jnp.concatenate([high, low], axis=1))
    shown_high, shown_low = split(shown[:, 0:512] + shown[:, 512:1024])
    faces = []
    for device in range(2):
        columns = slice(256 * device, 256 * (device + 1))
        outside_high, outside_low = [], []
        for face in range(6):
            rows = slice(TRACE_ROWS * (face ^ 1), TRACE_ROWS * (face ^ 1) + TRACE_ROWS)
            stacked = jnp.concatenate([shown_high[rows, columns], shown_low[rows, columns]], axis=0)
            found = mm(stacked, near[6 * device + face]).astype(BF)
            outside_high.append(found[:TRACE_ROWS])
            outside_low.append(found[TRACE_ROWS:])
        faces.append(jnp.concatenate(outside_high + outside_low, axis=0))
    return rates + LIFT * mm(lift_two, jnp.concatenate(faces, axis=1))


def weight_of(segment):
    acoustic = lax.axis_index("sec") > 0
    return jnp.where(acoustic, F32(SEGMENT_WEIGHTS[segment]), F32(0.0))


def first_inner_kernel(state, near, interior, trace, lift_two, carry_out):
    carry_out[...] = TIME_STEP * near_rates(
        state[...], near, interior[...], trace[...], lift_two[...]
    )


def first_outer_kernel(
    toward, across, back, sent_first, sent_second, state, carry, kinds, place, lift_two,
    kept_force, arrive, pick, send_kinds, trace,
    state_out, carry_out, first_out, second_out, force_out,
):
    came = arrived(toward[...], across[...], back[...])
    stacks = by_kind(
        (came[0][:, 256:384], came[1][:, 256:384]), (sent_first[...], sent_second[...]), kinds[...]
    )
    rates = far_rates(stacks, place[...], lift_two[...])
    got = jnp.concatenate(sides(came[0][:, 0:256], came[1][:, 0:256]), axis=0)
    high, low = split(jnp.transpose(got)[0:192])
    force = kept_force[...] + (mm(high, arrive[...]) + mm(low, arrive[...]))
    force_out[...] = force
    carry_now = carry[...] + (LIFT * TIME_STEP) * rates
    carry_now = jnp.concatenate([carry_now[0:64], carry_now[64:256] + TIME_STEP * force], axis=0)
    state_now = state[...] + weight_of(0) * carry_now
    state_out[...] = state_now
    carry_out[...] = carry_now
    sent = picked_traces(state_now, pick[...], send_kinds[...], trace[...])
    first_out[...], second_out[...] = sides(sent[:, :LANES], sent[:, LANES:])


def inner_kernel(segment, state, carry, force, near, interior, trace, lift_two, *refs):
    if segment == 1:
        state_now, carry_now = state[...], carry[...]
    else:
        (stacks, place), refs = refs[:2], refs[2:]
        rates = far_rates(stacks[...], place[...], lift_two[...])
        carry_now = carry[...] + (LIFT * TIME_STEP) * rates
        state_now = state[...] + weight_of(segment - 1) * carry_now
    rates = near_rates(state_now, near, interior[...], trace[...], lift_two[...])
    own = SEGMENT_CARRY[segment] * carry_now + TIME_STEP * rates
    own = jnp.concatenate([own[0:64], own[64:256] + TIME_STEP * force[...]], axis=0)
    ahead = state_now + weight_of(segment) * own
    if segment == 4:
        refs[0][...] = jnp.where(core_number() == 0, ahead[:, 0:256], ahead[:, 256:512])
        return
    pick, send_kinds, state_out, carry_out, base_out = refs
    state_out[...] = state_now
    carry_out[...] = own
    base_out[...] = picked_traces(ahead, pick[...], send_kinds[...], trace[...])


def outer_kernel(
    segment, toward, across, back, sent_first, sent_second, kinds, meet, reach, send_kinds, base,
    stacks_out, first_out, second_out,
):
    stacks = by_kind(
        arrived(toward[...], across[...], back[...]), (sent_first[...], sent_second[...]), kinds[...]
    )
    stacks_out[...] = stacks
    shown = mm(reach[...], mm(stacks, meet[...]).astype(BF))
    sent = base[...] + (weight_of(segment) * F32(LIFT * TIME_STEP)) * of_kind(shown, send_kinds[...])
    first_out[...], second_out[...] = sides(sent[:, :LANES], sent[:, LANES:])


def last_kernel(
    toward, across, back, sent_first, sent_second, kinds, own_place, lift_two, ahead, out
):
    stacks = by_kind(
        arrived(toward[...], across[...], back[...]), (sent_first[...], sent_second[...]), kinds[...]
    )
    rates = far_rates(stacks, own_place[...], lift_two[...])
    out[...] = ahead[...] + (weight_of(4) * F32(LIFT * TIME_STEP)) * rates


def call(kernel, outs, *args, flops=1 << 20):
    vmem = pl.BlockSpec(memory_space=pltpu.VMEM)
    size = sum(int(np.prod(a.shape)) * a.dtype.itemsize for a in (*args, *outs))
    return pl.pallas_call(
        kernel,
        out_shape=list(outs),
        in_specs=[vmem] * len(args),
        out_specs=[vmem] * len(outs),
        compiler_params=pltpu.CompilerParams(vmem_limit_bytes=32 << 20),
        cost_estimate=pl.CostEstimate(flops=flops, bytes_accessed=size, transcendentals=0),
    )(*args)


def arr(*shape, dtype=F32):
    return jax.ShapeDtypeStruct(shape, dtype)


def trade(first, second, sections):
    count = lax.axis_size("dom")
    toward, across, back = [], [], []
    for section in sections:
        for dom in range(count - 2):
            chip, low = dom >> 1, section * count + dom
            if chip & 1:
                across += [(low, low + 2), (low + 2, low)]
            elif chip & 2:
                toward.append((low, low + 2))
                back.append((low + 2, low))
            else:
                toward.append((low + 2, low))
                back.append((low, low + 2))
    came = []
    for value, pairs in ((second, toward), (first, across), (second, back)):
        came.append(lax.ppermute(value, ("sec", "dom"), pairs))
    return came


def swap(value):
    return lax.ppermute(value, "dom", [(at, at ^ 1) for at in range(lax.axis_size("dom"))])


def step(fields, source_map, new_owner, send_list, face_slot):
    cells = fields.reshape(ROWS, ELEMENTS)
    high, low = two_terms(interior_matrix())
    interior = jnp.asarray(np.concatenate([high, high, low], axis=1))
    trace = jnp.asarray(trace_matrix().astype(BF))
    lift_two = jnp.asarray(np.concatenate([lift_matrix()] * 2, axis=1).astype(BF))
    reach = jnp.asarray(np.concatenate([trace_matrix() @ lift_matrix()] * 2, axis=1).astype(BF))
    every = range(lax.axis_size("sec"))
    acoustic = every[1:]
    piece, whole = arr(TRACE_ROWS, LANES), arr(256, 512)

    names = jnp.zeros((264, 256), jnp.int32)
    for part, row, lane in (
        (face_slot, 256, 0),
        (source_map.reshape(1, 256), 262, 0),
        (new_owner.reshape(1, 64), 263, 0),
        (send_list.reshape(1, 96), 263, 128),
    ):
        rows, lanes = part.shape
        edges = ((row, 264 - row - rows, 0), (lane, 256 - lane - lanes, 0))
        names = names + lax.pad(part, jnp.int32(0), edges)
    packed = names.astype(F32) + lax.pad(cells, F32(0.0), ((0, 8, 0), (0, 0, 0)))
    (lamb,) = call(lamb_kernel, [arr(192, 256)], packed)
    lamb_parts = []
    for section in (1, 2, 3):
        lamb_parts.append(lax.ppermute(lamb, "sec", [(0, section)]))
    other = swap(packed)
    *leaving, chip, select, keep, arrive = call(
        depart_kernel,
        [
            arr(48, 256),
            arr(48, 256),
            arr(264, 512),
            arr(96, 512, dtype=BF),
            arr(512, 512, dtype=BF),
            arr(96, 512, dtype=BF),
        ],
        packed,
        other,
    )
    moved = trade(*leaving, every)
    kept, near, place, own_place, kinds, pick, send_kinds, meet = call(
        tables_kernel,
        [
            whole,
            arr(12, 256, 256, dtype=BF),
            arr(256, 512, dtype=BF),
            arr(256, 256, dtype=BF),
            arr(8, 256),
            arr(512, 256, dtype=BF),
            arr(8, 256),
            arr(256, 256, dtype=BF),
        ],
        chip,
        keep,
    )
    (force_mine,) = call(force_kernel, [arr(192, 256)], *lamb_parts, packed, kinds)
    force_other = swap(force_mine)
    state, *sent = call(
        arrive_kernel, [whole, piece, piece], *moved, kept, arrive, pick, send_kinds, trace
    )
    *wide, kept_force = call(
        force_depart_kernel,
        [arr(48, 384), arr(48, 384), arr(192, 512)],
        force_mine, force_other, select, keep, *sent,
    )
    came = trade(*wide, acoustic)
    (carry,) = call(first_inner_kernel, [whole], state, near, interior, trace, lift_two)
    state, carry, *later, force = call(
        first_outer_kernel,
        [whole, whole, piece, piece, arr(192, 512)],
        *came, *sent, state, carry, kinds, place, lift_two, kept_force, arrive, pick, send_kinds, trace,
    )
    stacks = None
    for segment in range(1, 5):
        sent, came = later, trade(*later, acoustic)
        args = [state, carry, force, near, interior, trace, lift_two]
        if segment > 1:
            args += [stacks, place]
        if segment == 4:
            (ahead,) = call(functools.partial(inner_kernel, segment), [arr(256, 256)], *args)
            break
        state, carry, base = call(
            functools.partial(inner_kernel, segment),
            [whole, whole, arr(TRACE_ROWS, 256)],
            *args, pick, send_kinds,
        )
        stacks, *later = call(
            functools.partial(outer_kernel, segment),
            [arr(12 * TRACE_ROWS, 256, dtype=BF), piece, piece],
            *came, *sent, kinds, meet, reach, send_kinds, base,
        )
    (out,) = call(
        last_kernel, [arr(256, 256)], *came, *sent, kinds, own_place, lift_two, ahead
    )
    return out.reshape(4, 64, ELEMENTS)


def solution(mesh):
    in_specs = (
        P(None, None, ("sec", "dom")),
        P(("sec", "dom")),
        P(("sec", "dom")),
        P(("sec", "dom")),
        P(None, ("sec", "dom")),
    )
    out_specs = P(None, None, ("sec", "dom"))
    return jax.shard_map(step, mesh=mesh, in_specs=in_specs, out_specs=out_specs, check_vma=False)
```

profile of v0, /device:TPU:250, one launch (start us, length us, event | category | flops | bytes accessed | tf_op | source)
XLA Modules:
  0.0 98.7 jit_solution(17089637876626845173)
XLA Ops:
  1.0 2.1 %collective-permute-start.3 = (f32[264,256]{1,0:T(8,128)S(1)}, f32[264,256]{1,0:T(8,128)S(1)}, u32[]{:S(2)}, u32[]{:S(2)}) collective-permute-start(f32[264,256]{1,0:T(8,128)S(1)} %pad_add_fusion.packed.mine), channel_id=1, source_target_pairs={{0,1},{1,0},{2,3},{3,2},{4,5},{5,4},{6,7},{7,6},{8,9},{9,8},{10,11... | collective-permute-start | bytes 811016 | tf_op jit(solution)/shard_map/ppermute | solution.py:507
  4.8 1.3 %collective-permute-start = (f32[192,256]{1,0:T(8,128)S(1)}, f32[192,256]{1,0:T(8,128)S(1)}, u32[]{:S(2)}, u32[]{:S(2)}) collective-permute-start(f32[192,256]{1,0:T(8,128)S(1)} %shard_map.91), channel_id=1, source_target_pairs={{0,128},{1,129},{2,130},{3,131},{4,132},{5,133},{6,134},{7,135},{8... | collective-permute-start | bytes 589832 | tf_op jit(solution)/shard_map/ppermute | solution.py:535
  6.7 1.7 %shard_map.93 = (f32[256,512]{1,0:T(8,128)S(1)}, bf16[12,256,256]{2,1,0:T(8,128)(2,1)S(1)}, bf16[256,512]{1,0:T(8,128)(2,1)S(1)}, bf16[256,256]{1,0:T(8,128)(2,1...) custom-call(f32[264,512]{1,0:T(8,128)S(1)} %get-tuple-element.48.chi, ...), custom_call_target="tpu_custom_call" | custom-call | flops 1048576 | bytes 3964928 | tf_op jit(solution)/shard_map/pallas_call | solution.py:472
  8.5 10.9 %collective-permute-done.first = f32[192,256]{1,0:T(8,128)S(1)} collective-permute-done((f32[192,256]{1,0:T(8,128)S(1)}, f32[192,256]{1,0:T(8,128)S(1)}, u32[]{:S(2)}, u32[]{:S(2)}) %collective-permute-start) | collective-permute-done | bytes 196640 | tf_op jit(solution)/shard_map/ppermute | solution.py:535
  19.6 1.9 %collective-permute-start.4 = (f32[192,256]{1,0:T(8,128)S(1)}, f32[192,256]{1,0:T(8,128)S(1)}, u32[]{:S(2)}, u32[]{:S(2)}) collective-permute-start(f32[192,256]{1,0:T(8,128)S(1)} %shard_map.94.mine), channel_id=1, source_target_pairs={{0,1},{1,0},{2,3},{3,2},{4,5},{5,4},{6,7},{7,6},{8,9},{9,8},{10,11... | collective-permute-start | bytes 589832 | tf_op jit(solution)/shard_map/ppermute | solution.py:507
  21.6 4.7 %collective-permute-start.6 = (f32[48,256]{1,0:T(8,128)S(1)}, f32[48,256]{1,0:T(8,128)S(1)}, u32[]{:S(2)}, u32[]{:S(2)}) collective-permute-start(f32[48,256]{1,0:T(8,128)S(1)} %get-tuple-element.53), channel_id=1, source_target_pairs={{2,4},{4,2},{3,5},{5,3},{6,8},{8,6},{7,9},{9,7},{10,12},{12,10},{1... | collective-permute-start | bytes 147464 | tf_op jit(solution)/shard_map/ppermute | solution.py:502
  26.3 1.8 %collective-permute-start.7 = (f32[48,256]{1,0:T(8,128)S(1)}, f32[48,256]{1,0:T(8,128)S(1)}, u32[]{:S(2)}, u32[]{:S(2)}) collective-permute-start(f32[48,256]{1,0:T(8,128)S(1)} %get-tuple-element.52), channel_id=1, source_target_pairs={{0,2},{1,3},{6,4},{7,5},{8,10},{9,11},{14,12},{15,13},{16,18},{17,... | collective-permute-start | bytes 147464 | tf_op jit(solution)/shard_map/ppermute | solution.py:502
  28.1 1.3 %collective-permute-start.5 = (f32[48,256]{1,0:T(8,128)S(1)}, f32[48,256]{1,0:T(8,128)S(1)}, u32[]{:S(2)}, u32[]{:S(2)}) collective-permute-start(f32[48,256]{1,0:T(8,128)S(1)} %get-tuple-element.52), channel_id=1, source_target_pairs={{2,0},{3,1},{4,6},{5,7},{10,8},{11,9},{12,14},{13,15},{18,16},{19,... | collective-permute-start | bytes 147464 | tf_op jit(solution)/shard_map/ppermute | solution.py:502
  29.4 1.5 %collective-permute-done.6.across = f32[48,256]{1,0:T(8,128)S(1)} collective-permute-done((f32[48,256]{1,0:T(8,128)S(1)}, f32[48,256]{1,0:T(8,128)S(1)}, u32[]{:S(2)}, u32[]{:S(2)}) %collective-permute-start.6) | collective-permute-done | bytes 49184 | tf_op jit(solution)/shard_map/ppermute | solution.py:502
  30.9 3.2 %collective-permute-done.5.toward = f32[48,256]{1,0:T(8,128)S(1)} collective-permute-done((f32[48,256]{1,0:T(8,128)S(1)}, f32[48,256]{1,0:T(8,128)S(1)}, u32[]{:S(2)}, u32[]{:S(2)}) %collective-permute-start.5) | collective-permute-done | bytes 49184 | tf_op jit(solution)/shard_map/ppermute | solution.py:502
  35.5 5.1 %collective-permute-start.9 = (f32[48,384]{1,0:T(8,128)S(1)}, f32[48,384]{1,0:T(8,128)S(1)}, u32[]{:S(2)}, u32[]{:S(2)}) collective-permute-start(f32[48,384]{1,0:T(8,128)S(1)} %get-tuple-element.61), channel_id=1, source_target_pairs={{130,132},{132,130},{131,133},{133,131},{134,136},{136,134},{135,1... | collective-permute-start | bytes 221192 | tf_op jit(solution)/shard_map/ppermute | solution.py:502
  40.6 1.3 %collective-permute-start.10 = (f32[48,384]{1,0:T(8,128)S(1)}, f32[48,384]{1,0:T(8,128)S(1)}, u32[]{:S(2)}, u32[]{:S(2)}) collective-permute-start(f32[48,384]{1,0:T(8,128)S(1)} %get-tuple-element.60), channel_id=1, source_target_pairs={{128,130},{129,131},{134,132},{135,133},{136,138},{137,139},{142,1... | collective-permute-start | bytes 221192 | tf_op jit(solution)/shard_map/ppermute | solution.py:502
  41.9 1.3 %collective-permute-start.8 = (f32[48,384]{1,0:T(8,128)S(1)}, f32[48,384]{1,0:T(8,128)S(1)}, u32[]{:S(2)}, u32[]{:S(2)}) collective-permute-start(f32[48,384]{1,0:T(8,128)S(1)} %get-tuple-element.60), channel_id=1, source_target_pairs={{130,128},{131,129},{132,134},{133,135},{138,136},{139,137},{140,1... | collective-permute-start | bytes 221192 | tf_op jit(solution)/shard_map/ppermute | solution.py:502
  45.0 3.1 %collective-permute-done.8.toward = f32[48,384]{1,0:T(8,128)S(1)} collective-permute-done((f32[48,384]{1,0:T(8,128)S(1)}, f32[48,384]{1,0:T(8,128)S(1)}, u32[]{:S(2)}, u32[]{:S(2)}) %collective-permute-start.8) | collective-permute-done | bytes 73760 | tf_op jit(solution)/shard_map/ppermute | solution.py:502
  49.3 4.0 %collective-permute-start.12 = (f32[48,128]{1,0:T(8,128)S(1)}, f32[48,128]{1,0:T(8,128)S(1)}, u32[]{:S(2)}, u32[]{:S(2)}) collective-permute-start(f32[48,128]{1,0:T(8,128)S(1)} %get-tuple-element.67.sent_first), channel_id=1, source_target_pairs={{130,132},{132,130},{131,133},{133,131},{134,136},{136,134},{135,1... | collective-permute-start | bytes 73736 | tf_op jit(solution)/shard_map/ppermute | solution.py:502
  54.7 1.3 %collective-permute-start.11 = (f32[48,128]{1,0:T(8,128)S(1)}, f32[48,128]{1,0:T(8,128)S(1)}, u32[]{:S(2)}, u32[]{:S(2)}) collective-permute-start(f32[48,128]{1,0:T(8,128)S(1)} %get-tuple-element.66.sent_second), channel_id=1, source_target_pairs={{130,128},{131,129},{132,134},{133,135},{138,136},{139,137},{140,1... | collective-permute-start | bytes 73736 | tf_op jit(solution)/shard_map/ppermute | solution.py:502
  56.0 1.6 %shard_map.99 = (f32[256,512]{1,0:T(8,128)S(1)}, f32[256,512]{1,0:T(8,128)S(1)}, f32[48,256]{1,0:T(8,128)S(1)}) custom-call(f32[256,512]{1,0:T(8,128)S(1)} %get-tuple-element.69.state, f32[256,512]{1,0:T(8,128)S(1)} %get-tuple-element.70.carry, f32[192,512]{1,0:T(8,128)S(1)} %get-tuple-element.71.force, bf16[12,256,256]{2,1,0:T(8,128)(2,1)S(1)} %get-tuple-element.63.near, ...), custom_call_target="tpu_custom_call" | custom-call | flops 1048576 | bytes 5218304 | tf_op jit(solution)/shard_map/pallas_call | solution.py:472
  58.4 2.0 %collective-permute-done.11.toward = f32[48,128]{1,0:T(8,128)S(1)} collective-permute-done((f32[48,128]{1,0:T(8,128)S(1)}, f32[48,128]{1,0:T(8,128)S(1)}, u32[]{:S(2)}, u32[]{:S(2)}) %collective-permute-start.11) | collective-permute-done | bytes 24608 | tf_op jit(solution)/shard_map/ppermute | solution.py:502
  61.0 5.1 %collective-permute-start.15 = (f32[48,128]{1,0:T(8,128)S(1)}, f32[48,128]{1,0:T(8,128)S(1)}, u32[]{:S(2)}, u32[]{:S(2)}) collective-permute-start(f32[48,128]{1,0:T(8,128)S(1)} %get-tuple-element.74.sent_first), channel_id=1, source_target_pairs={{130,132},{132,130},{131,133},{133,131},{134,136},{136,134},{135,1... | collective-permute-start | bytes 73736 | tf_op jit(solution)/shard_map/ppermute | solution.py:502
  66.1 1.3 %collective-permute-start.16 = (f32[48,128]{1,0:T(8,128)S(1)}, f32[48,128]{1,0:T(8,128)S(1)}, u32[]{:S(2)}, u32[]{:S(2)}) collective-permute-start(f32[48,128]{1,0:T(8,128)S(1)} %get-tuple-element.73.sent_second), channel_id=1, source_target_pairs={{128,130},{129,131},{134,132},{135,133},{136,138},{137,139},{142,1... | collective-permute-start | bytes 73736 | tf_op jit(solution)/shard_map/ppermute | solution.py:502
  67.4 1.3 %collective-permute-start.14 = (f32[48,128]{1,0:T(8,128)S(1)}, f32[48,128]{1,0:T(8,128)S(1)}, u32[]{:S(2)}, u32[]{:S(2)}) collective-permute-start(f32[48,128]{1,0:T(8,128)S(1)} %get-tuple-element.73.sent_second), channel_id=1, source_target_pairs={{130,128},{131,129},{132,134},{133,135},{138,136},{139,137},{140,1... | collective-permute-start | bytes 73736 | tf_op jit(solution)/shard_map/ppermute | solution.py:502
  68.7 2.1 %shard_map.101 = (f32[256,512]{1,0:T(8,128)S(1)}, f32[256,512]{1,0:T(8,128)S(1)}, f32[48,256]{1,0:T(8,128)S(1)}) custom-call(f32[256,512]{1,0:T(8,128)S(1)} %get-tuple-element.75.state, f32[256,512]{1,0:T(8,128)S(1)} %get-tuple-element.76.carry, f32[192,512]{1,0:T(8,128)S(1)} %get-tuple-element.71.force, bf16[12,256,256]{2,1,0:T(8,128)(2,1)S(1)} %get-tuple-element.63.near, ...), custom_call_target="tpu_custom_call" | custom-call | flops 1048576 | bytes 5775360 | tf_op jit(solution)/shard_map/pallas_call | solution.py:472
  70.9 2.3 %collective-permute-done.14.toward = f32[48,128]{1,0:T(8,128)S(1)} collective-permute-done((f32[48,128]{1,0:T(8,128)S(1)}, f32[48,128]{1,0:T(8,128)S(1)}, u32[]{:S(2)}, u32[]{:S(2)}) %collective-permute-start.14) | collective-permute-done | bytes 24608 | tf_op jit(solution)/shard_map/ppermute | solution.py:502
  73.7 4.0 %collective-permute-start.18 = (f32[48,128]{1,0:T(8,128)S(1)}, f32[48,128]{1,0:T(8,128)S(1)}, u32[]{:S(2)}, u32[]{:S(2)}) collective-permute-start(f32[48,128]{1,0:T(8,128)S(1)} %get-tuple-element.80.sent_first), channel_id=1, source_target_pairs={{130,132},{132,130},{131,133},{133,131},{134,136},{136,134},{135,1... | collective-permute-start | bytes 73736 | tf_op jit(solution)/shard_map/ppermute | solution.py:502
  77.7 1.3 %collective-permute-start.19 = (f32[48,128]{1,0:T(8,128)S(1)}, f32[48,128]{1,0:T(8,128)S(1)}, u32[]{:S(2)}, u32[]{:S(2)}) collective-permute-start(f32[48,128]{1,0:T(8,128)S(1)} %get-tuple-element.79.sent_second), channel_id=1, source_target_pairs={{128,130},{129,131},{134,132},{135,133},{136,138},{137,139},{142,1... | collective-permute-start | bytes 73736 | tf_op jit(solution)/shard_map/ppermute | solution.py:502
  79.0 1.5 %collective-permute-start.17 = (f32[48,128]{1,0:T(8,128)S(1)}, f32[48,128]{1,0:T(8,128)S(1)}, u32[]{:S(2)}, u32[]{:S(2)}) collective-permute-start(f32[48,128]{1,0:T(8,128)S(1)} %get-tuple-element.79.sent_second), channel_id=1, source_target_pairs={{130,128},{131,129},{132,134},{133,135},{138,136},{139,137},{140,1... | collective-permute-start | bytes 73736 | tf_op jit(solution)/shard_map/ppermute | solution.py:502
  80.5 2.1 %shard_map.103 = (f32[256,512]{1,0:T(8,128)S(1)}, f32[256,512]{1,0:T(8,128)S(1)}, f32[48,256]{1,0:T(8,128)S(1)}) custom-call(f32[256,512]{1,0:T(8,128)S(1)} %get-tuple-element.81.state, f32[256,512]{1,0:T(8,128)S(1)} %get-tuple-element.82.carry, f32[192,512]{1,0:T(8,128)S(1)} %get-tuple-element.71.force, bf16[12,256,256]{2,1,0:T(8,128)(2,1)S(1)} %get-tuple-element.63.near, ...), custom_call_target="tpu_custom_call" | custom-call | flops 1048576 | bytes 5775360 | tf_op jit(solution)/shard_map/pallas_call | solution.py:472
  82.7 2.0 %collective-permute-done.17.toward = f32[48,128]{1,0:T(8,128)S(1)} collective-permute-done((f32[48,128]{1,0:T(8,128)S(1)}, f32[48,128]{1,0:T(8,128)S(1)}, u32[]{:S(2)}, u32[]{:S(2)}) %collective-permute-start.17) | collective-permute-done | bytes 24608 | tf_op jit(solution)/shard_map/ppermute | solution.py:502
  85.3 5.1 %collective-permute-start.21 = (f32[48,128]{1,0:T(8,128)S(1)}, f32[48,128]{1,0:T(8,128)S(1)}, u32[]{:S(2)}, u32[]{:S(2)}) collective-permute-start(f32[48,128]{1,0:T(8,128)S(1)} %get-tuple-element.86.sent_first), channel_id=1, source_target_pairs={{130,132},{132,130},{131,133},{133,131},{134,136},{136,134},{135,1... | collective-permute-start | bytes 73736 | tf_op jit(solution)/shard_map/ppermute | solution.py:502
  91.8 1.3 %collective-permute-start.20 = (f32[48,128]{1,0:T(8,128)S(1)}, f32[48,128]{1,0:T(8,128)S(1)}, u32[]{:S(2)}, u32[]{:S(2)}) collective-permute-start(f32[48,128]{1,0:T(8,128)S(1)} %get-tuple-element.85.sent_second), channel_id=1, source_target_pairs={{130,128},{131,129},{132,134},{133,135},{138,136},{139,137},{140,1... | collective-permute-start | bytes 73736 | tf_op jit(solution)/shard_map/ppermute | solution.py:502
  93.1 1.7 %shard_map.105.ahead = f32[256,256]{1,0:T(8,128)S(1)} custom-call(f32[256,512]{1,0:T(8,128)S(1)} %get-tuple-element.88.state, f32[256,512]{1,0:T(8,128)S(1)} %get-tuple-element.89.carry, f32[192,512]{1,0:T(8,128)S(1)} %get-tuple-element.71.force, bf16[12,256,256]{2,1,0:T(8,128)(2,1)S(1)} %get-tuple-element.63.near, bf16[256,768]{1,0:T(8,128)(2,1)S(1)} %copy-done.1, ...), custom_call_target="tpu_custom_call" | custom-call | flops 1048576 | bytes 4669440 | tf_op jit(solution)/shard_map/pallas_call | solution.py:472
  94.8 2.7 %collective-permute-done.20.toward = f32[48,128]{1,0:T(8,128)S(1)} collective-permute-done((f32[48,128]{1,0:T(8,128)S(1)}, f32[48,128]{1,0:T(8,128)S(1)}, u32[]{:S(2)}, u32[]{:S(2)}) %collective-permute-start.20) | collective-permute-done | bytes 24608 | tf_op jit(solution)/shard_map/ppermute | solution.py:502
  (39 shorter events, 14.3 us)
Async XLA Ops:
  1.0 33.1 %copy-start.2 = (bf16[288,256]{1,0:T(8,128)(2,1)S(1)}, bf16[288,256]{1,0:T(8,128)(2,1)}, u32[]{:S(2)}) copy-start(bf16[288,256]{1,0:T(8,128)(2,1)} %constant.13.clone.trace) | copy-start | bytes 442372
  1.0 5.0 %collective-permute-start.3 = (f32[264,256]{1,0:T(8,128)S(1)}, f32[264,256]{1,0:T(8,128)S(1)}, u32[]{:S(2)}, u32[]{:S(2)}) collective-permute-start(f32[264,256]{1,0:T(8,128)S(1)} %pad_add_fusion.packed.mine), channel_id=1, source_target_pairs={{0,1},{1,0},{2,3},{3,2},{4,5},{5,4},{6,7},{7,6},{8,9},{9,8},{10,11... | collective-permute-start | bytes 811016 | tf_op jit(solution)/shard_map/ppermute | solution.py:507
  3.4 5.1 %collective-permute-start.2 = (f32[192,256]{1,0:T(8,128)S(1)}, f32[192,256]{1,0:T(8,128)S(1)}, u32[]{:S(2)}, u32[]{:S(2)}) collective-permute-start(f32[192,256]{1,0:T(8,128)S(1)} %shard_map.91), channel_id=1, source_target_pairs={{0,384},{1,385},{2,386},{3,387},{4,388},{5,389},{6,390},{7,391},{8... | collective-permute-start | bytes 589832 | tf_op jit(solution)/shard_map/ppermute | solution.py:535
  4.1 4.4 %collective-permute-start.1 = (f32[192,256]{1,0:T(8,128)S(1)}, f32[192,256]{1,0:T(8,128)S(1)}, u32[]{:S(2)}, u32[]{:S(2)}) collective-permute-start(f32[192,256]{1,0:T(8,128)S(1)} %shard_map.91), channel_id=1, source_target_pairs={{0,256},{1,257},{2,258},{3,259},{4,260},{5,261},{6,262},{7,263},{8... | collective-permute-start | bytes 589832 | tf_op jit(solution)/shard_map/ppermute | solution.py:535
  4.8 14.6 %collective-permute-start = (f32[192,256]{1,0:T(8,128)S(1)}, f32[192,256]{1,0:T(8,128)S(1)}, u32[]{:S(2)}, u32[]{:S(2)}) collective-permute-start(f32[192,256]{1,0:T(8,128)S(1)} %shard_map.91), channel_id=1, source_target_pairs={{0,128},{1,129},{2,130},{3,131},{4,132},{5,133},{6,134},{7,135},{8... | collective-permute-start | bytes 589832 | tf_op jit(solution)/shard_map/ppermute | solution.py:535
  19.4 23.8 %copy-start = (bf16[256,576]{1,0:T(8,128)(2,1)S(1)}, bf16[256,576]{1,0:T(8,128)(2,1)}, u32[]{:S(2)}) copy-start(bf16[256,576]{1,0:T(8,128)(2,1)} %constant.14.clone.lift_two) | copy-start | bytes 884740
  19.4 23.8 %copy-start.1 = (bf16[256,768]{1,0:T(8,128)(2,1)S(1)}, bf16[256,768]{1,0:T(8,128)(2,1)}, u32[]{:S(2)}) copy-start(bf16[256,768]{1,0:T(8,128)(2,1)} %constant.12.clone.interior) | copy-start | bytes 1179652
  19.6 15.2 %collective-permute-start.4 = (f32[192,256]{1,0:T(8,128)S(1)}, f32[192,256]{1,0:T(8,128)S(1)}, u32[]{:S(2)}, u32[]{:S(2)}) collective-permute-start(f32[192,256]{1,0:T(8,128)S(1)} %shard_map.94.mine), channel_id=1, source_target_pairs={{0,1},{1,0},{2,3},{3,2},{4,5},{5,4},{6,7},{7,6},{8,9},{9,8},{10,11... | collective-permute-start | bytes 589832 | tf_op jit(solution)/shard_map/ppermute | solution.py:507
  21.6 9.4 %collective-permute-start.6 = (f32[48,256]{1,0:T(8,128)S(1)}, f32[48,256]{1,0:T(8,128)S(1)}, u32[]{:S(2)}, u32[]{:S(2)}) collective-permute-start(f32[48,256]{1,0:T(8,128)S(1)} %get-tuple-element.53), channel_id=1, source_target_pairs={{2,4},{4,2},{3,5},{5,3},{6,8},{8,6},{7,9},{9,7},{10,12},{12,10},{1... | collective-permute-start | bytes 147464 | tf_op jit(solution)/shard_map/ppermute | solution.py:502
  26.3 4.7 %collective-permute-start.7 = (f32[48,256]{1,0:T(8,128)S(1)}, f32[48,256]{1,0:T(8,128)S(1)}, u32[]{:S(2)}, u32[]{:S(2)}) collective-permute-start(f32[48,256]{1,0:T(8,128)S(1)} %get-tuple-element.52), channel_id=1, source_target_pairs={{0,2},{1,3},{6,4},{7,5},{8,10},{9,11},{14,12},{15,13},{16,18},{17,... | collective-permute-start | bytes 147464 | tf_op jit(solution)/shard_map/ppermute | solution.py:502
  28.1 6.0 %collective-permute-start.5 = (f32[48,256]{1,0:T(8,128)S(1)}, f32[48,256]{1,0:T(8,128)S(1)}, u32[]{:S(2)}, u32[]{:S(2)}) collective-permute-start(f32[48,256]{1,0:T(8,128)S(1)} %get-tuple-element.52), channel_id=1, source_target_pairs={{2,0},{3,1},{4,6},{5,7},{10,8},{11,9},{12,14},{13,15},{18,16},{19,... | collective-permute-start | bytes 147464 | tf_op jit(solution)/shard_map/ppermute | solution.py:502
  35.5 9.6 %collective-permute-start.9 = (f32[48,384]{1,0:T(8,128)S(1)}, f32[48,384]{1,0:T(8,128)S(1)}, u32[]{:S(2)}, u32[]{:S(2)}) collective-permute-start(f32[48,384]{1,0:T(8,128)S(1)} %get-tuple-element.61), channel_id=1, source_target_pairs={{130,132},{132,130},{131,133},{133,131},{134,136},{136,134},{135,1... | collective-permute-start | bytes 221192 | tf_op jit(solution)/shard_map/ppermute | solution.py:502
  40.6 4.4 %collective-permute-start.10 = (f32[48,384]{1,0:T(8,128)S(1)}, f32[48,384]{1,0:T(8,128)S(1)}, u32[]{:S(2)}, u32[]{:S(2)}) collective-permute-start(f32[48,384]{1,0:T(8,128)S(1)} %get-tuple-element.60), channel_id=1, source_target_pairs={{128,130},{129,131},{134,132},{135,133},{136,138},{137,139},{142,1... | collective-permute-start | bytes 221192 | tf_op jit(solution)/shard_map/ppermute | solution.py:502
  41.9 6.2 %collective-permute-start.8 = (f32[48,384]{1,0:T(8,128)S(1)}, f32[48,384]{1,0:T(8,128)S(1)}, u32[]{:S(2)}, u32[]{:S(2)}) collective-permute-start(f32[48,384]{1,0:T(8,128)S(1)} %get-tuple-element.60), channel_id=1, source_target_pairs={{130,128},{131,129},{132,134},{133,135},{138,136},{139,137},{140,1... | collective-permute-start | bytes 221192 | tf_op jit(solution)/shard_map/ppermute | solution.py:502
  49.3 9.0 %collective-permute-start.12 = (f32[48,128]{1,0:T(8,128)S(1)}, f32[48,128]{1,0:T(8,128)S(1)}, u32[]{:S(2)}, u32[]{:S(2)}) collective-permute-start(f32[48,128]{1,0:T(8,128)S(1)} %get-tuple-element.67.sent_first), channel_id=1, source_target_pairs={{130,132},{132,130},{131,133},{133,131},{134,136},{136,134},{135,1... | collective-permute-start | bytes 73736 | tf_op jit(solution)/shard_map/ppermute | solution.py:502
  53.4 5.0 %collective-permute-start.13 = (f32[48,128]{1,0:T(8,128)S(1)}, f32[48,128]{1,0:T(8,128)S(1)}, u32[]{:S(2)}, u32[]{:S(2)}) collective-permute-start(f32[48,128]{1,0:T(8,128)S(1)} %get-tuple-element.66.sent_second), channel_id=1, source_target_pairs={{128,130},{129,131},{134,132},{135,133},{136,138},{137,139},{142,1... | collective-permute-start | bytes 73736 | tf_op jit(solution)/shard_map/ppermute | solution.py:502
  54.7 5.7 %collective-permute-start.11 = (f32[48,128]{1,0:T(8,128)S(1)}, f32[48,128]{1,0:T(8,128)S(1)}, u32[]{:S(2)}, u32[]{:S(2)}) collective-permute-start(f32[48,128]{1,0:T(8,128)S(1)} %get-tuple-element.66.sent_second), channel_id=1, source_target_pairs={{130,128},{131,129},{132,134},{133,135},{138,136},{139,137},{140,1... | collective-permute-start | bytes 73736 | tf_op jit(solution)/shard_map/ppermute | solution.py:502
  56.0 4.4 %copy-start.3 = (bf16[288,576]{1,0:T(8,128)(2,1)S(1)}, bf16[288,576]{1,0:T(8,128)(2,1)}, u32[]{:S(2)}) copy-start(bf16[288,576]{1,0:T(8,128)(2,1)} %constant.15.clone.reach) | copy-start | bytes 995332
  61.0 9.9 %collective-permute-start.15 = (f32[48,128]{1,0:T(8,128)S(1)}, f32[48,128]{1,0:T(8,128)S(1)}, u32[]{:S(2)}, u32[]{:S(2)}) collective-permute-start(f32[48,128]{1,0:T(8,128)S(1)} %get-tuple-element.74.sent_first), channel_id=1, source_target_pairs={{130,132},{132,130},{131,133},{133,131},{134,136},{136,134},{135,1... | collective-permute-start | bytes 73736 | tf_op jit(solution)/shard_map/ppermute | solution.py:502
  66.1 4.7 %collective-permute-start.16 = (f32[48,128]{1,0:T(8,128)S(1)}, f32[48,128]{1,0:T(8,128)S(1)}, u32[]{:S(2)}, u32[]{:S(2)}) collective-permute-start(f32[48,128]{1,0:T(8,128)S(1)} %get-tuple-element.73.sent_second), channel_id=1, source_target_pairs={{128,130},{129,131},{134,132},{135,133},{136,138},{137,139},{142,1... | collective-permute-start | bytes 73736 | tf_op jit(solution)/shard_map/ppermute | solution.py:502
  67.4 5.7 %collective-permute-start.14 = (f32[48,128]{1,0:T(8,128)S(1)}, f32[48,128]{1,0:T(8,128)S(1)}, u32[]{:S(2)}, u32[]{:S(2)}) collective-permute-start(f32[48,128]{1,0:T(8,128)S(1)} %get-tuple-element.73.sent_second), channel_id=1, source_target_pairs={{130,128},{131,129},{132,134},{133,135},{138,136},{139,137},{140,1... | collective-permute-start | bytes 73736 | tf_op jit(solution)/shard_map/ppermute | solution.py:502
  73.7 9.0 %collective-permute-start.18 = (f32[48,128]{1,0:T(8,128)S(1)}, f32[48,128]{1,0:T(8,128)S(1)}, u32[]{:S(2)}, u32[]{:S(2)}) collective-permute-start(f32[48,128]{1,0:T(8,128)S(1)} %get-tuple-element.80.sent_first), channel_id=1, source_target_pairs={{130,132},{132,130},{131,133},{133,131},{134,136},{136,134},{135,1... | collective-permute-start | bytes 73736 | tf_op jit(solution)/shard_map/ppermute | solution.py:502
  77.7 5.0 %collective-permute-start.19 = (f32[48,128]{1,0:T(8,128)S(1)}, f32[48,128]{1,0:T(8,128)S(1)}, u32[]{:S(2)}, u32[]{:S(2)}) collective-permute-start(f32[48,128]{1,0:T(8,128)S(1)} %get-tuple-element.79.sent_second), channel_id=1, source_target_pairs={{128,130},{129,131},{134,132},{135,133},{136,138},{137,139},{142,1... | collective-permute-start | bytes 73736 | tf_op jit(solution)/shard_map/ppermute | solution.py:502
  79.0 5.7 %collective-permute-start.17 = (f32[48,128]{1,0:T(8,128)S(1)}, f32[48,128]{1,0:T(8,128)S(1)}, u32[]{:S(2)}, u32[]{:S(2)}) collective-permute-start(f32[48,128]{1,0:T(8,128)S(1)} %get-tuple-element.79.sent_second), channel_id=1, source_target_pairs={{130,128},{131,129},{132,134},{133,135},{138,136},{139,137},{140,1... | collective-permute-start | bytes 73736 | tf_op jit(solution)/shard_map/ppermute | solution.py:502
  85.3 9.5 %collective-permute-start.21 = (f32[48,128]{1,0:T(8,128)S(1)}, f32[48,128]{1,0:T(8,128)S(1)}, u32[]{:S(2)}, u32[]{:S(2)}) collective-permute-start(f32[48,128]{1,0:T(8,128)S(1)} %get-tuple-element.86.sent_first), channel_id=1, source_target_pairs={{130,132},{132,130},{131,133},{133,131},{134,136},{136,134},{135,1... | collective-permute-start | bytes 73736 | tf_op jit(solution)/shard_map/ppermute | solution.py:502
  90.5 4.4 %collective-permute-start.22 = (f32[48,128]{1,0:T(8,128)S(1)}, f32[48,128]{1,0:T(8,128)S(1)}, u32[]{:S(2)}, u32[]{:S(2)}) collective-permute-start(f32[48,128]{1,0:T(8,128)S(1)} %get-tuple-element.85.sent_second), channel_id=1, source_target_pairs={{128,130},{129,131},{134,132},{135,133},{136,138},{137,139},{142,1... | collective-permute-start | bytes 73736 | tf_op jit(solution)/shard_map/ppermute | solution.py:502
  91.8 5.7 %collective-permute-start.20 = (f32[48,128]{1,0:T(8,128)S(1)}, f32[48,128]{1,0:T(8,128)S(1)}, u32[]{:S(2)}, u32[]{:S(2)}) collective-permute-start(f32[48,128]{1,0:T(8,128)S(1)} %get-tuple-element.85.sent_second), channel_id=1, source_target_pairs={{130,128},{131,129},{132,134},{133,135},{138,136},{139,137},{140,1... | collective-permute-start | bytes 73736 | tf_op jit(solution)/shard_map/ppermute | solution.py:502
where the time goes:
time: 99.3 us; the launch traced here: 98.7 us
  starting transfers between devices  51 us (51%)
  waiting for transfers between devices  29.2 us (29%)
  Pallas kernels  17.1 us (17%)
  other arithmetic  1 us (1%)
    ppermute x18, starting transfers between devices, trade(): came.append(lax.ppermute(value, ('sec', 'dom'), pairs))  44.4 us
    ppermute x18, waiting for transfers between devices, trade(): came.append(lax.ppermute(value, ('sec', 'dom'), pairs))  18.3 us
    pallas_call x16, Pallas kernels, call(): pl.pallas_call(kernel, out_shape=list(outs), in_specs=[vmem] * len(args),...  17.1 us
    ppermute x3, waiting for transfers between devices, step(): lamb_parts.append(lax.ppermute(lamb, 'sec', [(0, section)]))  10.9 us
    ppermute x2, starting transfers between devices, swap(): lax.ppermute(value, 'dom', [(at, at ^ 1) for at in range(lax.axis_size('d...  3.97 us
    ppermute x3, starting transfers between devices, step(): lamb_parts.append(lax.ppermute(lamb, 'sec', [(0, section)]))  2.64 us
  transfers between devices with their start and end apart: 23, of which 11 were waited for; matrix products, arithmetic and copies ran while one was open for 0% of the time, Pallas kernels for 12%

commit v1 on v0

--- a/solution.py
+++ b/solution.py
@@ -159,10 +159,6 @@
     return total
 
 
-def arrived(toward, across, back):
-    return across, toward + back
-
-
 def by_kind(came, sent, kinds):
     far = lane_iota((TRACE_ROWS, LANES)) < PIECES * FACE_CAP
     from_left, from_right = sides(*came)
@@ -224,10 +220,29 @@
     lamb_out[128:192] = rho * (w[0] * v[1] - w[1] * v[0])
 
 
-def depart_kernel(mine, other, first_out, second_out, chip_out, select_out, keep_out, arrive_out):
+def group_of(device, offset):
+    return 8 * device + {0: 0, -2: 1, -1: 2, 1: 3, 2: 4}[offset]
+
+
+def start_of(count, device, offset):
+    total = jnp.zeros((1, 1), F32)
+    for number in (0, -2, -1, 1, 2):
+        if number == offset:
+            return total
+        at = group_of(device, number)
+        total = total + count[at : at + 1]
+
+
+def target_of(members, rank, device, moves):
+    total = jnp.full((1, 256), -1.0, F32)
+    for offset, base in moves:
+        at = group_of(device, offset)
+        total = total + members[at : at + 1] * (rank[at : at + 1] + (base + 1.0))
+    return total
+
+
+def depart_kernel(mine, other, first_out, second_out, select_out, ranks_out):
     low, high = chip_halves(mine[...], other[...])
-    chip_out[:, 0:256] = low
-    chip_out[:, 256:512] = high
     first = (lax.axis_index("dom") & -2).astype(F32)
     spread = one_hot((lane_iota((64, 256)) >> 2) == row_iota((64, 256)))
     before = one_hot(row_iota((256, 256)) < lane_iota((256, 256)))
@@ -241,28 +256,10 @@
         members.append(jnp.where(member, 1.0, 0.0))
     members = jnp.concatenate(members, axis=0)
     rank = mm(members.astype(BF), before)
-    count = jnp.sum(members, axis=1, keepdims=True)
-
-    def group(device, offset):
-        return 8 * device + {0: 0, -2: 1, -1: 2, 1: 3, 2: 4}[offset]
-
-    def start(device, offset):
-        total = jnp.zeros((1, 1), F32)
-        for number in (0, -2, -1, 1, 2):
-            if number == offset:
-                return total
-            at = group(device, number)
-            total = total + count[at : at + 1]
-
-    def target(device, moves):
-        total = jnp.full((1, 256), -1.0, F32)
-        for offset, base in moves:
-            at = group(device, offset)
-            total = total + members[at : at + 1] * (rank[at : at + 1] + (base + 1.0))
-        return total
-
-    low_target = target(0, ((-2, 0.0), (-1, 16.0), (2, 48.0)))
-    high_target = target(1, ((-2, 32.0), (1, 64.0), (2, 80.0)))
+    ranks_out[0:16] = members
+    ranks_out[16:32] = rank
+    low_target = target_of(members, rank, 0, ((-2, 0.0), (-1, 16.0), (2, 48.0)))
+    high_target = target_of(members, rank, 1, ((-2, 32.0), (1, 64.0), (2, 80.0)))
     number = row_iota((96, 256)).astype(F32)
     select = jnp.concatenate([one_hot(low_target == number), one_hot(high_target == number)], axis=1)
     select_out[...] = select
@@ -271,35 +268,62 @@
     sent = mm_nt(select, cells_high) + mm_nt(select, cells_low)
     first_out[...], second_out[...] = sides(sent[0:48], sent[48:96])
 
-    low_place = target(0, ((0, 0.0), (1, 256.0 + start(1, -1))))
-    high_place = target(1, ((0, 256.0), (-1, start(0, 1))))
+
+def places_kernel(
+    mine, other, ranks, trace,
+    kept_out, keep_out, arrive_out, pick_out, send_kinds_out, arrive_pick_out, base_out,
+):
+    low, high = chip_halves(mine[...], other[...])
+    members, rank = ranks[0:16], ranks[16:32]
+    count = jnp.sum(members, axis=1, keepdims=True)
+    low_place = target_of(members, rank, 0, ((0, 0.0), (1, 256.0 + start_of(count, 1, -1))))
+    high_place = target_of(members, rank, 1, ((0, 256.0), (-1, start_of(count, 0, 1))))
     number = row_iota((512, 256)).astype(F32)
-    keep_out[:, 0:256] = one_hot(low_place == number)
-    keep_out[:, 256:512] = one_hot(high_place == number)
+    keep = jnp.concatenate([one_hot(low_place == number), one_hot(high_place == number)], axis=1)
+    keep_out[...] = keep
     column = lane_iota((16, 512)).astype(F32)
     number = row_iota((16, 512)).astype(F32)
-    for piece, (device, offset) in enumerate(((0, -2), (0, -1), (1, -2), (0, 2), (1, 1), (1, 2))):
-        at = group(device, offset)
-        begin = start(device, offset) + 256.0 * device
-        arrive_out[16 * piece : 16 * piece + 16, :] = one_hot(
-            (column - begin == number) & (number < count[at : at + 1])
-        )
-
-
-def tables_kernel(
-    chip, keep,
-    kept_out, local_out, place_out, own_place_out, kinds_out, pick_out, send_kinds_out, meet_out,
-):
-    high, low = split(chip[0:256])
-    kept_out[...] = mm_nt(high, keep[...]) + mm_nt(low, keep[...])
+    blocks = []
+    for device, offset in ((0, -2), (0, -1), (1, -2), (0, 2), (1, 1), (1, 2)):
+        at = group_of(device, offset)
+        begin = start_of(count, device, offset) + 256.0 * device
+        blocks.append(one_hot((column - begin == number) & (number < count[at : at + 1])))
+    arrive = jnp.concatenate(blocks, axis=0)
+    arrive_out[...] = arrive
+    cells_high, cells_low = split(jnp.concatenate([low[0:256], high[0:256]], axis=1))
+    kept = mm_nt(cells_high, keep) + mm_nt(cells_low, keep)
+    kept_out[...] = kept
+    lane = lane_iota((8, LANES))
+    lists = [jnp.broadcast_to(half[263:264, 128:256], (8, LANES)) for half in (low, high)]
+    left = jnp.where(lane < 48, lists[0], pltpu.roll(lists[1], 48, 1))
+    right = jnp.where(
+        lane < 24,
+        pltpu.roll(lists[0], LANES - 72, 1),
+        jnp.where(lane < 72, pltpu.roll(lists[1], LANES - 24, 1), pltpu.roll(lists[0], 24, 1)),
+    )
+    names = jnp.concatenate(
+        [jnp.where(lane < 96, left, -1.0), jnp.where(lane < 96, right, -1.0)], axis=1
+    ).astype(jnp.int32)
+    wide = lane_iota((8, 256))
+    second = ((wide >= 48) & (wide < 128)) | ((wide >= 152) & (wide < 200))
+    column = jnp.where(names < 0, -1, (names & 255) + jnp.where(second, 256, 0))
+    pick = one_hot(column[0:1] == row_iota((512, 256)))
+    pick_out[...] = pick
+    send_kinds = jnp.where((names >> 8) == row_iota((8, 256)), 1.0, 0.0)
+    send_kinds_out[...] = send_kinds
+    arrive_pick_out[...] = mm(arrive, pick).astype(BF)
+    base_out[...] = picked_traces(kept, pick, send_kinds, trace[...])
+
+
+def faces_kernel(mine, other, pick, local_out, place_out, own_place_out, kinds_out, meet_out):
     row = row_iota((256, 256))
     ones = jnp.ones((8, 256), BF)
     kinds = [jnp.zeros((1, 256), F32)] * 6
     places = []
-    for device in range(2):
+    for device, half in enumerate(chip_halves(mine[256:264], other[256:264])):
         place = jnp.zeros((256, 256), F32)
         for face in range(6):
-            where = chip[256 + face : 257 + face, 256 * device : 256 * (device + 1)].astype(jnp.int32)
+            where = half[face : face + 1].astype(jnp.int32)
             local_out[6 * device + face] = one_hot(where - ELEMENTS * (face ^ 1) == row)
             n = where - 6 * ELEMENTS
             if device == 0:
@@ -314,38 +338,7 @@
     place = jnp.concatenate(places, axis=1).astype(BF)
     place_out[...] = place
     kinds_out[...] = jnp.concatenate(kinds + [jnp.zeros((2, 256), F32)], axis=0)
-    lane = lane_iota((8, LANES))
-    lists = [
-        jnp.broadcast_to(chip[263:264, 256 * device + 128 : 256 * device + 256], (8, LANES))
-        for device in range(2)
-    ]
-    left = jnp.where(lane < 48, lists[0], pltpu.roll(lists[1], 48, 1))
-    right = jnp.where(
-        lane < 24,
-        pltpu.roll(lists[0], LANES - 72, 1),
-        jnp.where(lane < 72, pltpu.roll(lists[1], LANES - 24, 1), pltpu.roll(lists[0], 24, 1)),
-    )
-    names = jnp.concatenate(
-        [jnp.where(lane < 96, left, -1.0), jnp.where(lane < 96, right, -1.0)], axis=1
-    ).astype(jnp.int32)
-    wide = lane_iota((8, 256))
-    second = ((wide >= 48) & (wide < 128)) | ((wide >= 152) & (wide < 200))
-    column = jnp.where(names < 0, -1, (names & 255) + jnp.where(second, 256, 0))
-    pick = one_hot(column[0:1] == row_iota((512, 256)))
-    pick_out[...] = pick
-    meet_out[...] = mm(place, pick).astype(BF)
-    send_kinds_out[...] = jnp.where((names >> 8) == row_iota((8, 256)), 1.0, 0.0)
-
-
-def arrive_kernel(
-    toward, across, back, kept, arrive, pick, send_kinds, trace, state_out, first_out, second_out
-):
-    got = jnp.concatenate(sides(*arrived(toward[...], across[...], back[...])), axis=0)
-    high, low = split(jnp.transpose(got))
-    state = kept[...] + (mm(high, arrive[...]) + mm(low, arrive[...]))
-    state_out[...] = state
-    sent = picked_traces(state, pick[...], send_kinds[...], trace[...])
-    first_out[...], second_out[...] = sides(sent[:, :LANES], sent[:, LANES:])
+    meet_out[...] = mm(place, pick[...]).astype(BF)
 
 
 def force_kernel(first, second, third, packed, after, out):
@@ -355,18 +348,27 @@
     out[...] = mm(high, source) + mm(low, source)
 
 
-def force_depart_kernel(
-    mine, other, select, keep, own_first, own_second, first_out, second_out, kept_out
+def came_columns(first, second):
+    return split(jnp.transpose(jnp.concatenate(sides(first, second), axis=0)))
+
+
+def leave_kernel(
+    first, second, base, arrive_pick, send_kinds, trace, force_mine, force_other, select,
+    wide_first, wide_second, own_first, own_second,
 ):
-    force = jnp.concatenate(chip_halves(mine[...], other[...]), axis=1)
+    chosen = [mm(term, arrive_pick[...]).astype(BF) for term in came_columns(first[...], second[...])]
+    shown = mm(trace[...], jnp.concatenate(chosen, axis=1))
+    sent = base[...] + of_kind(shown[:, :256] + shown[:, 256:], send_kinds[...])
+    own = sides(sent[:, :LANES], sent[:, LANES:])
+    force = jnp.concatenate(chip_halves(force_mine[...], force_other[...]), axis=1)
     high, low = split(force)
-    sent = mm_nt(select[...], high) + mm_nt(select[...], low)
-    pieces = sides(sent[0:48], sent[48:96])
-    for out, piece, own in ((first_out, pieces[0], own_first), (second_out, pieces[1], own_second)):
-        out[:, 0:192] = piece
-        out[:, 192:256] = jnp.zeros((48, 64), F32)
-        out[:, 256:384] = own[...]
-    kept_out[...] = mm_nt(high, keep[...]) + mm_nt(low, keep[...])
+    moved = mm_nt(select[...], high) + mm_nt(select[...], low)
+    pieces = sides(moved[0:48], moved[48:96])
+    for wide, piece, part in zip((wide_first, wide_second), pieces, own):
+        wide[:, 0:192] = piece
+        wide[:, 192:256] = jnp.zeros((48, 64), F32)
+        wide[:, 256:384] = part
+    own_first[...], own_second[...] = own
 
 
 def near_rates(state, near, interior, trace, lift_two):
@@ -393,75 +395,81 @@
     return jnp.where(acoustic, F32(SEGMENT_WEIGHTS[segment]), F32(0.0))
 
 
-def first_inner_kernel(state, near, interior, trace, lift_two, carry_out):
-    carry_out[...] = TIME_STEP * near_rates(
-        state[...], near, interior[...], trace[...], lift_two[...]
-    )
+def first_inner_kernel(
+    first, second, kept, arrive, force_mine, force_other, keep, near, interior, trace, lift_two,
+    pick, send_kinds, state_out, carry_out, force_out, base_out,
+):
+    high, low = came_columns(first[...], second[...])
+    state = kept[...] + (mm(high, arrive[...]) + mm(low, arrive[...]))
+    state_out[...] = state
+    high, low = split(jnp.concatenate(chip_halves(force_mine[...], force_other[...]), axis=1))
+    force = mm_nt(high, keep[...]) + mm_nt(low, keep[...])
+    force_out[...] = force
+    own = TIME_STEP * near_rates(state, near, interior[...], trace[...], lift_two[...])
+    own = jnp.concatenate([own[0:64], own[64:256] + TIME_STEP * force], axis=0)
+    carry_out[...] = own
+    ahead = state + weight_of(0) * own
+    base_out[...] = picked_traces(ahead, pick[...], send_kinds[...], trace[...])
 
 
 def first_outer_kernel(
-    toward, across, back, sent_first, sent_second, state, carry, kinds, place, lift_two,
-    kept_force, arrive, pick, send_kinds, trace,
-    state_out, carry_out, first_out, second_out, force_out,
+    first, second, sent_first, sent_second, kinds, meet, reach, send_kinds, base, trace, arrive_pick,
+    stacks_out, first_out, second_out,
 ):
-    came = arrived(toward[...], across[...], back[...])
     stacks = by_kind(
-        (came[0][:, 256:384], came[1][:, 256:384]), (sent_first[...], sent_second[...]), kinds[...]
-    )
-    rates = far_rates(stacks, place[...], lift_two[...])
-    got = jnp.concatenate(sides(came[0][:, 0:256], came[1][:, 0:256]), axis=0)
-    high, low = split(jnp.transpose(got)[0:192])
-    force = kept_force[...] + (mm(high, arrive[...]) + mm(low, arrive[...]))
-    force_out[...] = force
+        (first[:, 256:384], second[:, 256:384]), (sent_first[...], sent_second[...]), kinds[...]
+    )
+    stacks_out[...] = stacks
+    shown = LIFT * mm(reach[...], mm(stacks, meet[...]).astype(BF))
+    chosen = [
+        jnp.concatenate([jnp.zeros((64, 256), BF), mm(term[0:192], arrive_pick[...]).astype(BF)], axis=0)
+        for term in came_columns(first[:, 0:256], second[:, 0:256])
+    ]
+    pushed = mm(trace[...], jnp.concatenate(chosen, axis=1))
+    shown = shown + (pushed[:, :256] + pushed[:, 256:])
+    sent = base[...] + (weight_of(0) * F32(TIME_STEP)) * of_kind(shown, send_kinds[...])
+    first_out[...], second_out[...] = sides(sent[:, :LANES], sent[:, LANES:])
+
+
+def inner_kernel(segment, state, carry, force, stacks, place, near, interior, trace, lift_two, *refs):
+    rates = far_rates(stacks[...], place[...], lift_two[...])
     carry_now = carry[...] + (LIFT * TIME_STEP) * rates
-    carry_now = jnp.concatenate([carry_now[0:64], carry_now[64:256] + TIME_STEP * force], axis=0)
-    state_now = state[...] + weight_of(0) * carry_now
-    state_out[...] = state_now
-    carry_out[...] = carry_now
-    sent = picked_traces(state_now, pick[...], send_kinds[...], trace[...])
-    first_out[...], second_out[...] = sides(sent[:, :LANES], sent[:, LANES:])
-
-
-def inner_kernel(segment, state, carry, force, near, interior, trace, lift_two, *refs):
+    force = force[...]
     if segment == 1:
-        state_now, carry_now = state[...], carry[...]
-    else:
-        (stacks, place), refs = refs[:2], refs[2:]
-        rates = far_rates(stacks[...], place[...], lift_two[...])
-        carry_now = carry[...] + (LIFT * TIME_STEP) * rates
-        state_now = state[...] + weight_of(segment - 1) * carry_now
+        (first, second, arrive), refs = refs[:3], refs[3:]
+        high, low = came_columns(first[:, 0:256], second[:, 0:256])
+        came = mm(high[0:192], arrive[...]) + mm(low[0:192], arrive[...])
+        carry_now = jnp.concatenate([carry_now[0:64], carry_now[64:256] + TIME_STEP * came], axis=0)
+        force = force + came
+    state_now = state[...] + weight_of(segment - 1) * carry_now
     rates = near_rates(state_now, near, interior[...], trace[...], lift_two[...])
     own = SEGMENT_CARRY[segment] * carry_now + TIME_STEP * rates
-    own = jnp.concatenate([own[0:64], own[64:256] + TIME_STEP * force[...]], axis=0)
+    own = jnp.concatenate([own[0:64], own[64:256] + TIME_STEP * force], axis=0)
     ahead = state_now + weight_of(segment) * own
     if segment == 4:
         refs[0][...] = jnp.where(core_number() == 0, ahead[:, 0:256], ahead[:, 256:512])
         return
-    pick, send_kinds, state_out, carry_out, base_out = refs
+    (pick, send_kinds, state_out, carry_out, base_out), refs = refs[:5], refs[5:]
     state_out[...] = state_now
     carry_out[...] = own
     base_out[...] = picked_traces(ahead, pick[...], send_kinds[...], trace[...])
+    if segment == 1:
+        refs[0][...] = force
 
 
 def outer_kernel(
-    segment, toward, across, back, sent_first, sent_second, kinds, meet, reach, send_kinds, base,
+    segment, first, second, sent_first, sent_second, kinds, meet, reach, send_kinds, base,
     stacks_out, first_out, second_out,
 ):
-    stacks = by_kind(
-        arrived(toward[...], across[...], back[...]), (sent_first[...], sent_second[...]), kinds[...]
-    )
+    stacks = by_kind((first[...], second[...]), (sent_first[...], sent_second[...]), kinds[...])
     stacks_out[...] = stacks
     shown = mm(reach[...], mm(stacks, meet[...]).astype(BF))
     sent = base[...] + (weight_of(segment) * F32(LIFT * TIME_STEP)) * of_kind(shown, send_kinds[...])
     first_out[...], second_out[...] = sides(sent[:, :LANES], sent[:, LANES:])
 
 
-def last_kernel(
-    toward, across, back, sent_first, sent_second, kinds, own_place, lift_two, ahead, out
-):
-    stacks = by_kind(
-        arrived(toward[...], across[...], back[...]), (sent_first[...], sent_second[...]), kinds[...]
-    )
+def last_kernel(first, second, sent_first, sent_second, kinds, own_place, lift_two, ahead, out):
+    stacks = by_kind((first[...], second[...]), (sent_first[...], sent_second[...]), kinds[...])
     rates = far_rates(stacks, own_place[...], lift_two[...])
     out[...] = ahead[...] + (weight_of(4) * F32(LIFT * TIME_STEP)) * rates
 
@@ -485,20 +493,14 @@
 
 def trade(first, second, sections):
     count = lax.axis_size("dom")
-    toward, across, back = [], [], []
-    for section in sections:
-        for dom in range(count - 2):
-            chip, low = dom >> 1, section * count + dom
-            if chip & 1:
-                across += [(low, low + 2), (low + 2, low)]
-            elif chip & 2:
-                toward.append((low, low + 2))
-                back.append((low + 2, low))
-            else:
-                toward.append((low + 2, low))
-                back.append((low, low + 2))
     came = []
-    for value, pairs in ((second, toward), (first, across), (second, back)):
+    for value, odd in ((first, 1), (second, 0)):
+        pairs = []
+        for section in sections:
+            for dom in range(count - 2):
+                if (dom >> 1) & 1 == odd:
+                    low = section * count + dom
+                    pairs += [(low, low + 2), (low + 2, low)]
         came.append(lax.ppermute(value, ("sec", "dom"), pairs))
     return came
 
@@ -534,69 +536,81 @@
     for section in (1, 2, 3):
         lamb_parts.append(lax.ppermute(lamb, "sec", [(0, section)]))
     other = swap(packed)
-    *leaving, chip, select, keep, arrive = call(
+    *leaving, select, ranks = call(
         depart_kernel,
+        [arr(48, 256), arr(48, 256), arr(96, 512, dtype=BF), arr(32, 256)],
+        packed,
+        other,
+    )
+    moved = trade(*leaving, every)
+    kept, keep, arrive, pick, send_kinds, arrive_pick, base = call(
+        places_kernel,
         [
-            arr(48, 256),
-            arr(48, 256),
-            arr(264, 512),
-            arr(96, 512, dtype=BF),
+            whole,
             arr(512, 512, dtype=BF),
             arr(96, 512, dtype=BF),
+            arr(512, 256, dtype=BF),
+            arr(8, 256),
+            arr(96, 256, dtype=BF),
+            arr(TRACE_ROWS, 256),
         ],
         packed,
         other,
-    )
-    moved = trade(*leaving, every)
-    kept, near, place, own_place, kinds, pick, send_kinds, meet = call(
-        tables_kernel,
+        ranks,
+        trace,
+    )
+    (force_mine,) = call(force_kernel, [arr(192, 256)], *lamb_parts, packed, send_kinds)
+    force_other = swap(force_mine)
+    *wide, own_first, own_second = call(
+        leave_kernel,
+        [arr(48, 384), arr(48, 384), piece, piece],
+        *moved, base, arrive_pick, send_kinds, trace, force_mine, force_other, select,
+    )
+    sent = [own_first, own_second]
+    came = trade(*wide, acoustic)
+    near, place, own_place, kinds, meet = call(
+        faces_kernel,
         [
-            whole,
             arr(12, 256, 256, dtype=BF),
             arr(256, 512, dtype=BF),
             arr(256, 256, dtype=BF),
             arr(8, 256),
-            arr(512, 256, dtype=BF),
-            arr(8, 256),
             arr(256, 256, dtype=BF),
         ],
-        chip,
-        keep,
-    )
-    (force_mine,) = call(force_kernel, [arr(192, 256)], *lamb_parts, packed, kinds)
-    force_other = swap(force_mine)
-    state, *sent = call(
-        arrive_kernel, [whole, piece, piece], *moved, kept, arrive, pick, send_kinds, trace
-    )
-    *wide, kept_force = call(
-        force_depart_kernel,
-        [arr(48, 384), arr(48, 384), arr(192, 512)],
-        force_mine, force_other, select, keep, *sent,
-    )
-    came = trade(*wide, acoustic)
-    (carry,) = call(first_inner_kernel, [whole], state, near, interior, trace, lift_two)
-    state, carry, *later, force = call(
+        packed,
+        other,
+        pick,
+    )
+    state, carry, force, base = call(
+        first_inner_kernel,
+        [whole, whole, arr(192, 512), arr(TRACE_ROWS, 256)],
+        *moved, kept, arrive, force_mine, force_other, keep, near, interior, trace, lift_two,
+        pick, send_kinds,
+    )
+    sending = [arr(12 * TRACE_ROWS, 256, dtype=BF), piece, piece]
+    stacks, *later = call(
         first_outer_kernel,
-        [whole, whole, piece, piece, arr(192, 512)],
-        *came, *sent, state, carry, kinds, place, lift_two, kept_force, arrive, pick, send_kinds, trace,
-    )
-    stacks = None
+        sending,
+        *came, *sent, kinds, meet, reach, send_kinds, base, trace, arrive_pick,
+    )
+    extra = [*came, arrive]
     for segment in range(1, 5):
         sent, came = later, trade(*later, acoustic)
-        args = [state, carry, force, near, interior, trace, lift_two]
-        if segment > 1:
-            args += [stacks, place]
+        inner = functools.partial(inner_kernel, segment)
+        args = [state, carry, force, stacks, place, near, interior, trace, lift_two]
         if segment == 4:
-            (ahead,) = call(functools.partial(inner_kernel, segment), [arr(256, 256)], *args)
+            (ahead,) = call(inner, [arr(256, 256)], *args)
             break
-        state, carry, base = call(
-            functools.partial(inner_kernel, segment),
-            [whole, whole, arr(TRACE_ROWS, 256)],
-            *args, pick, send_kinds,
-        )
+        outs = [whole, whole, arr(TRACE_ROWS, 256)]
+        if segment == 1:
+            state, carry, base, force = call(
+                inner, [*outs, arr(192, 512)], *args, *extra, pick, send_kinds
+            )
+        else:
+            state, carry, base = call(inner, outs, *args, pick, send_kinds)
         stacks, *later = call(
             functools.partial(outer_kernel, segment),
-            [arr(12 * TRACE_ROWS, 256, dtype=BF), piece, piece],
+            sending,
             *came, *sent, kinds, meet, reach, send_kinds, base,
         )
     (out,) = call(

time: 99.3 us -> 88.9 us (0.90)
  waiting for transfers between devices: 29.2 us -> 23.1 us
  starting transfers between devices: 51 us -> 45.7 us
  Pallas kernels: 17.1 us -> 18.3 us
    ppermute x18 -> x12, waiting for transfers between devices: 18.3 us -> 11.5 us  [trade(): came.append(lax.ppermute(value, ('sec', 'dom'), pairs))]
    ppermute x18 -> x12, starting transfers between devices: 44.4 us -> 39.2 us  [trade(): came.append(lax.ppermute(value, ('sec', 'dom'), pairs))]
    pallas_call x16, Pallas kernels: 17.1 us -> 18.3 us  [call(): pl.pallas_call(kernel, out_shape=list(outs), in_specs=[vmem] * len(args),...]
  transfers between devices with their start and end apart: 23 -> 17, of which waited for: 11 -> 12; matrix products, arithmetic and copies ran while one was open for 0% -> 0% of each run, Pallas kernels for 12% -> 16%
where the time goes in v1:
time: 88.9 us; the launch traced here: 88.4 us
  starting transfers between devices  45.7 us (51%)
  waiting for transfers between devices  23.1 us (26%)
  Pallas kernels  18.3 us (21%)
  other arithmetic  1.04 us (1%)
    ppermute x12, starting transfers between devices, trade(): came.append(lax.ppermute(value, ('sec', 'dom'), pairs))  39.2 us
    pallas_call x16, Pallas kernels, call(): pl.pallas_call(kernel, out_shape=list(outs), in_specs=[vmem] * len(args),...  18.3 us
    ppermute x3, waiting for transfers between devices, step(): lamb_parts.append(lax.ppermute(lamb, 'sec', [(0, section)]))  11.6 us
    ppermute x12, waiting for transfers between devices, trade(): came.append(lax.ppermute(value, ('sec', 'dom'), pairs))  11.5 us
    ppermute x2, starting transfers between devices, swap(): lax.ppermute(value, 'dom', [(at, at ^ 1) for at in range(lax.axis_size('d...  3.84 us
    ppermute x3, starting transfers between devices, step(): lamb_parts.append(lax.ppermute(lamb, 'sec', [(0, section)]))  2.64 us
  transfers between devices with their start and end apart: 17, of which 12 were waited for; matrix products, arithmetic and copies ran while one was open for 0% of the time, Pallas kernels for 16%

profile of v1, /device:TPU:250, one launch (start us, length us, event | category | flops | bytes accessed | tf_op | source)
XLA Modules:
  0.0 88.4 jit_solution(10706102573425455058)
XLA Ops:
  0.0 1.0 %pad_add_fusion.mine.packed = f32[264,256]{1,0:T(8,128)S(1)} fusion(f32[256,256]{1,0:T(8,128)} %bitcast.5, s32[1,96]{1,0:T(1,128)} %bitcast.7, s32[1,64]{1,0:T(1,128)} %bitcast.8, s32[1,256]{1,0:T(1,128)} %bitcast.6, s32[6,256]{1,0:T(8,128)} %param.13), kind=kLoop, calls=%fused_computation | loop fusion | flops 337920 | bytes 540288 | tf_op jit(solution)/shard_map/add | solution.py:533
  1.0 1.9 %collective-permute-start = (f32[264,256]{1,0:T(8,128)S(1)}, f32[264,256]{1,0:T(8,128)S(1)}, u32[]{:S(2)}, u32[]{:S(2)}) collective-permute-start(f32[264,256]{1,0:T(8,128)S(1)} %pad_add_fusion.mine.packed), channel_id=1, source_target_pairs={{0,1},{1,0},{2,3},{3,2},{4,5},{5,4},{6,7},{7,6},{8,9},{9,8},{10,11... | collective-permute-start | bytes 811016 | tf_op jit(solution)/shard_map/ppermute | solution.py:509
  4.7 1.3 %collective-permute-start.3 = (f32[192,256]{1,0:T(8,128)S(1)}, f32[192,256]{1,0:T(8,128)S(1)}, u32[]{:S(2)}, u32[]{:S(2)}) collective-permute-start(f32[192,256]{1,0:T(8,128)S(1)} %shard_map.93), channel_id=1, source_target_pairs={{0,128},{1,129},{2,130},{3,131},{4,132},{5,133},{6,134},{7,135},{8... | collective-permute-start | bytes 589832 | tf_op jit(solution)/shard_map/ppermute | solution.py:537
  6.5 1.2 %shard_map.92 = (f32[256,512]{1,0:T(8,128)S(1)}, bf16[512,512]{1,0:T(8,128)(2,1)S(1)}, bf16[96,512]{1,0:T(8,128)(2,1)S(1)}, bf16[512,256]{1,0:T(8,128)(2,1)S(1)}...) custom-call(f32[264,256]{1,0:T(8,128)S(1)} %pad_add_fusion.mine.packed, ...), custom_call_target="tpu_custom_call" | custom-call | flops 1048576 | bytes 2236416 | tf_op jit(solution)/shard_map/pallas_call | solution.py:480
  7.7 11.5 %collective-permute-done.3.first = f32[192,256]{1,0:T(8,128)S(1)} collective-permute-done((f32[192,256]{1,0:T(8,128)S(1)}, f32[192,256]{1,0:T(8,128)S(1)}, u32[]{:S(2)}, u32[]{:S(2)}) %collective-permute-start.3) | collective-permute-done | bytes 196640 | tf_op jit(solution)/shard_map/ppermute | solution.py:537
  19.5 1.9 %collective-permute-start.6 = (f32[192,256]{1,0:T(8,128)S(1)}, f32[192,256]{1,0:T(8,128)S(1)}, u32[]{:S(2)}, u32[]{:S(2)}) collective-permute-start(f32[192,256]{1,0:T(8,128)S(1)} %shard_map.94.force_mine), channel_id=1, source_target_pairs={{0,1},{1,0},{2,3},{3,2},{4,5},{5,4},{6,7},{7,6},{8,9},{9,8},{10,11... | collective-permute-start | bytes 589832 | tf_op jit(solution)/shard_map/ppermute | solution.py:509
  21.4 4.7 %collective-permute-start.1 = (f32[48,256]{1,0:T(8,128)S(1)}, f32[48,256]{1,0:T(8,128)S(1)}, u32[]{:S(2)}, u32[]{:S(2)}) collective-permute-start(f32[48,256]{1,0:T(8,128)S(1)} %get-tuple-element.51), channel_id=1, source_target_pairs={{2,4},{4,2},{3,5},{5,3},{6,8},{8,6},{7,9},{9,7},{10,12},{12,10},{1... | collective-permute-start | bytes 147464 | tf_op jit(solution)/shard_map/ppermute | solution.py:504
  26.1 1.9 %collective-permute-start.2 = (f32[48,256]{1,0:T(8,128)S(1)}, f32[48,256]{1,0:T(8,128)S(1)}, u32[]{:S(2)}, u32[]{:S(2)}) collective-permute-start(f32[48,256]{1,0:T(8,128)S(1)} %get-tuple-element.52), channel_id=1, source_target_pairs={{0,2},{2,0},{1,3},{3,1},{4,6},{6,4},{5,7},{7,5},{8,10},{10,8},{9,1... | collective-permute-start | bytes 147464 | tf_op jit(solution)/shard_map/ppermute | solution.py:504
  28.1 2.7 %collective-permute-done.1.first = f32[48,256]{1,0:T(8,128)S(1)} collective-permute-done((f32[48,256]{1,0:T(8,128)S(1)}, f32[48,256]{1,0:T(8,128)S(1)}, u32[]{:S(2)}, u32[]{:S(2)}) %collective-permute-start.1) | collective-permute-done | bytes 49184 | tf_op jit(solution)/shard_map/ppermute | solution.py:504
  30.8 1.3 %collective-permute-done.2.second = f32[48,256]{1,0:T(8,128)S(1)} collective-permute-done((f32[48,256]{1,0:T(8,128)S(1)}, f32[48,256]{1,0:T(8,128)S(1)}, u32[]{:S(2)}, u32[]{:S(2)}) %collective-permute-start.2) | collective-permute-done | bytes 49184 | tf_op jit(solution)/shard_map/ppermute | solution.py:504
  32.7 4.5 %collective-permute-start.7 = (f32[48,384]{1,0:T(8,128)S(1)}, f32[48,384]{1,0:T(8,128)S(1)}, u32[]{:S(2)}, u32[]{:S(2)}) collective-permute-start(f32[48,384]{1,0:T(8,128)S(1)} %get-tuple-element.58), channel_id=1, source_target_pairs={{130,132},{132,130},{131,133},{133,131},{134,136},{136,134},{135,1... | collective-permute-start | bytes 221192 | tf_op jit(solution)/shard_map/ppermute | solution.py:504
  37.2 1.9 %collective-permute-start.8 = (f32[48,384]{1,0:T(8,128)S(1)}, f32[48,384]{1,0:T(8,128)S(1)}, u32[]{:S(2)}, u32[]{:S(2)}) collective-permute-start(f32[48,384]{1,0:T(8,128)S(1)} %get-tuple-element.59), channel_id=1, source_target_pairs={{128,130},{130,128},{129,131},{131,129},{132,134},{134,132},{133,1... | collective-permute-start | bytes 221192 | tf_op jit(solution)/shard_map/ppermute | solution.py:504
  39.1 1.4 %shard_map.96 = (bf16[12,256,256]{2,1,0:T(8,128)(2,1)S(1)}, bf16[256,512]{1,0:T(8,128)(2,1)S(1)}, bf16[256,256]{1,0:T(8,128)(2,1)S(1)}, f32[8,256]{1,0:T(8,128)S(1)}, bf16[256,256]{1,0:T(8,128)(2,1)S(1)}) custom-call(f32[264,256]{1,0:T(8,128)S(1)} %pad_add_fusion.mine.packed, f32[264,256]{1,0:T(8,128)S(1)} %collective-permute-done.other, ...), custom_call_target="tpu_custom_call" | custom-call | flops 1048576 | bytes 2908160 | tf_op jit(solution)/shard_map/pallas_call | solution.py:480
  40.6 2.1 %shard_map.97 = (f32[256,512]{1,0:T(8,128)S(1)}, f32[256,512]{1,0:T(8,128)S(1)}, f32[192,512]{1,0:T(8,128)S(1)}, f32[48,256]{1,0:T(8,128)S(1)}) custom-call(f32[48,256]{1,0:T(8,128)S(1)} %collective-permute-done.1.first, f32[48,256]{1,0:T(8,128)S(1)} %collective-permute-done.2.second, f32[256,512]{1,0:T(8,128)S(1)} %get-tuple-element.65.kept, ...), custom_call_target="tpu_custom_call" | custom-call | flops 1048576 | bytes 5808128 | tf_op jit(solution)/shard_map/pallas_call | solution.py:480
  44.3 4.7 %collective-permute-start.9 = (f32[48,128]{1,0:T(8,128)S(1)}, f32[48,128]{1,0:T(8,128)S(1)}, u32[]{:S(2)}, u32[]{:S(2)}) collective-permute-start(f32[48,128]{1,0:T(8,128)S(1)} %get-tuple-element.70.sent_first), channel_id=1, source_target_pairs={{130,132},{132,130},{131,133},{133,131},{134,136},{136,134},{135,1... | collective-permute-start | bytes 73736 | tf_op jit(solution)/shard_map/ppermute | solution.py:504
  49.0 1.9 %collective-permute-start.10 = (f32[48,128]{1,0:T(8,128)S(1)}, f32[48,128]{1,0:T(8,128)S(1)}, u32[]{:S(2)}, u32[]{:S(2)}) collective-permute-start(f32[48,128]{1,0:T(8,128)S(1)} %get-tuple-element.71.sent_second), channel_id=1, source_target_pairs={{128,130},{130,128},{129,131},{131,129},{132,134},{134,132},{133,1... | collective-permute-start | bytes 73736 | tf_op jit(solution)/shard_map/ppermute | solution.py:504
  50.9 2.3 %shard_map.99 = (f32[256,512]{1,0:T(8,128)S(1)}, f32[256,512]{1,0:T(8,128)S(1)}, f32[48,256]{1,0:T(8,128)S(1)}, f32[192,512]{1,0:T(8,128)S(1)}) custom-call(f32[256,512]{1,0:T(8,128)S(1)} %get-tuple-element.72.state, f32[256,512]{1,0:T(8,128)S(1)} %get-tuple-element.73.carry, f32[192,512]{1,0:T(8,128)S(1)} %get-tuple-element.74.force, ...), custom_call_target="tpu_custom_call" | custom-call | flops 1048576 | bytes 6414336 | tf_op jit(solution)/shard_map/pallas_call | solution.py:480
  53.3 1.4 %collective-permute-done.10.second = f32[48,128]{1,0:T(8,128)S(1)} collective-permute-done((f32[48,128]{1,0:T(8,128)S(1)}, f32[48,128]{1,0:T(8,128)S(1)}, u32[]{:S(2)}, u32[]{:S(2)}) %collective-permute-start.10) | collective-permute-done | bytes 24608 | tf_op jit(solution)/shard_map/ppermute | solution.py:504
  55.2 4.5 %collective-permute-start.11 = (f32[48,128]{1,0:T(8,128)S(1)}, f32[48,128]{1,0:T(8,128)S(1)}, u32[]{:S(2)}, u32[]{:S(2)}) collective-permute-start(f32[48,128]{1,0:T(8,128)S(1)} %get-tuple-element.78.sent_first), channel_id=1, source_target_pairs={{130,132},{132,130},{131,133},{133,131},{134,136},{136,134},{135,1... | collective-permute-start | bytes 73736 | tf_op jit(solution)/shard_map/ppermute | solution.py:504
  59.7 1.9 %collective-permute-start.12 = (f32[48,128]{1,0:T(8,128)S(1)}, f32[48,128]{1,0:T(8,128)S(1)}, u32[]{:S(2)}, u32[]{:S(2)}) collective-permute-start(f32[48,128]{1,0:T(8,128)S(1)} %get-tuple-element.79.sent_second), channel_id=1, source_target_pairs={{128,130},{130,128},{129,131},{131,129},{132,134},{134,132},{133,1... | collective-permute-start | bytes 73736 | tf_op jit(solution)/shard_map/ppermute | solution.py:504
  61.6 2.1 %shard_map.101 = (f32[256,512]{1,0:T(8,128)S(1)}, f32[256,512]{1,0:T(8,128)S(1)}, f32[48,256]{1,0:T(8,128)S(1)}) custom-call(f32[256,512]{1,0:T(8,128)S(1)} %get-tuple-element.80.state, f32[256,512]{1,0:T(8,128)S(1)} %get-tuple-element.81.carry, f32[192,512]{1,0:T(8,128)S(1)} %get-tuple-element.82.force, bf16[576,256]{1,0:T(8,128)(2,1)S(1)} %get-tuple-element.83.stacks, ...), custom_call_target="tpu_custom_call" | custom-call | flops 1048576 | bytes 5775360 | tf_op jit(solution)/shard_map/pallas_call | solution.py:480
  64.3 1.2 %collective-permute-done.12.second = f32[48,128]{1,0:T(8,128)S(1)} collective-permute-done((f32[48,128]{1,0:T(8,128)S(1)}, f32[48,128]{1,0:T(8,128)S(1)}, u32[]{:S(2)}, u32[]{:S(2)}) %collective-permute-start.12) | collective-permute-done | bytes 24608 | tf_op jit(solution)/shard_map/ppermute | solution.py:504
  66.0 4.7 %collective-permute-start.13 = (f32[48,128]{1,0:T(8,128)S(1)}, f32[48,128]{1,0:T(8,128)S(1)}, u32[]{:S(2)}, u32[]{:S(2)}) collective-permute-start(f32[48,128]{1,0:T(8,128)S(1)} %get-tuple-element.85.sent_first), channel_id=1, source_target_pairs={{130,132},{132,130},{131,133},{133,131},{134,136},{136,134},{135,1... | collective-permute-start | bytes 73736 | tf_op jit(solution)/shard_map/ppermute | solution.py:504
  70.7 2.1 %collective-permute-start.14 = (f32[48,128]{1,0:T(8,128)S(1)}, f32[48,128]{1,0:T(8,128)S(1)}, u32[]{:S(2)}, u32[]{:S(2)}) collective-permute-start(f32[48,128]{1,0:T(8,128)S(1)} %get-tuple-element.86.sent_second), channel_id=1, source_target_pairs={{128,130},{130,128},{129,131},{131,129},{132,134},{134,132},{133,1... | collective-permute-start | bytes 73736 | tf_op jit(solution)/shard_map/ppermute | solution.py:504
  72.8 2.1 %shard_map.103 = (f32[256,512]{1,0:T(8,128)S(1)}, f32[256,512]{1,0:T(8,128)S(1)}, f32[48,256]{1,0:T(8,128)S(1)}) custom-call(f32[256,512]{1,0:T(8,128)S(1)} %get-tuple-element.87.state, f32[256,512]{1,0:T(8,128)S(1)} %get-tuple-element.88.carry, f32[192,512]{1,0:T(8,128)S(1)} %get-tuple-element.82.force, bf16[576,256]{1,0:T(8,128)(2,1)S(1)} %get-tuple-element.89.stacks, ...), custom_call_target="tpu_custom_call" | custom-call | flops 1048576 | bytes 5775360 | tf_op jit(solution)/shard_map/pallas_call | solution.py:480
  75.1 1.4 %collective-permute-done.14.second = f32[48,128]{1,0:T(8,128)S(1)} collective-permute-done((f32[48,128]{1,0:T(8,128)S(1)}, f32[48,128]{1,0:T(8,128)S(1)}, u32[]{:S(2)}, u32[]{:S(2)}) %collective-permute-start.14) | collective-permute-done | bytes 24608 | tf_op jit(solution)/shard_map/ppermute | solution.py:504
  77.0 4.5 %collective-permute-start.15 = (f32[48,128]{1,0:T(8,128)S(1)}, f32[48,128]{1,0:T(8,128)S(1)}, u32[]{:S(2)}, u32[]{:S(2)}) collective-permute-start(f32[48,128]{1,0:T(8,128)S(1)} %get-tuple-element.91.sent_first), channel_id=1, source_target_pairs={{130,132},{132,130},{131,133},{133,131},{134,136},{136,134},{135,1... | collective-permute-start | bytes 73736 | tf_op jit(solution)/shard_map/ppermute | solution.py:504
  81.5 1.9 %collective-permute-start.16 = (f32[48,128]{1,0:T(8,128)S(1)}, f32[48,128]{1,0:T(8,128)S(1)}, u32[]{:S(2)}, u32[]{:S(2)}) collective-permute-start(f32[48,128]{1,0:T(8,128)S(1)} %get-tuple-element.92.sent_second), channel_id=1, source_target_pairs={{128,130},{130,128},{129,131},{131,129},{132,134},{134,132},{133,1... | collective-permute-start | bytes 73736 | tf_op jit(solution)/shard_map/ppermute | solution.py:504
  83.4 1.7 %shard_map.105.ahead = f32[256,256]{1,0:T(8,128)S(1)} custom-call(f32[256,512]{1,0:T(8,128)S(1)} %get-tuple-element.94.state, f32[256,512]{1,0:T(8,128)S(1)} %get-tuple-element.95.carry, f32[192,512]{1,0:T(8,128)S(1)} %get-tuple-element.82.force, bf16[576,256]{1,0:T(8,128)(2,1)S(1)} %get-tuple-element.96.stacks, ...), custom_call_target="tpu_custom_call" | custom-call | flops 1048576 | bytes 4669440 | tf_op jit(solution)/shard_map/pallas_call | solution.py:480
  85.1 0.9 %collective-permute-done.15.first = f32[48,128]{1,0:T(8,128)S(1)} collective-permute-done((f32[48,128]{1,0:T(8,128)S(1)}, f32[48,128]{1,0:T(8,128)S(1)}, u32[]{:S(2)}, u32[]{:S(2)}) %collective-permute-start.15) | collective-permute-done | bytes 24608 | tf_op jit(solution)/shard_map/ppermute | solution.py:504
  86.0 1.2 %collective-permute-done.16.second = f32[48,128]{1,0:T(8,128)S(1)} collective-permute-done((f32[48,128]{1,0:T(8,128)S(1)}, f32[48,128]{1,0:T(8,128)S(1)}, u32[]{:S(2)}, u32[]{:S(2)}) %collective-permute-start.16) | collective-permute-done | bytes 24608 | tf_op jit(solution)/shard_map/ppermute | solution.py:504
  87.2 1.2 %shard_map.106 = f32[256,256]{1,0:T(8,128)} custom-call(f32[48,128]{1,0:T(8,128)S(1)} %collective-permute-done.15.first, f32[48,128]{1,0:T(8,128)S(1)} %collective-permute-done.16.second, f32[48,128]{1,0:T(8,128)S(1)} %get-tuple-element.91.sent_first, f32[48,128]{1,0:T(8,128)S(1)} %get-tuple-element.92.sent_second, f32[8,256]{1,0:T(8,128)S(1)} %get-tuple-element.63.kinds, ...), custom_call_target="tpu_custom_call" | custom-call | flops 1048576 | bytes 1056768 | tf_op jit(solution)/shard_map/pallas_call | solution.py:480
  (27 shorter events, 7.0 us)
Async XLA Ops:
  0.0 6.5 %copy-start.2 = (bf16[288,256]{1,0:T(8,128)(2,1)S(1)}, bf16[288,256]{1,0:T(8,128)(2,1)}, u32[]{:S(2)}) copy-start(bf16[288,256]{1,0:T(8,128)(2,1)} %constant.13.clone.trace) | copy-start | bytes 442372
  1.0 4.9 %collective-permute-start = (f32[264,256]{1,0:T(8,128)S(1)}, f32[264,256]{1,0:T(8,128)S(1)}, u32[]{:S(2)}, u32[]{:S(2)}) collective-permute-start(f32[264,256]{1,0:T(8,128)S(1)} %pad_add_fusion.mine.packed), channel_id=1, source_target_pairs={{0,1},{1,0},{2,3},{3,2},{4,5},{5,4},{6,7},{7,6},{8,9},{9,8},{10,11... | collective-permute-start | bytes 811016 | tf_op jit(solution)/shard_map/ppermute | solution.py:509
  3.3 4.4 %collective-permute-start.5 = (f32[192,256]{1,0:T(8,128)S(1)}, f32[192,256]{1,0:T(8,128)S(1)}, u32[]{:S(2)}, u32[]{:S(2)}) collective-permute-start(f32[192,256]{1,0:T(8,128)S(1)} %shard_map.93), channel_id=1, source_target_pairs={{0,384},{1,385},{2,386},{3,387},{4,388},{5,389},{6,390},{7,391},{8... | collective-permute-start | bytes 589832 | tf_op jit(solution)/shard_map/ppermute | solution.py:537
  4.0 3.8 %collective-permute-start.4 = (f32[192,256]{1,0:T(8,128)S(1)}, f32[192,256]{1,0:T(8,128)S(1)}, u32[]{:S(2)}, u32[]{:S(2)}) collective-permute-start(f32[192,256]{1,0:T(8,128)S(1)} %shard_map.93), channel_id=1, source_target_pairs={{0,256},{1,257},{2,258},{3,259},{4,260},{5,261},{6,262},{7,263},{8... | collective-permute-start | bytes 589832 | tf_op jit(solution)/shard_map/ppermute | solution.py:537
  4.7 14.6 %collective-permute-start.3 = (f32[192,256]{1,0:T(8,128)S(1)}, f32[192,256]{1,0:T(8,128)S(1)}, u32[]{:S(2)}, u32[]{:S(2)}) collective-permute-start(f32[192,256]{1,0:T(8,128)S(1)} %shard_map.93), channel_id=1, source_target_pairs={{0,128},{1,129},{2,130},{3,131},{4,132},{5,133},{6,134},{7,135},{8... | collective-permute-start | bytes 589832 | tf_op jit(solution)/shard_map/ppermute | solution.py:537
  6.5 34.0 %copy-start = (bf16[256,576]{1,0:T(8,128)(2,1)S(1)}, bf16[256,576]{1,0:T(8,128)(2,1)}, u32[]{:S(2)}) copy-start(bf16[256,576]{1,0:T(8,128)(2,1)} %constant.14.clone.lift_two) | copy-start | bytes 884740
  6.5 34.0 %copy-start.1 = (bf16[256,768]{1,0:T(8,128)(2,1)S(1)}, bf16[256,768]{1,0:T(8,128)(2,1)}, u32[]{:S(2)}) copy-start(bf16[256,768]{1,0:T(8,128)(2,1)} %constant.12.clone.interior) | copy-start | bytes 1179652
  19.5 12.6 %collective-permute-start.6 = (f32[192,256]{1,0:T(8,128)S(1)}, f32[192,256]{1,0:T(8,128)S(1)}, u32[]{:S(2)}, u32[]{:S(2)}) collective-permute-start(f32[192,256]{1,0:T(8,128)S(1)} %shard_map.94.force_mine), channel_id=1, source_target_pairs={{0,1},{1,0},{2,3},{3,2},{4,5},{5,4},{6,7},{7,6},{8,9},{9,8},{10,11... | collective-permute-start | bytes 589832 | tf_op jit(solution)/shard_map/ppermute | solution.py:509
  21.4 9.4 %collective-permute-start.1 = (f32[48,256]{1,0:T(8,128)S(1)}, f32[48,256]{1,0:T(8,128)S(1)}, u32[]{:S(2)}, u32[]{:S(2)}) collective-permute-start(f32[48,256]{1,0:T(8,128)S(1)} %get-tuple-element.51), channel_id=1, source_target_pairs={{2,4},{4,2},{3,5},{5,3},{6,8},{8,6},{7,9},{9,7},{10,12},{12,10},{1... | collective-permute-start | bytes 147464 | tf_op jit(solution)/shard_map/ppermute | solution.py:504
  26.1 6.0 %collective-permute-start.2 = (f32[48,256]{1,0:T(8,128)S(1)}, f32[48,256]{1,0:T(8,128)S(1)}, u32[]{:S(2)}, u32[]{:S(2)}) collective-permute-start(f32[48,256]{1,0:T(8,128)S(1)} %get-tuple-element.52), channel_id=1, source_target_pairs={{0,2},{2,0},{1,3},{3,1},{4,6},{6,4},{5,7},{7,5},{8,10},{10,8},{9,1... | collective-permute-start | bytes 147464 | tf_op jit(solution)/shard_map/ppermute | solution.py:504
  32.7 9.9 %collective-permute-start.7 = (f32[48,384]{1,0:T(8,128)S(1)}, f32[48,384]{1,0:T(8,128)S(1)}, u32[]{:S(2)}, u32[]{:S(2)}) collective-permute-start(f32[48,384]{1,0:T(8,128)S(1)} %get-tuple-element.58), channel_id=1, source_target_pairs={{130,132},{132,130},{131,133},{133,131},{134,136},{136,134},{135,1... | collective-permute-start | bytes 221192 | tf_op jit(solution)/shard_map/ppermute | solution.py:504
  37.2 6.2 %collective-permute-start.8 = (f32[48,384]{1,0:T(8,128)S(1)}, f32[48,384]{1,0:T(8,128)S(1)}, u32[]{:S(2)}, u32[]{:S(2)}) collective-permute-start(f32[48,384]{1,0:T(8,128)S(1)} %get-tuple-element.59), channel_id=1, source_target_pairs={{128,130},{130,128},{129,131},{131,129},{132,134},{134,132},{133,1... | collective-permute-start | bytes 221192 | tf_op jit(solution)/shard_map/ppermute | solution.py:504
  40.5 2.9 %copy-start.3 = (bf16[288,576]{1,0:T(8,128)(2,1)S(1)}, bf16[288,576]{1,0:T(8,128)(2,1)}, u32[]{:S(2)}) copy-start(bf16[288,576]{1,0:T(8,128)(2,1)} %constant.15.clone.reach) | copy-start | bytes 995332
  44.3 9.0 %collective-permute-start.9 = (f32[48,128]{1,0:T(8,128)S(1)}, f32[48,128]{1,0:T(8,128)S(1)}, u32[]{:S(2)}, u32[]{:S(2)}) collective-permute-start(f32[48,128]{1,0:T(8,128)S(1)} %get-tuple-element.70.sent_first), channel_id=1, source_target_pairs={{130,132},{132,130},{131,133},{133,131},{134,136},{136,134},{135,1... | collective-permute-start | bytes 73736 | tf_op jit(solution)/shard_map/ppermute | solution.py:504
  49.0 5.7 %collective-permute-start.10 = (f32[48,128]{1,0:T(8,128)S(1)}, f32[48,128]{1,0:T(8,128)S(1)}, u32[]{:S(2)}, u32[]{:S(2)}) collective-permute-start(f32[48,128]{1,0:T(8,128)S(1)} %get-tuple-element.71.sent_second), channel_id=1, source_target_pairs={{128,130},{130,128},{129,131},{131,129},{132,134},{134,132},{133,1... | collective-permute-start | bytes 73736 | tf_op jit(solution)/shard_map/ppermute | solution.py:504
  55.2 9.0 %collective-permute-start.11 = (f32[48,128]{1,0:T(8,128)S(1)}, f32[48,128]{1,0:T(8,128)S(1)}, u32[]{:S(2)}, u32[]{:S(2)}) collective-permute-start(f32[48,128]{1,0:T(8,128)S(1)} %get-tuple-element.78.sent_first), channel_id=1, source_target_pairs={{130,132},{132,130},{131,133},{133,131},{134,136},{136,134},{135,1... | collective-permute-start | bytes 73736 | tf_op jit(solution)/shard_map/ppermute | solution.py:504
  59.7 5.7 %collective-permute-start.12 = (f32[48,128]{1,0:T(8,128)S(1)}, f32[48,128]{1,0:T(8,128)S(1)}, u32[]{:S(2)}, u32[]{:S(2)}) collective-permute-start(f32[48,128]{1,0:T(8,128)S(1)} %get-tuple-element.79.sent_second), channel_id=1, source_target_pairs={{128,130},{130,128},{129,131},{131,129},{132,134},{134,132},{133,1... | collective-permute-start | bytes 73736 | tf_op jit(solution)/shard_map/ppermute | solution.py:504
  66.0 9.0 %collective-permute-start.13 = (f32[48,128]{1,0:T(8,128)S(1)}, f32[48,128]{1,0:T(8,128)S(1)}, u32[]{:S(2)}, u32[]{:S(2)}) collective-permute-start(f32[48,128]{1,0:T(8,128)S(1)} %get-tuple-element.85.sent_first), channel_id=1, source_target_pairs={{130,132},{132,130},{131,133},{133,131},{134,136},{136,134},{135,1... | collective-permute-start | bytes 73736 | tf_op jit(solution)/shard_map/ppermute | solution.py:504
  70.7 5.7 %collective-permute-start.14 = (f32[48,128]{1,0:T(8,128)S(1)}, f32[48,128]{1,0:T(8,128)S(1)}, u32[]{:S(2)}, u32[]{:S(2)}) collective-permute-start(f32[48,128]{1,0:T(8,128)S(1)} %get-tuple-element.86.sent_second), channel_id=1, source_target_pairs={{128,130},{130,128},{129,131},{131,129},{132,134},{134,132},{133,1... | collective-permute-start | bytes 73736 | tf_op jit(solution)/shard_map/ppermute | solution.py:504
  77.0 9.0 %collective-permute-start.15 = (f32[48,128]{1,0:T(8,128)S(1)}, f32[48,128]{1,0:T(8,128)S(1)}, u32[]{:S(2)}, u32[]{:S(2)}) collective-permute-start(f32[48,128]{1,0:T(8,128)S(1)} %get-tuple-element.91.sent_first), channel_id=1, source_target_pairs={{130,132},{132,130},{131,133},{133,131},{134,136},{136,134},{135,1... | collective-permute-start | bytes 73736 | tf_op jit(solution)/shard_map/ppermute | solution.py:504
  81.5 5.7 %collective-permute-start.16 = (f32[48,128]{1,0:T(8,128)S(1)}, f32[48,128]{1,0:T(8,128)S(1)}, u32[]{:S(2)}, u32[]{:S(2)}) collective-permute-start(f32[48,128]{1,0:T(8,128)S(1)} %get-tuple-element.92.sent_second), channel_id=1, source_target_pairs={{128,130},{130,128},{129,131},{131,129},{132,134},{134,132},{133,1... | collective-permute-start | bytes 73736 | tf_op jit(solution)/shard_map/ppermute | solution.py:504

commit v2 on v1

--- a/solution.py
+++ b/solution.py
@@ -341,7 +341,7 @@
     meet_out[...] = mm(place, pick[...]).astype(BF)
 
 
-def force_kernel(first, second, third, packed, after, out):
+def force_kernel(first, second, third, packed, out):
     lamb = first[...] + second[...] + third[...]
     high, low = split(lamb)
     source = one_hot(packed[262:263].astype(jnp.int32) == row_iota((256, 256)))
@@ -468,20 +468,30 @@
     first_out[...], second_out[...] = sides(sent[:, :LANES], sent[:, LANES:])
 
 
-def last_kernel(first, second, sent_first, sent_second, kinds, own_place, lift_two, ahead, out):
+def last_kernel(
+    first, second, sent_first, sent_second, kinds, own_place, lift_two, ahead, out, held, done
+):
     stacks = by_kind((first[...], second[...]), (sent_first[...], sent_second[...]), kinds[...])
-    rates = far_rates(stacks, own_place[...], lift_two[...])
-    out[...] = ahead[...] + (weight_of(4) * F32(LIFT * TIME_STEP)) * rates
-
-
-def call(kernel, outs, *args, flops=1 << 20):
+    outside = mm(stacks, own_place[...]).astype(BF)
+    scale = weight_of(4) * F32(LIFT * TIME_STEP)
+    copies = []
+    for number, rows in enumerate((slice(0, 128), slice(128, 256))):
+        held[rows] = ahead[rows] + scale * mm(lift_two[rows], outside)
+        copies.append(pltpu.make_async_copy(held.at[rows], out.at[rows], done.at[number]))
+        copies[-1].start()
+    for copy in copies:
+        copy.wait()
+
+
+def call(kernel, outs, *args, flops=1 << 20, far=False, scratch=()):
     vmem = pl.BlockSpec(memory_space=pltpu.VMEM)
     size = sum(int(np.prod(a.shape)) * a.dtype.itemsize for a in (*args, *outs))
     return pl.pallas_call(
         kernel,
         out_shape=list(outs),
         in_specs=[vmem] * len(args),
-        out_specs=[vmem] * len(outs),
+        out_specs=[pl.BlockSpec(memory_space=pl.ANY) if far else vmem] * len(outs),
+        scratch_shapes=list(scratch),
         compiler_params=pltpu.CompilerParams(vmem_limit_bytes=32 << 20),
         cost_estimate=pl.CostEstimate(flops=flops, bytes_accessed=size, transcendentals=0),
     )(*args)
@@ -543,6 +553,8 @@
         other,
     )
     moved = trade(*leaving, every)
+    (force_mine,) = call(force_kernel, [arr(192, 256)], *lamb_parts, packed)
+    force_other = swap(force_mine)
     kept, keep, arrive, pick, send_kinds, arrive_pick, base = call(
         places_kernel,
         [
@@ -559,8 +571,6 @@
         ranks,
         trace,
     )
-    (force_mine,) = call(force_kernel, [arr(192, 256)], *lamb_parts, packed, send_kinds)
-    force_other = swap(force_mine)
     *wide, own_first, own_second = call(
         leave_kernel,
         [arr(48, 384), arr(48, 384), piece, piece],
@@ -614,7 +624,11 @@
             *came, *sent, kinds, meet, reach, send_kinds, base,
         )
     (out,) = call(
-        last_kernel, [arr(256, 256)], *came, *sent, kinds, own_place, lift_two, ahead
+        last_kernel,
+        [arr(256, 256)],
+        *came, *sent, kinds, own_place, lift_two, ahead,
+        far=True,
+        scratch=(pltpu.VMEM((256, 256), F32), pltpu.SemaphoreType.DMA((2,))),
     )
     return out.reshape(4, 64, ELEMENTS)
 

time: 88.9 us -> 87.2 us (0.981)
  the two profiles are of different devices: /device:TPU:250 before, /device:TPU:258 now
where the time goes in v2:
time: 87.2 us; the launch traced here: 86.7 us
  starting transfers between devices  46.6 us (53%)
  waiting for transfers between devices  20.3 us (23%)
  Pallas kernels  18.3 us (21%)
  other arithmetic  1.04 us (1%)
    ppermute x12, starting transfers between devices, trade(): came.append(lax.ppermute(value, ('sec', 'dom'), pairs))  40 us
    pallas_call x16, Pallas kernels, call(): pl.pallas_call(kernel, out_shape=list(outs), in_specs=[vmem] * len(args),...  18.3 us
    ppermute x3, waiting for transfers between devices, step(): lamb_parts.append(lax.ppermute(lamb, 'sec', [(0, section)]))  10.7 us
    ppermute x12, waiting for transfers between devices, trade(): came.append(lax.ppermute(value, ('sec', 'dom'), pairs))  9.53 us
    ppermute x2, starting transfers between devices, swap(): lax.ppermute(value, 'dom', [(at, at ^ 1) for at in range(lax.axis_size('d...  3.97 us
    ppermute x3, starting transfers between devices, step(): lamb_parts.append(lax.ppermute(lamb, 'sec', [(0, section)]))  2.64 us
  transfers between devices with their start and end apart: 17, of which 12 were waited for; matrix products, arithmetic and copies ran while one was open for 0% of the time, Pallas kernels for 16%

profile of v2, /device:TPU:258, one launch (start us, length us, event | category | flops | bytes accessed | tf_op | source)
XLA Modules:
  0.0 86.7 jit_solution(15574812446069602940)
XLA Ops:
  0.0 1.0 %pad_add_fusion.mine.packed = f32[264,256]{1,0:T(8,128)S(1)} fusion(f32[256,256]{1,0:T(8,128)} %bitcast.5, s32[1,96]{1,0:T(1,128)} %bitcast.7, s32[1,64]{1,0:T(1,128)} %bitcast.8, s32[1,256]{1,0:T(1,128)} %bitcast.6, s32[6,256]{1,0:T(8,128)} %param.13), kind=kLoop, calls=%fused_computation | loop fusion | flops 337920 | bytes 540288 | tf_op jit(solution)/shard_map/add | solution.py:543
  2.7 1.3 %collective-permute-start.3 = (f32[192,256]{1,0:T(8,128)S(1)}, f32[192,256]{1,0:T(8,128)S(1)}, u32[]{:S(2)}, u32[]{:S(2)}) collective-permute-start(f32[192,256]{1,0:T(8,128)S(1)} %shard_map.93), channel_id=1, source_target_pairs={{0,128},{1,129},{2,130},{3,131},{4,132},{5,133},{6,134},{7,135},{8... | collective-permute-start | bytes 589832 | tf_op jit(solution)/shard_map/ppermute | solution.py:547
  4.0 1.9 %collective-permute-start = (f32[264,256]{1,0:T(8,128)S(1)}, f32[264,256]{1,0:T(8,128)S(1)}, u32[]{:S(2)}, u32[]{:S(2)}) collective-permute-start(f32[264,256]{1,0:T(8,128)S(1)} %pad_add_fusion.mine.packed), channel_id=1, source_target_pairs={{0,1},{1,0},{2,3},{3,2},{4,5},{5,4},{6,7},{7,6},{8,9},{9,8},{10,11... | collective-permute-start | bytes 811016 | tf_op jit(solution)/shard_map/ppermute | solution.py:519
  6.0 10.7 %collective-permute-done.3.first = f32[192,256]{1,0:T(8,128)S(1)} collective-permute-done((f32[192,256]{1,0:T(8,128)S(1)}, f32[192,256]{1,0:T(8,128)S(1)}, u32[]{:S(2)}, u32[]{:S(2)}) %collective-permute-start.3) | collective-permute-done | bytes 196640 | tf_op jit(solution)/shard_map/ppermute | solution.py:547
  17.0 2.1 %collective-permute-start.6 = (f32[192,256]{1,0:T(8,128)S(1)}, f32[192,256]{1,0:T(8,128)S(1)}, u32[]{:S(2)}, u32[]{:S(2)}) collective-permute-start(f32[192,256]{1,0:T(8,128)S(1)} %shard_map.94.force_mine), channel_id=1, source_target_pairs={{0,1},{1,0},{2,3},{3,2},{4,5},{5,4},{6,7},{7,6},{8,9},{9,8},{10,11... | collective-permute-start | bytes 589832 | tf_op jit(solution)/shard_map/ppermute | solution.py:519
  19.5 4.5 %collective-permute-start.1 = (f32[48,256]{1,0:T(8,128)S(1)}, f32[48,256]{1,0:T(8,128)S(1)}, u32[]{:S(2)}, u32[]{:S(2)}) collective-permute-start(f32[48,256]{1,0:T(8,128)S(1)} %get-tuple-element.51), channel_id=1, source_target_pairs={{2,4},{4,2},{3,5},{5,3},{6,8},{8,6},{7,9},{9,7},{10,12},{12,10},{1... | collective-permute-start | bytes 147464 | tf_op jit(solution)/shard_map/ppermute | solution.py:514
  24.0 2.5 %collective-permute-start.2 = (f32[48,256]{1,0:T(8,128)S(1)}, f32[48,256]{1,0:T(8,128)S(1)}, u32[]{:S(2)}, u32[]{:S(2)}) collective-permute-start(f32[48,256]{1,0:T(8,128)S(1)} %get-tuple-element.52), channel_id=1, source_target_pairs={{0,2},{2,0},{1,3},{3,1},{4,6},{6,4},{5,7},{7,5},{8,10},{10,8},{9,1... | collective-permute-start | bytes 147464 | tf_op jit(solution)/shard_map/ppermute | solution.py:514
  26.5 1.2 %shard_map.92 = (f32[256,512]{1,0:T(8,128)S(1)}, bf16[512,512]{1,0:T(8,128)(2,1)S(1)}, bf16[96,512]{1,0:T(8,128)(2,1)S(1)}, bf16[512,256]{1,0:T(8,128)(2,1)S(1)}...) custom-call(f32[264,256]{1,0:T(8,128)S(1)} %pad_add_fusion.mine.packed, ...), custom_call_target="tpu_custom_call" | custom-call | flops 1048576 | bytes 2236416 | tf_op jit(solution)/shard_map/pallas_call | solution.py:489
  27.7 1.2 %collective-permute-done.1.first = f32[48,256]{1,0:T(8,128)S(1)} collective-permute-done((f32[48,256]{1,0:T(8,128)S(1)}, f32[48,256]{1,0:T(8,128)S(1)}, u32[]{:S(2)}, u32[]{:S(2)}) %collective-permute-start.1) | collective-permute-done | bytes 49184 | tf_op jit(solution)/shard_map/ppermute | solution.py:514
  28.9 1.1 %collective-permute-done.2.second = f32[48,256]{1,0:T(8,128)S(1)} collective-permute-done((f32[48,256]{1,0:T(8,128)S(1)}, f32[48,256]{1,0:T(8,128)S(1)}, u32[]{:S(2)}, u32[]{:S(2)}) %collective-permute-start.2) | collective-permute-done | bytes 49184 | tf_op jit(solution)/shard_map/ppermute | solution.py:514
  30.6 4.7 %collective-permute-start.7 = (f32[48,384]{1,0:T(8,128)S(1)}, f32[48,384]{1,0:T(8,128)S(1)}, u32[]{:S(2)}, u32[]{:S(2)}) collective-permute-start(f32[48,384]{1,0:T(8,128)S(1)} %get-tuple-element.58), channel_id=1, source_target_pairs={{130,132},{132,130},{131,133},{133,131},{134,136},{136,134},{135,1... | collective-permute-start | bytes 221192 | tf_op jit(solution)/shard_map/ppermute | solution.py:514
  35.3 2.1 %collective-permute-start.8 = (f32[48,384]{1,0:T(8,128)S(1)}, f32[48,384]{1,0:T(8,128)S(1)}, u32[]{:S(2)}, u32[]{:S(2)}) collective-permute-start(f32[48,384]{1,0:T(8,128)S(1)} %get-tuple-element.59), channel_id=1, source_target_pairs={{128,130},{130,128},{129,131},{131,129},{132,134},{134,132},{133,1... | collective-permute-start | bytes 221192 | tf_op jit(solution)/shard_map/ppermute | solution.py:514
  37.4 1.4 %shard_map.96 = (bf16[12,256,256]{2,1,0:T(8,128)(2,1)S(1)}, bf16[256,512]{1,0:T(8,128)(2,1)S(1)}, bf16[256,256]{1,0:T(8,128)(2,1)S(1)}, f32[8,256]{1,0:T(8,128)S(1)}, bf16[256,256]{1,0:T(8,128)(2,1)S(1)}) custom-call(f32[264,256]{1,0:T(8,128)S(1)} %pad_add_fusion.mine.packed, f32[264,256]{1,0:T(8,128)S(1)} %collective-permute-done.other, ...), custom_call_target="tpu_custom_call" | custom-call | flops 1048576 | bytes 2908160 | tf_op jit(solution)/shard_map/pallas_call | solution.py:489
  38.8 2.1 %shard_map.97 = (f32[256,512]{1,0:T(8,128)S(1)}, f32[256,512]{1,0:T(8,128)S(1)}, f32[192,512]{1,0:T(8,128)S(1)}, f32[48,256]{1,0:T(8,128)S(1)}) custom-call(f32[48,256]{1,0:T(8,128)S(1)} %collective-permute-done.1.first, f32[48,256]{1,0:T(8,128)S(1)} %collective-permute-done.2.second, f32[256,512]{1,0:T(8,128)S(1)} %get-tuple-element.65.kept, ...), custom_call_target="tpu_custom_call" | custom-call | flops 1048576 | bytes 5808128 | tf_op jit(solution)/shard_map/pallas_call | solution.py:489
  41.5 0.8 shard_map.98
  42.3 4.5 %collective-permute-start.9 = (f32[48,128]{1,0:T(8,128)S(1)}, f32[48,128]{1,0:T(8,128)S(1)}, u32[]{:S(2)}, u32[]{:S(2)}) collective-permute-start(f32[48,128]{1,0:T(8,128)S(1)} %get-tuple-element.70.sent_first), channel_id=1, source_target_pairs={{130,132},{132,130},{131,133},{133,131},{134,136},{136,134},{135,1... | collective-permute-start | bytes 73736 | tf_op jit(solution)/shard_map/ppermute | solution.py:514
  46.8 1.9 %collective-permute-start.10 = (f32[48,128]{1,0:T(8,128)S(1)}, f32[48,128]{1,0:T(8,128)S(1)}, u32[]{:S(2)}, u32[]{:S(2)}) collective-permute-start(f32[48,128]{1,0:T(8,128)S(1)} %get-tuple-element.71.sent_second), channel_id=1, source_target_pairs={{128,130},{130,128},{129,131},{131,129},{132,134},{134,132},{133,1... | collective-permute-start | bytes 73736 | tf_op jit(solution)/shard_map/ppermute | solution.py:514
  48.7 2.3 %shard_map.99 = (f32[256,512]{1,0:T(8,128)S(1)}, f32[256,512]{1,0:T(8,128)S(1)}, f32[48,256]{1,0:T(8,128)S(1)}, f32[192,512]{1,0:T(8,128)S(1)}) custom-call(f32[256,512]{1,0:T(8,128)S(1)} %get-tuple-element.72.state, f32[256,512]{1,0:T(8,128)S(1)} %get-tuple-element.73.carry, f32[192,512]{1,0:T(8,128)S(1)} %get-tuple-element.74.force, ...), custom_call_target="tpu_custom_call" | custom-call | flops 1048576 | bytes 6414336 | tf_op jit(solution)/shard_map/pallas_call | solution.py:489
  51.4 1.2 %collective-permute-done.10.second = f32[48,128]{1,0:T(8,128)S(1)} collective-permute-done((f32[48,128]{1,0:T(8,128)S(1)}, f32[48,128]{1,0:T(8,128)S(1)}, u32[]{:S(2)}, u32[]{:S(2)}) %collective-permute-start.10) | collective-permute-done | bytes 24608 | tf_op jit(solution)/shard_map/ppermute | solution.py:514
  53.1 4.7 %collective-permute-start.11 = (f32[48,128]{1,0:T(8,128)S(1)}, f32[48,128]{1,0:T(8,128)S(1)}, u32[]{:S(2)}, u32[]{:S(2)}) collective-permute-start(f32[48,128]{1,0:T(8,128)S(1)} %get-tuple-element.78.sent_first), channel_id=1, source_target_pairs={{130,132},{132,130},{131,133},{133,131},{134,136},{136,134},{135,1... | collective-permute-start | bytes 73736 | tf_op jit(solution)/shard_map/ppermute | solution.py:514
  57.8 1.9 %collective-permute-start.12 = (f32[48,128]{1,0:T(8,128)S(1)}, f32[48,128]{1,0:T(8,128)S(1)}, u32[]{:S(2)}, u32[]{:S(2)}) collective-permute-start(f32[48,128]{1,0:T(8,128)S(1)} %get-tuple-element.79.sent_second), channel_id=1, source_target_pairs={{128,130},{130,128},{129,131},{131,129},{132,134},{134,132},{133,1... | collective-permute-start | bytes 73736 | tf_op jit(solution)/shard_map/ppermute | solution.py:514
  59.7 2.1 %shard_map.101 = (f32[256,512]{1,0:T(8,128)S(1)}, f32[256,512]{1,0:T(8,128)S(1)}, f32[48,256]{1,0:T(8,128)S(1)}) custom-call(f32[256,512]{1,0:T(8,128)S(1)} %get-tuple-element.80.state, f32[256,512]{1,0:T(8,128)S(1)} %get-tuple-element.81.carry, f32[192,512]{1,0:T(8,128)S(1)} %get-tuple-element.82.force, bf16[576,256]{1,0:T(8,128)(2,1)S(1)} %get-tuple-element.83.stacks, ...), custom_call_target="tpu_custom_call" | custom-call | flops 1048576 | bytes 5775360 | tf_op jit(solution)/shard_map/pallas_call | solution.py:489
  62.1 1.4 %collective-permute-done.12.second = f32[48,128]{1,0:T(8,128)S(1)} collective-permute-done((f32[48,128]{1,0:T(8,128)S(1)}, f32[48,128]{1,0:T(8,128)S(1)}, u32[]{:S(2)}, u32[]{:S(2)}) %collective-permute-start.12) | collective-permute-done | bytes 24608 | tf_op jit(solution)/shard_map/ppermute | solution.py:514
  64.1 4.5 %collective-permute-start.13 = (f32[48,128]{1,0:T(8,128)S(1)}, f32[48,128]{1,0:T(8,128)S(1)}, u32[]{:S(2)}, u32[]{:S(2)}) collective-permute-start(f32[48,128]{1,0:T(8,128)S(1)} %get-tuple-element.85.sent_first), channel_id=1, source_target_pairs={{130,132},{132,130},{131,133},{133,131},{134,136},{136,134},{135,1... | collective-permute-start | bytes 73736 | tf_op jit(solution)/shard_map/ppermute | solution.py:514
  68.6 2.1 %collective-permute-start.14 = (f32[48,128]{1,0:T(8,128)S(1)}, f32[48,128]{1,0:T(8,128)S(1)}, u32[]{:S(2)}, u32[]{:S(2)}) collective-permute-start(f32[48,128]{1,0:T(8,128)S(1)} %get-tuple-element.86.sent_second), channel_id=1, source_target_pairs={{128,130},{130,128},{129,131},{131,129},{132,134},{134,132},{133,1... | collective-permute-start | bytes 73736 | tf_op jit(solution)/shard_map/ppermute | solution.py:514
  70.7 2.1 %shard_map.103 = (f32[256,512]{1,0:T(8,128)S(1)}, f32[256,512]{1,0:T(8,128)S(1)}, f32[48,256]{1,0:T(8,128)S(1)}) custom-call(f32[256,512]{1,0:T(8,128)S(1)} %get-tuple-element.87.state, f32[256,512]{1,0:T(8,128)S(1)} %get-tuple-element.88.carry, f32[192,512]{1,0:T(8,128)S(1)} %get-tuple-element.82.force, bf16[576,256]{1,0:T(8,128)(2,1)S(1)} %get-tuple-element.89.stacks, ...), custom_call_target="tpu_custom_call" | custom-call | flops 1048576 | bytes 5775360 | tf_op jit(solution)/shard_map/pallas_call | solution.py:489
  73.1 1.2 %collective-permute-done.14.second = f32[48,128]{1,0:T(8,128)S(1)} collective-permute-done((f32[48,128]{1,0:T(8,128)S(1)}, f32[48,128]{1,0:T(8,128)S(1)}, u32[]{:S(2)}, u32[]{:S(2)}) %collective-permute-start.14) | collective-permute-done | bytes 24608 | tf_op jit(solution)/shard_map/ppermute | solution.py:514
  74.9 4.7 %collective-permute-start.15 = (f32[48,128]{1,0:T(8,128)S(1)}, f32[48,128]{1,0:T(8,128)S(1)}, u32[]{:S(2)}, u32[]{:S(2)}) collective-permute-start(f32[48,128]{1,0:T(8,128)S(1)} %get-tuple-element.91.sent_first), channel_id=1, source_target_pairs={{130,132},{132,130},{131,133},{133,131},{134,136},{136,134},{135,1... | collective-permute-start | bytes 73736 | tf_op jit(solution)/shard_map/ppermute | solution.py:514
  79.6 1.9 %collective-permute-start.16 = (f32[48,128]{1,0:T(8,128)S(1)}, f32[48,128]{1,0:T(8,128)S(1)}, u32[]{:S(2)}, u32[]{:S(2)}) collective-permute-start(f32[48,128]{1,0:T(8,128)S(1)} %get-tuple-element.92.sent_second), channel_id=1, source_target_pairs={{128,130},{130,128},{129,131},{131,129},{132,134},{134,132},{133,1... | collective-permute-start | bytes 73736 | tf_op jit(solution)/shard_map/ppermute | solution.py:514
  81.5 1.7 %shard_map.105.ahead = f32[256,256]{1,0:T(8,128)S(1)} custom-call(f32[256,512]{1,0:T(8,128)S(1)} %get-tuple-element.94.state, f32[256,512]{1,0:T(8,128)S(1)} %get-tuple-element.95.carry, f32[192,512]{1,0:T(8,128)S(1)} %get-tuple-element.82.force, bf16[576,256]{1,0:T(8,128)(2,1)S(1)} %get-tuple-element.96.stacks, ...), custom_call_target="tpu_custom_call" | custom-call | flops 1048576 | bytes 4669440 | tf_op jit(solution)/shard_map/pallas_call | solution.py:489
  83.9 1.4 %collective-permute-done.16.second = f32[48,128]{1,0:T(8,128)S(1)} collective-permute-done((f32[48,128]{1,0:T(8,128)S(1)}, f32[48,128]{1,0:T(8,128)S(1)}, u32[]{:S(2)}, u32[]{:S(2)}) %collective-permute-start.16) | collective-permute-done | bytes 24608 | tf_op jit(solution)/shard_map/ppermute | solution.py:514
  85.3 1.2 %shard_map.106 = f32[256,256]{1,0:T(8,128)} custom-call(f32[48,128]{1,0:T(8,128)S(1)} %collective-permute-done.15.first, f32[48,128]{1,0:T(8,128)S(1)} %collective-permute-done.16.second, f32[48,128]{1,0:T(8,128)S(1)} %get-tuple-element.91.sent_first, f32[48,128]{1,0:T(8,128)S(1)} %get-tuple-element.92.sent_second, f32[8,256]{1,0:T(8,128)S(1)} %get-tuple-element.63.kinds, ...), custom_call_target="tpu_custom_call" | custom-call | flops 1048576 | bytes 1056768 | tf_op jit(solution)/shard_map/pallas_call | solution.py:489
  (27 shorter events, 6.9 us)
Async XLA Ops:
  0.0 26.5 %copy-start.2 = (bf16[288,256]{1,0:T(8,128)(2,1)S(1)}, bf16[288,256]{1,0:T(8,128)(2,1)}, u32[]{:S(2)}) copy-start(bf16[288,256]{1,0:T(8,128)(2,1)} %constant.13.clone.trace) | copy-start | bytes 442372
  1.4 4.6 %collective-permute-start.5 = (f32[192,256]{1,0:T(8,128)S(1)}, f32[192,256]{1,0:T(8,128)S(1)}, u32[]{:S(2)}, u32[]{:S(2)}) collective-permute-start(f32[192,256]{1,0:T(8,128)S(1)} %shard_map.93), channel_id=1, source_target_pairs={{0,384},{1,385},{2,386},{3,387},{4,388},{5,389},{6,390},{7,391},{8... | collective-permute-start | bytes 589832 | tf_op jit(solution)/shard_map/ppermute | solution.py:547
  2.1 3.9 %collective-permute-start.4 = (f32[192,256]{1,0:T(8,128)S(1)}, f32[192,256]{1,0:T(8,128)S(1)}, u32[]{:S(2)}, u32[]{:S(2)}) collective-permute-start(f32[192,256]{1,0:T(8,128)S(1)} %shard_map.93), channel_id=1, source_target_pairs={{0,256},{1,257},{2,258},{3,259},{4,260},{5,261},{6,262},{7,263},{8... | collective-permute-start | bytes 589832 | tf_op jit(solution)/shard_map/ppermute | solution.py:547
  2.7 14.0 %collective-permute-start.3 = (f32[192,256]{1,0:T(8,128)S(1)}, f32[192,256]{1,0:T(8,128)S(1)}, u32[]{:S(2)}, u32[]{:S(2)}) collective-permute-start(f32[192,256]{1,0:T(8,128)S(1)} %shard_map.93), channel_id=1, source_target_pairs={{0,128},{1,129},{2,130},{3,131},{4,132},{5,133},{6,134},{7,135},{8... | collective-permute-start | bytes 589832 | tf_op jit(solution)/shard_map/ppermute | solution.py:547
  4.0 15.0 %collective-permute-start = (f32[264,256]{1,0:T(8,128)S(1)}, f32[264,256]{1,0:T(8,128)S(1)}, u32[]{:S(2)}, u32[]{:S(2)}) collective-permute-start(f32[264,256]{1,0:T(8,128)S(1)} %pad_add_fusion.mine.packed), channel_id=1, source_target_pairs={{0,1},{1,0},{2,3},{3,2},{4,5},{5,4},{6,7},{7,6},{8,9},{9,8},{10,11... | collective-permute-start | bytes 811016 | tf_op jit(solution)/shard_map/ppermute | solution.py:519
  16.9 21.9 %copy-start = (bf16[256,576]{1,0:T(8,128)(2,1)S(1)}, bf16[256,576]{1,0:T(8,128)(2,1)}, u32[]{:S(2)}) copy-start(bf16[256,576]{1,0:T(8,128)(2,1)} %constant.14.clone.lift_two) | copy-start | bytes 884740
  16.9 21.9 %copy-start.1 = (bf16[256,768]{1,0:T(8,128)(2,1)S(1)}, bf16[256,768]{1,0:T(8,128)(2,1)}, u32[]{:S(2)}) copy-start(bf16[256,768]{1,0:T(8,128)(2,1)} %constant.12.clone.interior) | copy-start | bytes 1179652
  17.0 13.0 %collective-permute-start.6 = (f32[192,256]{1,0:T(8,128)S(1)}, f32[192,256]{1,0:T(8,128)S(1)}, u32[]{:S(2)}, u32[]{:S(2)}) collective-permute-start(f32[192,256]{1,0:T(8,128)S(1)} %shard_map.94.force_mine), channel_id=1, source_target_pairs={{0,1},{1,0},{2,3},{3,2},{4,5},{5,4},{6,7},{7,6},{8,9},{9,8},{10,11... | collective-permute-start | bytes 589832 | tf_op jit(solution)/shard_map/ppermute | solution.py:519
  19.5 9.4 %collective-permute-start.1 = (f32[48,256]{1,0:T(8,128)S(1)}, f32[48,256]{1,0:T(8,128)S(1)}, u32[]{:S(2)}, u32[]{:S(2)}) collective-permute-start(f32[48,256]{1,0:T(8,128)S(1)} %get-tuple-element.51), channel_id=1, source_target_pairs={{2,4},{4,2},{3,5},{5,3},{6,8},{8,6},{7,9},{9,7},{10,12},{12,10},{1... | collective-permute-start | bytes 147464 | tf_op jit(solution)/shard_map/ppermute | solution.py:514
  24.0 6.0 %collective-permute-start.2 = (f32[48,256]{1,0:T(8,128)S(1)}, f32[48,256]{1,0:T(8,128)S(1)}, u32[]{:S(2)}, u32[]{:S(2)}) collective-permute-start(f32[48,256]{1,0:T(8,128)S(1)} %get-tuple-element.52), channel_id=1, source_target_pairs={{0,2},{2,0},{1,3},{3,1},{4,6},{6,4},{5,7},{7,5},{8,10},{10,8},{9,1... | collective-permute-start | bytes 147464 | tf_op jit(solution)/shard_map/ppermute | solution.py:514
  30.6 10.4 %collective-permute-start.7 = (f32[48,384]{1,0:T(8,128)S(1)}, f32[48,384]{1,0:T(8,128)S(1)}, u32[]{:S(2)}, u32[]{:S(2)}) collective-permute-start(f32[48,384]{1,0:T(8,128)S(1)} %get-tuple-element.58), channel_id=1, source_target_pairs={{130,132},{132,130},{131,133},{133,131},{134,136},{136,134},{135,1... | collective-permute-start | bytes 221192 | tf_op jit(solution)/shard_map/ppermute | solution.py:514
  35.3 6.2 %collective-permute-start.8 = (f32[48,384]{1,0:T(8,128)S(1)}, f32[48,384]{1,0:T(8,128)S(1)}, u32[]{:S(2)}, u32[]{:S(2)}) collective-permute-start(f32[48,384]{1,0:T(8,128)S(1)} %get-tuple-element.59), channel_id=1, source_target_pairs={{128,130},{130,128},{129,131},{131,129},{132,134},{134,132},{133,1... | collective-permute-start | bytes 221192 | tf_op jit(solution)/shard_map/ppermute | solution.py:514
  38.8 2.7 %copy-start.3 = (bf16[288,576]{1,0:T(8,128)(2,1)S(1)}, bf16[288,576]{1,0:T(8,128)(2,1)}, u32[]{:S(2)}) copy-start(bf16[288,576]{1,0:T(8,128)(2,1)} %constant.15.clone.reach) | copy-start | bytes 995332
  42.3 9.0 %collective-permute-start.9 = (f32[48,128]{1,0:T(8,128)S(1)}, f32[48,128]{1,0:T(8,128)S(1)}, u32[]{:S(2)}, u32[]{:S(2)}) collective-permute-start(f32[48,128]{1,0:T(8,128)S(1)} %get-tuple-element.70.sent_first), channel_id=1, source_target_pairs={{130,132},{132,130},{131,133},{133,131},{134,136},{136,134},{135,1... | collective-permute-start | bytes 73736 | tf_op jit(solution)/shard_map/ppermute | solution.py:514
  46.8 5.7 %collective-permute-start.10 = (f32[48,128]{1,0:T(8,128)S(1)}, f32[48,128]{1,0:T(8,128)S(1)}, u32[]{:S(2)}, u32[]{:S(2)}) collective-permute-start(f32[48,128]{1,0:T(8,128)S(1)} %get-tuple-element.71.sent_second), channel_id=1, source_target_pairs={{128,130},{130,128},{129,131},{131,129},{132,134},{134,132},{133,1... | collective-permute-start | bytes 73736 | tf_op jit(solution)/shard_map/ppermute | solution.py:514
  53.1 9.0 %collective-permute-start.11 = (f32[48,128]{1,0:T(8,128)S(1)}, f32[48,128]{1,0:T(8,128)S(1)}, u32[]{:S(2)}, u32[]{:S(2)}) collective-permute-start(f32[48,128]{1,0:T(8,128)S(1)} %get-tuple-element.78.sent_first), channel_id=1, source_target_pairs={{130,132},{132,130},{131,133},{133,131},{134,136},{136,134},{135,1... | collective-permute-start | bytes 73736 | tf_op jit(solution)/shard_map/ppermute | solution.py:514
  57.8 5.7 %collective-permute-start.12 = (f32[48,128]{1,0:T(8,128)S(1)}, f32[48,128]{1,0:T(8,128)S(1)}, u32[]{:S(2)}, u32[]{:S(2)}) collective-permute-start(f32[48,128]{1,0:T(8,128)S(1)} %get-tuple-element.79.sent_second), channel_id=1, source_target_pairs={{128,130},{130,128},{129,131},{131,129},{132,134},{134,132},{133,1... | collective-permute-start | bytes 73736 | tf_op jit(solution)/shard_map/ppermute | solution.py:514
  64.1 9.0 %collective-permute-start.13 = (f32[48,128]{1,0:T(8,128)S(1)}, f32[48,128]{1,0:T(8,128)S(1)}, u32[]{:S(2)}, u32[]{:S(2)}) collective-permute-start(f32[48,128]{1,0:T(8,128)S(1)} %get-tuple-element.85.sent_first), channel_id=1, source_target_pairs={{130,132},{132,130},{131,133},{133,131},{134,136},{136,134},{135,1... | collective-permute-start | bytes 73736 | tf_op jit(solution)/shard_map/ppermute | solution.py:514
  68.6 5.7 %collective-permute-start.14 = (f32[48,128]{1,0:T(8,128)S(1)}, f32[48,128]{1,0:T(8,128)S(1)}, u32[]{:S(2)}, u32[]{:S(2)}) collective-permute-start(f32[48,128]{1,0:T(8,128)S(1)} %get-tuple-element.86.sent_second), channel_id=1, source_target_pairs={{128,130},{130,128},{129,131},{131,129},{132,134},{134,132},{133,1... | collective-permute-start | bytes 73736 | tf_op jit(solution)/shard_map/ppermute | solution.py:514
  74.9 9.0 %collective-permute-start.15 = (f32[48,128]{1,0:T(8,128)S(1)}, f32[48,128]{1,0:T(8,128)S(1)}, u32[]{:S(2)}, u32[]{:S(2)}) collective-permute-start(f32[48,128]{1,0:T(8,128)S(1)} %get-tuple-element.91.sent_first), channel_id=1, source_target_pairs={{130,132},{132,130},{131,133},{133,131},{134,136},{136,134},{135,1... | collective-permute-start | bytes 73736 | tf_op jit(solution)/shard_map/ppermute | solution.py:514
  79.6 5.7 %collective-permute-start.16 = (f32[48,128]{1,0:T(8,128)S(1)}, f32[48,128]{1,0:T(8,128)S(1)}, u32[]{:S(2)}, u32[]{:S(2)}) collective-permute-start(f32[48,128]{1,0:T(8,128)S(1)} %get-tuple-element.92.sent_second), channel_id=1, source_target_pairs={{128,130},{130,128},{129,131},{131,129},{132,134},{134,132},{133,1... | collective-permute-start | bytes 73736 | tf_op jit(solution)/shard_map/ppermute | solution.py:514

commit v3 on v2

--- a/solution.py
+++ b/solution.py
@@ -241,8 +241,8 @@
     return total
 
 
-def depart_kernel(mine, other, first_out, second_out, select_out, ranks_out):
-    low, high = chip_halves(mine[...], other[...])
+def depart_kernel(mine, other, other_flow, first_out, second_out, select_out, ranks_out):
+    low, high = chip_halves(mine[...], other[...] + other_flow[...])
     first = (lax.axis_index("dom") & -2).astype(F32)
     spread = one_hot((lane_iota((64, 256)) >> 2) == row_iota((64, 256)))
     before = one_hot(row_iota((256, 256)) < lane_iota((256, 256)))
@@ -270,10 +270,10 @@
 
 
 def places_kernel(
-    mine, other, ranks, trace,
+    mine, other, other_flow, ranks, trace,
     kept_out, keep_out, arrive_out, pick_out, send_kinds_out, arrive_pick_out, base_out,
 ):
-    low, high = chip_halves(mine[...], other[...])
+    low, high = chip_halves(mine[...], other[...] + other_flow[...])
     members, rank = ranks[0:16], ranks[16:32]
     count = jnp.sum(members, axis=1, keepdims=True)
     low_place = target_of(members, rank, 0, ((0, 0.0), (1, 256.0 + start_of(count, 1, -1))))
@@ -315,12 +315,12 @@
     base_out[...] = picked_traces(kept, pick, send_kinds, trace[...])
 
 
-def faces_kernel(mine, other, pick, local_out, place_out, own_place_out, kinds_out, meet_out):
+def faces_kernel(mine, other, other_flow, pick, local_out, place_out, own_place_out, kinds_out, meet_out):
     row = row_iota((256, 256))
     ones = jnp.ones((8, 256), BF)
     kinds = [jnp.zeros((1, 256), F32)] * 6
     places = []
-    for device, half in enumerate(chip_halves(mine[256:264], other[256:264])):
+    for device, half in enumerate(chip_halves(mine[256:264], other[256:264] + other_flow[256:264])):
         place = jnp.zeros((256, 256), F32)
         for face in range(6):
             where = half[face : face + 1].astype(jnp.int32)
@@ -515,8 +515,10 @@
     return came
 
 
-def swap(value):
-    return lax.ppermute(value, "dom", [(at, at ^ 1) for at in range(lax.axis_size("dom"))])
+def swap(value, sections):
+    count = lax.axis_size("dom")
+    pairs = [(section * count + at, section * count + (at ^ 1)) for section in sections for at in range(count)]
+    return lax.ppermute(value, ("sec", "dom"), pairs)
 
 
 def step(fields, source_map, new_owner, send_list, face_slot):
@@ -545,16 +547,17 @@
     lamb_parts = []
     for section in (1, 2, 3):
         lamb_parts.append(lax.ppermute(lamb, "sec", [(0, section)]))
-    other = swap(packed)
+    other = swap(packed, acoustic)
+    other_flow = swap(packed, every[:1])
+    mates = (packed, other, other_flow)
     *leaving, select, ranks = call(
         depart_kernel,
         [arr(48, 256), arr(48, 256), arr(96, 512, dtype=BF), arr(32, 256)],
-        packed,
-        other,
+        *mates,
     )
     moved = trade(*leaving, every)
     (force_mine,) = call(force_kernel, [arr(192, 256)], *lamb_parts, packed)
-    force_other = swap(force_mine)
+    force_other = swap(force_mine, acoustic)
     kept, keep, arrive, pick, send_kinds, arrive_pick, base = call(
         places_kernel,
         [
@@ -566,8 +569,7 @@
             arr(96, 256, dtype=BF),
             arr(TRACE_ROWS, 256),
         ],
-        packed,
-        other,
+        *mates,
         ranks,
         trace,
     )
@@ -587,8 +589,7 @@
             arr(8, 256),
             arr(256, 256, dtype=BF),
         ],
-        packed,
-        other,
+        *mates,
         pick,
     )
     state, carry, force, base = call(

time: 87.2 us -> 87.2 us (level)
    ppermute x2 -> x3, starting transfers between devices: 3.97 us -> 4.52 us  [swap(): return lax.ppermute(value, ('sec', 'dom'), pairs)]
  transfers between devices with their start and end apart: 17 -> 18, of which waited for: 12 -> 12; matrix products, arithmetic and copies ran while one was open for 0% -> 0% of each run, Pallas kernels for 16% -> 16%
where the time goes in v3:
time: 87.2 us; the launch traced here: 86.7 us
  starting transfers between devices  47.3 us (54%)
  waiting for transfers between devices  19.6 us (22%)
  Pallas kernels  18.3 us (21%)
  other arithmetic  1.04 us (1%)
    ppermute x12, starting transfers between devices, trade(): came.append(lax.ppermute(value, ('sec', 'dom'), pairs))  40.1 us
    pallas_call x16, Pallas kernels, call(): pl.pallas_call(kernel, out_shape=list(outs), in_specs=[vmem] * len(args),...  18.3 us
    ppermute x3, waiting for transfers between devices, step(): lamb_parts.append(lax.ppermute(lamb, 'sec', [(0, section)]))  10 us
    ppermute x12, waiting for transfers between devices, trade(): came.append(lax.ppermute(value, ('sec', 'dom'), pairs))  9.53 us
    ppermute x3, starting transfers between devices, swap(): return lax.ppermute(value, ('sec', 'dom'), pairs)  4.52 us
    ppermute x3, starting transfers between devices, step(): lamb_parts.append(lax.ppermute(lamb, 'sec', [(0, section)]))  2.64 us
  transfers between devices with their start and end apart: 18, of which 12 were waited for; matrix products, arithmetic and copies ran while one was open for 0% of the time, Pallas kernels for 16%

profile of v3, /device:TPU:258, one launch (start us, length us, event | category | flops | bytes accessed | tf_op | source)
XLA Modules:
  0.0 86.7 jit_solution(6641279809432882426)
XLA Ops:
  0.0 1.0 %pad_add_fusion.mine.packed = f32[264,256]{1,0:T(8,128)S(1)} fusion(f32[256,256]{1,0:T(8,128)} %bitcast.5, s32[1,96]{1,0:T(1,128)} %bitcast.7, s32[1,64]{1,0:T(1,128)} %bitcast.8, s32[1,256]{1,0:T(1,128)} %bitcast.6, s32[6,256]{1,0:T(8,128)} %param.13), kind=kLoop, calls=%fused_computation | loop fusion | flops 337920 | bytes 540288 | tf_op jit(solution)/shard_map/add | solution.py:545
  2.7 1.3 %collective-permute-start.4 = (f32[192,256]{1,0:T(8,128)S(1)}, f32[192,256]{1,0:T(8,128)S(1)}, u32[]{:S(2)}, u32[]{:S(2)}) collective-permute-start(f32[192,256]{1,0:T(8,128)S(1)} %shard_map.93), channel_id=1, source_target_pairs={{0,128},{1,129},{2,130},{3,131},{4,132},{5,133},{6,134},{7,135},{8... | collective-permute-start | bytes 589832 | tf_op jit(solution)/shard_map/ppermute | solution.py:549
  4.7 1.9 %collective-permute-start = (f32[264,256]{1,0:T(8,128)S(1)}, f32[264,256]{1,0:T(8,128)S(1)}, u32[]{:S(2)}, u32[]{:S(2)}) collective-permute-start(f32[264,256]{1,0:T(8,128)S(1)} %pad_add_fusion.mine.packed), channel_id=1, source_target_pairs={{128,129},{129,128},{130,131},{131,130},{132,133},{133,132},{134,1... | collective-permute-start | bytes 811016 | tf_op jit(solution)/shard_map/ppermute | solution.py:521
  6.7 10.0 %collective-permute-done.4.first = f32[192,256]{1,0:T(8,128)S(1)} collective-permute-done((f32[192,256]{1,0:T(8,128)S(1)}, f32[192,256]{1,0:T(8,128)S(1)}, u32[]{:S(2)}, u32[]{:S(2)}) %collective-permute-start.4) | collective-permute-done | bytes 196640 | tf_op jit(solution)/shard_map/ppermute | solution.py:549
  16.9 1.9 %collective-permute-start.7 = (f32[192,256]{1,0:T(8,128)S(1)}, f32[192,256]{1,0:T(8,128)S(1)}, u32[]{:S(2)}, u32[]{:S(2)}) collective-permute-start(f32[192,256]{1,0:T(8,128)S(1)} %shard_map.94.force_mine), channel_id=1, source_target_pairs={{128,129},{129,128},{130,131},{131,130},{132,133},{133,132},{134,1... | collective-permute-start | bytes 589832 | tf_op jit(solution)/shard_map/ppermute | solution.py:521
  19.4 4.6 %collective-permute-start.2 = (f32[48,256]{1,0:T(8,128)S(1)}, f32[48,256]{1,0:T(8,128)S(1)}, u32[]{:S(2)}, u32[]{:S(2)}) collective-permute-start(f32[48,256]{1,0:T(8,128)S(1)} %get-tuple-element.51), channel_id=1, source_target_pairs={{2,4},{4,2},{3,5},{5,3},{6,8},{8,6},{7,9},{9,7},{10,12},{12,10},{1... | collective-permute-start | bytes 147464 | tf_op jit(solution)/shard_map/ppermute | solution.py:514
  24.0 2.5 %collective-permute-start.3 = (f32[48,256]{1,0:T(8,128)S(1)}, f32[48,256]{1,0:T(8,128)S(1)}, u32[]{:S(2)}, u32[]{:S(2)}) collective-permute-start(f32[48,256]{1,0:T(8,128)S(1)} %get-tuple-element.52), channel_id=1, source_target_pairs={{0,2},{2,0},{1,3},{3,1},{4,6},{6,4},{5,7},{7,5},{8,10},{10,8},{9,1... | collective-permute-start | bytes 147464 | tf_op jit(solution)/shard_map/ppermute | solution.py:514
  26.5 1.2 %shard_map.92 = (f32[256,512]{1,0:T(8,128)S(1)}, bf16[512,512]{1,0:T(8,128)(2,1)S(1)}, bf16[96,512]{1,0:T(8,128)(2,1)S(1)}, bf16[512,256]{1,0:T(8,128)(2,1)S(1)}...) custom-call(f32[264,256]{1,0:T(8,128)S(1)} %pad_add_fusion.mine.packed, ...), custom_call_target="tpu_custom_call" | custom-call | flops 1048576 | bytes 2506752 | tf_op jit(solution)/shard_map/pallas_call | solution.py:489
  27.8 1.1 %collective-permute-done.2.first = f32[48,256]{1,0:T(8,128)S(1)} collective-permute-done((f32[48,256]{1,0:T(8,128)S(1)}, f32[48,256]{1,0:T(8,128)S(1)}, u32[]{:S(2)}, u32[]{:S(2)}) %collective-permute-start.2) | collective-permute-done | bytes 49184 | tf_op jit(solution)/shard_map/ppermute | solution.py:514
  28.9 1.1 %collective-permute-done.3.second = f32[48,256]{1,0:T(8,128)S(1)} collective-permute-done((f32[48,256]{1,0:T(8,128)S(1)}, f32[48,256]{1,0:T(8,128)S(1)}, u32[]{:S(2)}, u32[]{:S(2)}) %collective-permute-start.3) | collective-permute-done | bytes 49184 | tf_op jit(solution)/shard_map/ppermute | solution.py:514
  30.6 4.7 %collective-permute-start.8 = (f32[48,384]{1,0:T(8,128)S(1)}, f32[48,384]{1,0:T(8,128)S(1)}, u32[]{:S(2)}, u32[]{:S(2)}) collective-permute-start(f32[48,384]{1,0:T(8,128)S(1)} %get-tuple-element.58), channel_id=1, source_target_pairs={{130,132},{132,130},{131,133},{133,131},{134,136},{136,134},{135,1... | collective-permute-start | bytes 221192 | tf_op jit(solution)/shard_map/ppermute | solution.py:514
  35.3 2.1 %collective-permute-start.9 = (f32[48,384]{1,0:T(8,128)S(1)}, f32[48,384]{1,0:T(8,128)S(1)}, u32[]{:S(2)}, u32[]{:S(2)}) collective-permute-start(f32[48,384]{1,0:T(8,128)S(1)} %get-tuple-element.59), channel_id=1, source_target_pairs={{128,130},{130,128},{129,131},{131,129},{132,134},{134,132},{133,1... | collective-permute-start | bytes 221192 | tf_op jit(solution)/shard_map/ppermute | solution.py:514
  37.4 1.4 %shard_map.96 = (bf16[12,256,256]{2,1,0:T(8,128)(2,1)S(1)}, bf16[256,512]{1,0:T(8,128)(2,1)S(1)}, bf16[256,256]{1,0:T(8,128)(2,1)S(1)}, f32[8,256]{1,0:T(8,128)S(1)}, bf16[256,256]{1,0:T(8,128)(2,1)S(1)}) custom-call(f32[264,256]{1,0:T(8,128)S(1)} %pad_add_fusion.mine.packed, f32[264,256]{1,0:T(8,128)S(1)} %collective-permute-done.other, ...), custom_call_target="tpu_custom_call" | custom-call | flops 1048576 | bytes 3178496 | tf_op jit(solution)/shard_map/pallas_call | solution.py:489
  38.8 2.1 %shard_map.97 = (f32[256,512]{1,0:T(8,128)S(1)}, f32[256,512]{1,0:T(8,128)S(1)}, f32[192,512]{1,0:T(8,128)S(1)}, f32[48,256]{1,0:T(8,128)S(1)}) custom-call(f32[48,256]{1,0:T(8,128)S(1)} %collective-permute-done.2.first, f32[48,256]{1,0:T(8,128)S(1)} %collective-permute-done.3.second, f32[256,512]{1,0:T(8,128)S(1)} %get-tuple-element.65.kept, ...), custom_call_target="tpu_custom_call" | custom-call | flops 1048576 | bytes 5808128 | tf_op jit(solution)/shard_map/pallas_call | solution.py:489
  41.5 0.8 shard_map.98
  42.4 4.5 %collective-permute-start.10 = (f32[48,128]{1,0:T(8,128)S(1)}, f32[48,128]{1,0:T(8,128)S(1)}, u32[]{:S(2)}, u32[]{:S(2)}) collective-permute-start(f32[48,128]{1,0:T(8,128)S(1)} %get-tuple-element.70.sent_first), channel_id=1, source_target_pairs={{130,132},{132,130},{131,133},{133,131},{134,136},{136,134},{135,1... | collective-permute-start | bytes 73736 | tf_op jit(solution)/shard_map/ppermute | solution.py:514
  46.8 1.9 %collective-permute-start.11 = (f32[48,128]{1,0:T(8,128)S(1)}, f32[48,128]{1,0:T(8,128)S(1)}, u32[]{:S(2)}, u32[]{:S(2)}) collective-permute-start(f32[48,128]{1,0:T(8,128)S(1)} %get-tuple-element.71.sent_second), channel_id=1, source_target_pairs={{128,130},{130,128},{129,131},{131,129},{132,134},{134,132},{133,1... | collective-permute-start | bytes 73736 | tf_op jit(solution)/shard_map/ppermute | solution.py:514
  48.8 2.3 %shard_map.99 = (f32[256,512]{1,0:T(8,128)S(1)}, f32[256,512]{1,0:T(8,128)S(1)}, f32[48,256]{1,0:T(8,128)S(1)}, f32[192,512]{1,0:T(8,128)S(1)}) custom-call(f32[256,512]{1,0:T(8,128)S(1)} %get-tuple-element.72.state, f32[256,512]{1,0:T(8,128)S(1)} %get-tuple-element.73.carry, f32[192,512]{1,0:T(8,128)S(1)} %get-tuple-element.74.force, ...), custom_call_target="tpu_custom_call" | custom-call | flops 1048576 | bytes 6414336 | tf_op jit(solution)/shard_map/pallas_call | solution.py:489
  51.4 1.2 %collective-permute-done.11.second = f32[48,128]{1,0:T(8,128)S(1)} collective-permute-done((f32[48,128]{1,0:T(8,128)S(1)}, f32[48,128]{1,0:T(8,128)S(1)}, u32[]{:S(2)}, u32[]{:S(2)}) %collective-permute-start.11) | collective-permute-done | bytes 24608 | tf_op jit(solution)/shard_map/ppermute | solution.py:514
  53.1 4.7 %collective-permute-start.12 = (f32[48,128]{1,0:T(8,128)S(1)}, f32[48,128]{1,0:T(8,128)S(1)}, u32[]{:S(2)}, u32[]{:S(2)}) collective-permute-start(f32[48,128]{1,0:T(8,128)S(1)} %get-tuple-element.78.sent_first), channel_id=1, source_target_pairs={{130,132},{132,130},{131,133},{133,131},{134,136},{136,134},{135,1... | collective-permute-start | bytes 73736 | tf_op jit(solution)/shard_map/ppermute | solution.py:514
  57.8 1.9 %collective-permute-start.13 = (f32[48,128]{1,0:T(8,128)S(1)}, f32[48,128]{1,0:T(8,128)S(1)}, u32[]{:S(2)}, u32[]{:S(2)}) collective-permute-start(f32[48,128]{1,0:T(8,128)S(1)} %get-tuple-element.79.sent_second), channel_id=1, source_target_pairs={{128,130},{130,128},{129,131},{131,129},{132,134},{134,132},{133,1... | collective-permute-start | bytes 73736 | tf_op jit(solution)/shard_map/ppermute | solution.py:514
  59.8 2.1 %shard_map.101 = (f32[256,512]{1,0:T(8,128)S(1)}, f32[256,512]{1,0:T(8,128)S(1)}, f32[48,256]{1,0:T(8,128)S(1)}) custom-call(f32[256,512]{1,0:T(8,128)S(1)} %get-tuple-element.80.state, f32[256,512]{1,0:T(8,128)S(1)} %get-tuple-element.81.carry, f32[192,512]{1,0:T(8,128)S(1)} %get-tuple-element.82.force, bf16[576,256]{1,0:T(8,128)(2,1)S(1)} %get-tuple-element.83.stacks, ...), custom_call_target="tpu_custom_call" | custom-call | flops 1048576 | bytes 5775360 | tf_op jit(solution)/shard_map/pallas_call | solution.py:489
  62.2 1.4 %collective-permute-done.13.second = f32[48,128]{1,0:T(8,128)S(1)} collective-permute-done((f32[48,128]{1,0:T(8,128)S(1)}, f32[48,128]{1,0:T(8,128)S(1)}, u32[]{:S(2)}, u32[]{:S(2)}) %collective-permute-start.13) | collective-permute-done | bytes 24608 | tf_op jit(solution)/shard_map/ppermute | solution.py:514
  64.1 4.5 %collective-permute-start.14 = (f32[48,128]{1,0:T(8,128)S(1)}, f32[48,128]{1,0:T(8,128)S(1)}, u32[]{:S(2)}, u32[]{:S(2)}) collective-permute-start(f32[48,128]{1,0:T(8,128)S(1)} %get-tuple-element.85.sent_first), channel_id=1, source_target_pairs={{130,132},{132,130},{131,133},{133,131},{134,136},{136,134},{135,1... | collective-permute-start | bytes 73736 | tf_op jit(solution)/shard_map/ppermute | solution.py:514
  68.6 2.1 %collective-permute-start.15 = (f32[48,128]{1,0:T(8,128)S(1)}, f32[48,128]{1,0:T(8,128)S(1)}, u32[]{:S(2)}, u32[]{:S(2)}) collective-permute-start(f32[48,128]{1,0:T(8,128)S(1)} %get-tuple-element.86.sent_second), channel_id=1, source_target_pairs={{128,130},{130,128},{129,131},{131,129},{132,134},{134,132},{133,1... | collective-permute-start | bytes 73736 | tf_op jit(solution)/shard_map/ppermute | solution.py:514
  70.7 2.1 %shard_map.103 = (f32[256,512]{1,0:T(8,128)S(1)}, f32[256,512]{1,0:T(8,128)S(1)}, f32[48,256]{1,0:T(8,128)S(1)}) custom-call(f32[256,512]{1,0:T(8,128)S(1)} %get-tuple-element.87.state, f32[256,512]{1,0:T(8,128)S(1)} %get-tuple-element.88.carry, f32[192,512]{1,0:T(8,128)S(1)} %get-tuple-element.82.force, bf16[576,256]{1,0:T(8,128)(2,1)S(1)} %get-tuple-element.89.stacks, ...), custom_call_target="tpu_custom_call" | custom-call | flops 1048576 | bytes 5775360 | tf_op jit(solution)/shard_map/pallas_call | solution.py:489
  73.2 1.2 %collective-permute-done.15.second = f32[48,128]{1,0:T(8,128)S(1)} collective-permute-done((f32[48,128]{1,0:T(8,128)S(1)}, f32[48,128]{1,0:T(8,128)S(1)}, u32[]{:S(2)}, u32[]{:S(2)}) %collective-permute-start.15) | collective-permute-done | bytes 24608 | tf_op jit(solution)/shard_map/ppermute | solution.py:514
  74.9 4.7 %collective-permute-start.16 = (f32[48,128]{1,0:T(8,128)S(1)}, f32[48,128]{1,0:T(8,128)S(1)}, u32[]{:S(2)}, u32[]{:S(2)}) collective-permute-start(f32[48,128]{1,0:T(8,128)S(1)} %get-tuple-element.91.sent_first), channel_id=1, source_target_pairs={{130,132},{132,130},{131,133},{133,131},{134,136},{136,134},{135,1... | collective-permute-start | bytes 73736 | tf_op jit(solution)/shard_map/ppermute | solution.py:514
  79.6 1.9 %collective-permute-start.17 = (f32[48,128]{1,0:T(8,128)S(1)}, f32[48,128]{1,0:T(8,128)S(1)}, u32[]{:S(2)}, u32[]{:S(2)}) collective-permute-start(f32[48,128]{1,0:T(8,128)S(1)} %get-tuple-element.92.sent_second), channel_id=1, source_target_pairs={{128,130},{130,128},{129,131},{131,129},{132,134},{134,132},{133,1... | collective-permute-start | bytes 73736 | tf_op jit(solution)/shard_map/ppermute | solution.py:514
  81.5 1.7 %shard_map.105.ahead = f32[256,256]{1,0:T(8,128)S(1)} custom-call(f32[256,512]{1,0:T(8,128)S(1)} %get-tuple-element.94.state, f32[256,512]{1,0:T(8,128)S(1)} %get-tuple-element.95.carry, f32[192,512]{1,0:T(8,128)S(1)} %get-tuple-element.82.force, bf16[576,256]{1,0:T(8,128)(2,1)S(1)} %get-tuple-element.96.stacks, ...), custom_call_target="tpu_custom_call" | custom-call | flops 1048576 | bytes 4669440 | tf_op jit(solution)/shard_map/pallas_call | solution.py:489
  83.9 1.4 %collective-permute-done.17.second = f32[48,128]{1,0:T(8,128)S(1)} collective-permute-done((f32[48,128]{1,0:T(8,128)S(1)}, f32[48,128]{1,0:T(8,128)S(1)}, u32[]{:S(2)}, u32[]{:S(2)}) %collective-permute-start.17) | collective-permute-done | bytes 24608 | tf_op jit(solution)/shard_map/ppermute | solution.py:514
  85.3 1.2 %shard_map.106 = f32[256,256]{1,0:T(8,128)} custom-call(f32[48,128]{1,0:T(8,128)S(1)} %collective-permute-done.16.first, f32[48,128]{1,0:T(8,128)S(1)} %collective-permute-done.17.second, f32[48,128]{1,0:T(8,128)S(1)} %get-tuple-element.91.sent_first, f32[48,128]{1,0:T(8,128)S(1)} %get-tuple-element.92.sent_second, f32[8,256]{1,0:T(8,128)S(1)} %get-tuple-element.63.kinds, ...), custom_call_target="tpu_custom_call" | custom-call | flops 1048576 | bytes 1056768 | tf_op jit(solution)/shard_map/pallas_call | solution.py:489
  (29 shorter events, 7.6 us)
Async XLA Ops:
  0.0 26.5 %copy-start.2 = (bf16[288,256]{1,0:T(8,128)(2,1)S(1)}, bf16[288,256]{1,0:T(8,128)(2,1)}, u32[]{:S(2)}) copy-start(bf16[288,256]{1,0:T(8,128)(2,1)} %constant.13.clone.trace) | copy-start | bytes 442372
  1.4 5.3 %collective-permute-start.6 = (f32[192,256]{1,0:T(8,128)S(1)}, f32[192,256]{1,0:T(8,128)S(1)}, u32[]{:S(2)}, u32[]{:S(2)}) collective-permute-start(f32[192,256]{1,0:T(8,128)S(1)} %shard_map.93), channel_id=1, source_target_pairs={{0,384},{1,385},{2,386},{3,387},{4,388},{5,389},{6,390},{7,391},{8... | collective-permute-start | bytes 589832 | tf_op jit(solution)/shard_map/ppermute | solution.py:549
  2.1 4.6 %collective-permute-start.5 = (f32[192,256]{1,0:T(8,128)S(1)}, f32[192,256]{1,0:T(8,128)S(1)}, u32[]{:S(2)}, u32[]{:S(2)}) collective-permute-start(f32[192,256]{1,0:T(8,128)S(1)} %shard_map.93), channel_id=1, source_target_pairs={{0,256},{1,257},{2,258},{3,259},{4,260},{5,261},{6,262},{7,263},{8... | collective-permute-start | bytes 589832 | tf_op jit(solution)/shard_map/ppermute | solution.py:549
  2.7 14.0 %collective-permute-start.4 = (f32[192,256]{1,0:T(8,128)S(1)}, f32[192,256]{1,0:T(8,128)S(1)}, u32[]{:S(2)}, u32[]{:S(2)}) collective-permute-start(f32[192,256]{1,0:T(8,128)S(1)} %shard_map.93), channel_id=1, source_target_pairs={{0,128},{1,129},{2,130},{3,131},{4,132},{5,133},{6,134},{7,135},{8... | collective-permute-start | bytes 589832 | tf_op jit(solution)/shard_map/ppermute | solution.py:549
  4.0 14.8 %collective-permute-start.1 = (f32[264,256]{1,0:T(8,128)S(1)}, f32[264,256]{1,0:T(8,128)S(1)}, u32[]{:S(2)}, u32[]{:S(2)}) collective-permute-start(f32[264,256]{1,0:T(8,128)S(1)} %pad_add_fusion.mine.packed), channel_id=1, source_target_pairs={{0,1},{1,0},{2,3},{3,2},{4,5},{5,4},{6,7},{7,6},{8,9},{9,8},{10,11... | collective-permute-start | bytes 811016 | tf_op jit(solution)/shard_map/ppermute | solution.py:521
  4.7 14.2 %collective-permute-start = (f32[264,256]{1,0:T(8,128)S(1)}, f32[264,256]{1,0:T(8,128)S(1)}, u32[]{:S(2)}, u32[]{:S(2)}) collective-permute-start(f32[264,256]{1,0:T(8,128)S(1)} %pad_add_fusion.mine.packed), channel_id=1, source_target_pairs={{128,129},{129,128},{130,131},{131,130},{132,133},{133,132},{134,1... | collective-permute-start | bytes 811016 | tf_op jit(solution)/shard_map/ppermute | solution.py:521
  16.9 13.1 %collective-permute-start.7 = (f32[192,256]{1,0:T(8,128)S(1)}, f32[192,256]{1,0:T(8,128)S(1)}, u32[]{:S(2)}, u32[]{:S(2)}) collective-permute-start(f32[192,256]{1,0:T(8,128)S(1)} %shard_map.94.force_mine), channel_id=1, source_target_pairs={{128,129},{129,128},{130,131},{131,130},{132,133},{133,132},{134,1... | collective-permute-start | bytes 589832 | tf_op jit(solution)/shard_map/ppermute | solution.py:521
  19.4 19.4 %copy-start = (bf16[256,576]{1,0:T(8,128)(2,1)S(1)}, bf16[256,576]{1,0:T(8,128)(2,1)}, u32[]{:S(2)}) copy-start(bf16[256,576]{1,0:T(8,128)(2,1)} %constant.14.clone.lift_two) | copy-start | bytes 884740
  19.4 19.4 %copy-start.1 = (bf16[256,768]{1,0:T(8,128)(2,1)S(1)}, bf16[256,768]{1,0:T(8,128)(2,1)}, u32[]{:S(2)}) copy-start(bf16[256,768]{1,0:T(8,128)(2,1)} %constant.12.clone.interior) | copy-start | bytes 1179652
  19.4 9.5 %collective-permute-start.2 = (f32[48,256]{1,0:T(8,128)S(1)}, f32[48,256]{1,0:T(8,128)S(1)}, u32[]{:S(2)}, u32[]{:S(2)}) collective-permute-start(f32[48,256]{1,0:T(8,128)S(1)} %get-tuple-element.51), channel_id=1, source_target_pairs={{2,4},{4,2},{3,5},{5,3},{6,8},{8,6},{7,9},{9,7},{10,12},{12,10},{1... | collective-permute-start | bytes 147464 | tf_op jit(solution)/shard_map/ppermute | solution.py:514
  24.0 6.0 %collective-permute-start.3 = (f32[48,256]{1,0:T(8,128)S(1)}, f32[48,256]{1,0:T(8,128)S(1)}, u32[]{:S(2)}, u32[]{:S(2)}) collective-permute-start(f32[48,256]{1,0:T(8,128)S(1)} %get-tuple-element.52), channel_id=1, source_target_pairs={{0,2},{2,0},{1,3},{3,1},{4,6},{6,4},{5,7},{7,5},{8,10},{10,8},{9,1... | collective-permute-start | bytes 147464 | tf_op jit(solution)/shard_map/ppermute | solution.py:514
  30.6 10.3 %collective-permute-start.8 = (f32[48,384]{1,0:T(8,128)S(1)}, f32[48,384]{1,0:T(8,128)S(1)}, u32[]{:S(2)}, u32[]{:S(2)}) collective-permute-start(f32[48,384]{1,0:T(8,128)S(1)} %get-tuple-element.58), channel_id=1, source_target_pairs={{130,132},{132,130},{131,133},{133,131},{134,136},{136,134},{135,1... | collective-permute-start | bytes 221192 | tf_op jit(solution)/shard_map/ppermute | solution.py:514
  35.3 6.2 %collective-permute-start.9 = (f32[48,384]{1,0:T(8,128)S(1)}, f32[48,384]{1,0:T(8,128)S(1)}, u32[]{:S(2)}, u32[]{:S(2)}) collective-permute-start(f32[48,384]{1,0:T(8,128)S(1)} %get-tuple-element.59), channel_id=1, source_target_pairs={{128,130},{130,128},{129,131},{131,129},{132,134},{134,132},{133,1... | collective-permute-start | bytes 221192 | tf_op jit(solution)/shard_map/ppermute | solution.py:514
  38.8 2.7 %copy-start.3 = (bf16[288,576]{1,0:T(8,128)(2,1)S(1)}, bf16[288,576]{1,0:T(8,128)(2,1)}, u32[]{:S(2)}) copy-start(bf16[288,576]{1,0:T(8,128)(2,1)} %constant.15.clone.reach) | copy-start | bytes 995332
  42.4 9.0 %collective-permute-start.10 = (f32[48,128]{1,0:T(8,128)S(1)}, f32[48,128]{1,0:T(8,128)S(1)}, u32[]{:S(2)}, u32[]{:S(2)}) collective-permute-start(f32[48,128]{1,0:T(8,128)S(1)} %get-tuple-element.70.sent_first), channel_id=1, source_target_pairs={{130,132},{132,130},{131,133},{133,131},{134,136},{136,134},{135,1... | collective-permute-start | bytes 73736 | tf_op jit(solution)/shard_map/ppermute | solution.py:514
  46.8 5.7 %collective-permute-start.11 = (f32[48,128]{1,0:T(8,128)S(1)}, f32[48,128]{1,0:T(8,128)S(1)}, u32[]{:S(2)}, u32[]{:S(2)}) collective-permute-start(f32[48,128]{1,0:T(8,128)S(1)} %get-tuple-element.71.sent_second), channel_id=1, source_target_pairs={{128,130},{130,128},{129,131},{131,129},{132,134},{134,132},{133,1... | collective-permute-start | bytes 73736 | tf_op jit(solution)/shard_map/ppermute | solution.py:514
  53.1 9.0 %collective-permute-start.12 = (f32[48,128]{1,0:T(8,128)S(1)}, f32[48,128]{1,0:T(8,128)S(1)}, u32[]{:S(2)}, u32[]{:S(2)}) collective-permute-start(f32[48,128]{1,0:T(8,128)S(1)} %get-tuple-element.78.sent_first), channel_id=1, source_target_pairs={{130,132},{132,130},{131,133},{133,131},{134,136},{136,134},{135,1... | collective-permute-start | bytes 73736 | tf_op jit(solution)/shard_map/ppermute | solution.py:514
  57.8 5.7 %collective-permute-start.13 = (f32[48,128]{1,0:T(8,128)S(1)}, f32[48,128]{1,0:T(8,128)S(1)}, u32[]{:S(2)}, u32[]{:S(2)}) collective-permute-start(f32[48,128]{1,0:T(8,128)S(1)} %get-tuple-element.79.sent_second), channel_id=1, source_target_pairs={{128,130},{130,128},{129,131},{131,129},{132,134},{134,132},{133,1... | collective-permute-start | bytes 73736 | tf_op jit(solution)/shard_map/ppermute | solution.py:514
  64.1 9.0 %collective-permute-start.14 = (f32[48,128]{1,0:T(8,128)S(1)}, f32[48,128]{1,0:T(8,128)S(1)}, u32[]{:S(2)}, u32[]{:S(2)}) collective-permute-start(f32[48,128]{1,0:T(8,128)S(1)} %get-tuple-element.85.sent_first), channel_id=1, source_target_pairs={{130,132},{132,130},{131,133},{133,131},{134,136},{136,134},{135,1... | collective-permute-start | bytes 73736 | tf_op jit(solution)/shard_map/ppermute | solution.py:514
  68.6 5.7 %collective-permute-start.15 = (f32[48,128]{1,0:T(8,128)S(1)}, f32[48,128]{1,0:T(8,128)S(1)}, u32[]{:S(2)}, u32[]{:S(2)}) collective-permute-start(f32[48,128]{1,0:T(8,128)S(1)} %get-tuple-element.86.sent_second), channel_id=1, source_target_pairs={{128,130},{130,128},{129,131},{131,129},{132,134},{134,132},{133,1... | collective-permute-start | bytes 73736 | tf_op jit(solution)/shard_map/ppermute | solution.py:514
  74.9 9.0 %collective-permute-start.16 = (f32[48,128]{1,0:T(8,128)S(1)}, f32[48,128]{1,0:T(8,128)S(1)}, u32[]{:S(2)}, u32[]{:S(2)}) collective-permute-start(f32[48,128]{1,0:T(8,128)S(1)} %get-tuple-element.91.sent_first), channel_id=1, source_target_pairs={{130,132},{132,130},{131,133},{133,131},{134,136},{136,134},{135,1... | collective-permute-start | bytes 73736 | tf_op jit(solution)/shard_map/ppermute | solution.py:514
  79.6 5.7 %collective-permute-start.17 = (f32[48,128]{1,0:T(8,128)S(1)}, f32[48,128]{1,0:T(8,128)S(1)}, u32[]{:S(2)}, u32[]{:S(2)}) collective-permute-start(f32[48,128]{1,0:T(8,128)S(1)} %get-tuple-element.92.sent_second), channel_id=1, source_target_pairs={{128,130},{130,128},{129,131},{131,129},{132,134},{134,132},{133,1... | collective-permute-start | bytes 73736 | tf_op jit(solution)/shard_map/ppermute | solution.py:514

commit v4 on v3

--- a/solution.py
+++ b/solution.py
@@ -136,6 +136,11 @@
     return jnp.where(mask, 1.0, 0.0).astype(BF)
 
 
+def rows_named(names, row):
+    hit = names.astype(jnp.int32).astype(jnp.int16) == row
+    return jnp.where(hit, jnp.ones(row.shape, BF), jnp.zeros(row.shape, BF))
+
+
 def lane_iota(shape):
     return lax.broadcasted_iota(jnp.int32, shape, 1)
 
@@ -166,10 +171,10 @@
     got = jnp.concatenate(
         [jnp.where(far, from_right, own_left), jnp.where(far, from_left, own_right)], axis=1
     )
-    masked = jnp.concatenate(
-        [jnp.where(kinds[face : face + 1] > 0, got, 0.0) for face in range(6)], axis=0
-    )
-    return jnp.concatenate(split(masked), axis=0)
+    chosen = jnp.where(kinds > 0, 1.0, 0.0).astype(BF)
+    return jnp.concatenate(
+        [term * chosen[face : face + 1] for term in split(got) for face in range(6)], axis=0
+    )
 
 
 def far_rates(stacks, place, lift_two):
@@ -278,8 +283,8 @@
     count = jnp.sum(members, axis=1, keepdims=True)
     low_place = target_of(members, rank, 0, ((0, 0.0), (1, 256.0 + start_of(count, 1, -1))))
     high_place = target_of(members, rank, 1, ((0, 256.0), (-1, start_of(count, 0, 1))))
-    number = row_iota((512, 256)).astype(F32)
-    keep = jnp.concatenate([one_hot(low_place == number), one_hot(high_place == number)], axis=1)
+    row = row_iota((512, 256)).astype(jnp.int16)
+    keep = jnp.concatenate([rows_named(low_place, row), rows_named(high_place, row)], axis=1)
     keep_out[...] = keep
     column = lane_iota((16, 512)).astype(F32)
     number = row_iota((16, 512)).astype(F32)
@@ -307,7 +312,7 @@
     wide = lane_iota((8, 256))
     second = ((wide >= 48) & (wide < 128)) | ((wide >= 152) & (wide < 200))
     column = jnp.where(names < 0, -1, (names & 255) + jnp.where(second, 256, 0))
-    pick = one_hot(column[0:1] == row_iota((512, 256)))
+    pick = rows_named(column[0:1], row)
     pick_out[...] = pick
     send_kinds = jnp.where((names >> 8) == row_iota((8, 256)), 1.0, 0.0)
     send_kinds_out[...] = send_kinds
@@ -316,26 +321,26 @@
 
 
 def faces_kernel(mine, other, other_flow, pick, local_out, place_out, own_place_out, kinds_out, meet_out):
-    row = row_iota((256, 256))
+    row = row_iota((256, 256)).astype(jnp.int16)
     ones = jnp.ones((8, 256), BF)
     kinds = [jnp.zeros((1, 256), F32)] * 6
     places = []
     for device, half in enumerate(chip_halves(mine[256:264], other[256:264] + other_flow[256:264])):
-        place = jnp.zeros((256, 256), F32)
+        place = jnp.zeros((256, 256), BF)
         for face in range(6):
             where = half[face : face + 1].astype(jnp.int32)
-            local_out[6 * device + face] = one_hot(where - ELEMENTS * (face ^ 1) == row)
+            local_out[6 * device + face] = rows_named(where - ELEMENTS * (face ^ 1), row)
             n = where - 6 * ELEMENTS
             if device == 0:
                 entry = jnp.where(n < 48, n + 128, jnp.where(n < 72, n + 24, n - 72))
             else:
                 entry = jnp.where(n < 48, n + 176, n - 24)
-            hit = jnp.where(jnp.where(n < 0, -1, entry) == row, 1.0, 0.0)
+            hit = rows_named(jnp.where(n < 0, -1, entry), row)
             place = place + hit
-            kinds[face] = kinds[face] + mm_nt(ones, hit.astype(BF))[0:1]
+            kinds[face] = kinds[face] + mm_nt(ones, hit)[0:1]
         places.append(place)
-    own_place_out[...] = jnp.where(core_number() == 0, places[0], places[1]).astype(BF)
-    place = jnp.concatenate(places, axis=1).astype(BF)
+    own_place_out[...] = jnp.where(core_number() == 0, places[0], places[1])
+    place = jnp.concatenate(places, axis=1)
     place_out[...] = place
     kinds_out[...] = jnp.concatenate(kinds + [jnp.zeros((2, 256), F32)], axis=0)
     meet_out[...] = mm(place, pick[...]).astype(BF)

time: 87.2 us -> 87.2 us (level)
  transfers between devices with their start and end apart: 18 -> 18, of which waited for: 12 -> 12; matrix products, arithmetic and copies ran while one was open for 0% -> 0% of each run, Pallas kernels for 16% -> 15%
where the time goes in v4:
time: 87.2 us; the launch traced here: 86.7 us
  starting transfers between devices  47.3 us (54%)
  waiting for transfers between devices  20.3 us (23%)
  Pallas kernels  17.5 us (20%)
  other arithmetic  1.04 us (1%)
    ppermute x12, starting transfers between devices, trade(): came.append(lax.ppermute(value, ('sec', 'dom'), pairs))  40.1 us
    pallas_call x16, Pallas kernels, call(): pl.pallas_call(kernel, out_shape=list(outs), in_specs=[vmem] * len(args),...  17.5 us
    ppermute x12, waiting for transfers between devices, trade(): came.append(lax.ppermute(value, ('sec', 'dom'), pairs))  10.3 us
    ppermute x3, waiting for transfers between devices, step(): lamb_parts.append(lax.ppermute(lamb, 'sec', [(0, section)]))  10 us
    ppermute x3, starting transfers between devices, swap(): return lax.ppermute(value, ('sec', 'dom'), pairs)  4.52 us
    ppermute x3, starting transfers between devices, step(): lamb_parts.append(lax.ppermute(lamb, 'sec', [(0, section)]))  2.64 us
  transfers between devices with their start and end apart: 18, of which 12 were waited for; matrix products, arithmetic and copies ran while one was open for 0% of the time, Pallas kernels for 15%

profile of v4, /device:TPU:258, one launch (start us, length us, event | category | flops | bytes accessed | tf_op | source)
XLA Modules:
  0.0 86.7 jit_solution(12722805749047644708)
XLA Ops:
  0.0 1.0 %pad_add_fusion.mine.packed = f32[264,256]{1,0:T(8,128)S(1)} fusion(f32[256,256]{1,0:T(8,128)} %bitcast.5, s32[1,96]{1,0:T(1,128)} %bitcast.7, s32[1,64]{1,0:T(1,128)} %bitcast.8, s32[1,256]{1,0:T(1,128)} %bitcast.6, s32[6,256]{1,0:T(8,128)} %param.13), kind=kLoop, calls=%fused_computation | loop fusion | flops 337920 | bytes 540288 | tf_op jit(solution)/shard_map/add | solution.py:550
  2.7 1.3 %collective-permute-start.4 = (f32[192,256]{1,0:T(8,128)S(1)}, f32[192,256]{1,0:T(8,128)S(1)}, u32[]{:S(2)}, u32[]{:S(2)}) collective-permute-start(f32[192,256]{1,0:T(8,128)S(1)} %shard_map.93), channel_id=1, source_target_pairs={{0,128},{1,129},{2,130},{3,131},{4,132},{5,133},{6,134},{7,135},{8... | collective-permute-start | bytes 589832 | tf_op jit(solution)/shard_map/ppermute | solution.py:554
  4.7 1.9 %collective-permute-start = (f32[264,256]{1,0:T(8,128)S(1)}, f32[264,256]{1,0:T(8,128)S(1)}, u32[]{:S(2)}, u32[]{:S(2)}) collective-permute-start(f32[264,256]{1,0:T(8,128)S(1)} %pad_add_fusion.mine.packed), channel_id=1, source_target_pairs={{128,129},{129,128},{130,131},{131,130},{132,133},{133,132},{134,1... | collective-permute-start | bytes 811016 | tf_op jit(solution)/shard_map/ppermute | solution.py:526
  6.7 10.0 %collective-permute-done.4.first = f32[192,256]{1,0:T(8,128)S(1)} collective-permute-done((f32[192,256]{1,0:T(8,128)S(1)}, f32[192,256]{1,0:T(8,128)S(1)}, u32[]{:S(2)}, u32[]{:S(2)}) %collective-permute-start.4) | collective-permute-done | bytes 196640 | tf_op jit(solution)/shard_map/ppermute | solution.py:554
  16.9 1.9 %collective-permute-start.7 = (f32[192,256]{1,0:T(8,128)S(1)}, f32[192,256]{1,0:T(8,128)S(1)}, u32[]{:S(2)}, u32[]{:S(2)}) collective-permute-start(f32[192,256]{1,0:T(8,128)S(1)} %shard_map.94.force_mine), channel_id=1, source_target_pairs={{128,129},{129,128},{130,131},{131,130},{132,133},{133,132},{134,1... | collective-permute-start | bytes 589832 | tf_op jit(solution)/shard_map/ppermute | solution.py:526
  19.4 4.6 %collective-permute-start.2 = (f32[48,256]{1,0:T(8,128)S(1)}, f32[48,256]{1,0:T(8,128)S(1)}, u32[]{:S(2)}, u32[]{:S(2)}) collective-permute-start(f32[48,256]{1,0:T(8,128)S(1)} %get-tuple-element.51), channel_id=1, source_target_pairs={{2,4},{4,2},{3,5},{5,3},{6,8},{8,6},{7,9},{9,7},{10,12},{12,10},{1... | collective-permute-start | bytes 147464 | tf_op jit(solution)/shard_map/ppermute | solution.py:519
  24.0 2.5 %collective-permute-start.3 = (f32[48,256]{1,0:T(8,128)S(1)}, f32[48,256]{1,0:T(8,128)S(1)}, u32[]{:S(2)}, u32[]{:S(2)}) collective-permute-start(f32[48,256]{1,0:T(8,128)S(1)} %get-tuple-element.52), channel_id=1, source_target_pairs={{0,2},{2,0},{1,3},{3,1},{4,6},{6,4},{5,7},{7,5},{8,10},{10,8},{9,1... | collective-permute-start | bytes 147464 | tf_op jit(solution)/shard_map/ppermute | solution.py:519
  26.5 1.1 %shard_map.92 = (f32[256,512]{1,0:T(8,128)S(1)}, bf16[512,512]{1,0:T(8,128)(2,1)S(1)}, bf16[96,512]{1,0:T(8,128)(2,1)S(1)}, bf16[512,256]{1,0:T(8,128)(2,1)S(1)}...) custom-call(f32[264,256]{1,0:T(8,128)S(1)} %pad_add_fusion.mine.packed, ...), custom_call_target="tpu_custom_call" | custom-call | flops 1048576 | bytes 2506752 | tf_op jit(solution)/shard_map/pallas_call | solution.py:494
  27.6 1.3 %collective-permute-done.2.first = f32[48,256]{1,0:T(8,128)S(1)} collective-permute-done((f32[48,256]{1,0:T(8,128)S(1)}, f32[48,256]{1,0:T(8,128)S(1)}, u32[]{:S(2)}, u32[]{:S(2)}) %collective-permute-start.2) | collective-permute-done | bytes 49184 | tf_op jit(solution)/shard_map/ppermute | solution.py:519
  28.9 1.1 %collective-permute-done.3.second = f32[48,256]{1,0:T(8,128)S(1)} collective-permute-done((f32[48,256]{1,0:T(8,128)S(1)}, f32[48,256]{1,0:T(8,128)S(1)}, u32[]{:S(2)}, u32[]{:S(2)}) %collective-permute-start.3) | collective-permute-done | bytes 49184 | tf_op jit(solution)/shard_map/ppermute | solution.py:519
  30.6 4.7 %collective-permute-start.8 = (f32[48,384]{1,0:T(8,128)S(1)}, f32[48,384]{1,0:T(8,128)S(1)}, u32[]{:S(2)}, u32[]{:S(2)}) collective-permute-start(f32[48,384]{1,0:T(8,128)S(1)} %get-tuple-element.58), channel_id=1, source_target_pairs={{130,132},{132,130},{131,133},{133,131},{134,136},{136,134},{135,1... | collective-permute-start | bytes 221192 | tf_op jit(solution)/shard_map/ppermute | solution.py:519
  35.3 2.1 %collective-permute-start.9 = (f32[48,384]{1,0:T(8,128)S(1)}, f32[48,384]{1,0:T(8,128)S(1)}, u32[]{:S(2)}, u32[]{:S(2)}) collective-permute-start(f32[48,384]{1,0:T(8,128)S(1)} %get-tuple-element.59), channel_id=1, source_target_pairs={{128,130},{130,128},{129,131},{131,129},{132,134},{134,132},{133,1... | collective-permute-start | bytes 221192 | tf_op jit(solution)/shard_map/ppermute | solution.py:519
  38.2 2.1 %shard_map.97 = (f32[256,512]{1,0:T(8,128)S(1)}, f32[256,512]{1,0:T(8,128)S(1)}, f32[192,512]{1,0:T(8,128)S(1)}, f32[48,256]{1,0:T(8,128)S(1)}) custom-call(f32[48,256]{1,0:T(8,128)S(1)} %collective-permute-done.2.first, f32[48,256]{1,0:T(8,128)S(1)} %collective-permute-done.3.second, f32[256,512]{1,0:T(8,128)S(1)} %get-tuple-element.65.kept, ...), custom_call_target="tpu_custom_call" | custom-call | flops 1048576 | bytes 5808128 | tf_op jit(solution)/shard_map/pallas_call | solution.py:494
  40.3 1.2 %collective-permute-done.9.second.refs_1_ = f32[48,384]{1,0:T(8,128)S(1)} collective-permute-done((f32[48,384]{1,0:T(8,128)S(1)}, f32[48,384]{1,0:T(8,128)S(1)}, u32[]{:S(2)}, u32[]{:S(2)}) %collective-permute-start.9) | collective-permute-done | bytes 73760 | tf_op jit(solution)/shard_map/ppermute | solution.py:519
  41.5 0.8 shard_map.98
  42.4 4.5 %collective-permute-start.10 = (f32[48,128]{1,0:T(8,128)S(1)}, f32[48,128]{1,0:T(8,128)S(1)}, u32[]{:S(2)}, u32[]{:S(2)}) collective-permute-start(f32[48,128]{1,0:T(8,128)S(1)} %get-tuple-element.70.sent_first), channel_id=1, source_target_pairs={{130,132},{132,130},{131,133},{133,131},{134,136},{136,134},{135,1... | collective-permute-start | bytes 73736 | tf_op jit(solution)/shard_map/ppermute | solution.py:519
  46.8 1.9 %collective-permute-start.11 = (f32[48,128]{1,0:T(8,128)S(1)}, f32[48,128]{1,0:T(8,128)S(1)}, u32[]{:S(2)}, u32[]{:S(2)}) collective-permute-start(f32[48,128]{1,0:T(8,128)S(1)} %get-tuple-element.71.sent_second), channel_id=1, source_target_pairs={{128,130},{130,128},{129,131},{131,129},{132,134},{134,132},{133,1... | collective-permute-start | bytes 73736 | tf_op jit(solution)/shard_map/ppermute | solution.py:519
  48.8 2.3 %shard_map.99 = (f32[256,512]{1,0:T(8,128)S(1)}, f32[256,512]{1,0:T(8,128)S(1)}, f32[48,256]{1,0:T(8,128)S(1)}, f32[192,512]{1,0:T(8,128)S(1)}) custom-call(f32[256,512]{1,0:T(8,128)S(1)} %get-tuple-element.72.state, f32[256,512]{1,0:T(8,128)S(1)} %get-tuple-element.73.carry, f32[192,512]{1,0:T(8,128)S(1)} %get-tuple-element.74.force, ...), custom_call_target="tpu_custom_call" | custom-call | flops 1048576 | bytes 6414336 | tf_op jit(solution)/shard_map/pallas_call | solution.py:494
  51.4 1.2 %collective-permute-done.11.second = f32[48,128]{1,0:T(8,128)S(1)} collective-permute-done((f32[48,128]{1,0:T(8,128)S(1)}, f32[48,128]{1,0:T(8,128)S(1)}, u32[]{:S(2)}, u32[]{:S(2)}) %collective-permute-start.11) | collective-permute-done | bytes 24608 | tf_op jit(solution)/shard_map/ppermute | solution.py:519
  53.1 4.7 %collective-permute-start.12 = (f32[48,128]{1,0:T(8,128)S(1)}, f32[48,128]{1,0:T(8,128)S(1)}, u32[]{:S(2)}, u32[]{:S(2)}) collective-permute-start(f32[48,128]{1,0:T(8,128)S(1)} %get-tuple-element.78.sent_first), channel_id=1, source_target_pairs={{130,132},{132,130},{131,133},{133,131},{134,136},{136,134},{135,1... | collective-permute-start | bytes 73736 | tf_op jit(solution)/shard_map/ppermute | solution.py:519
  57.8 1.9 %collective-permute-start.13 = (f32[48,128]{1,0:T(8,128)S(1)}, f32[48,128]{1,0:T(8,128)S(1)}, u32[]{:S(2)}, u32[]{:S(2)}) collective-permute-start(f32[48,128]{1,0:T(8,128)S(1)} %get-tuple-element.79.sent_second), channel_id=1, source_target_pairs={{128,130},{130,128},{129,131},{131,129},{132,134},{134,132},{133,1... | collective-permute-start | bytes 73736 | tf_op jit(solution)/shard_map/ppermute | solution.py:519
  59.7 2.1 %shard_map.101 = (f32[256,512]{1,0:T(8,128)S(1)}, f32[256,512]{1,0:T(8,128)S(1)}, f32[48,256]{1,0:T(8,128)S(1)}) custom-call(f32[256,512]{1,0:T(8,128)S(1)} %get-tuple-element.80.state, f32[256,512]{1,0:T(8,128)S(1)} %get-tuple-element.81.carry, f32[192,512]{1,0:T(8,128)S(1)} %get-tuple-element.82.force, bf16[576,256]{1,0:T(8,128)(2,1)S(1)} %get-tuple-element.83.stacks, ...), custom_call_target="tpu_custom_call" | custom-call | flops 1048576 | bytes 5775360 | tf_op jit(solution)/shard_map/pallas_call | solution.py:494
  62.2 1.4 %collective-permute-done.13.second = f32[48,128]{1,0:T(8,128)S(1)} collective-permute-done((f32[48,128]{1,0:T(8,128)S(1)}, f32[48,128]{1,0:T(8,128)S(1)}, u32[]{:S(2)}, u32[]{:S(2)}) %collective-permute-start.13) | collective-permute-done | bytes 24608 | tf_op jit(solution)/shard_map/ppermute | solution.py:519
  64.1 4.5 %collective-permute-start.14 = (f32[48,128]{1,0:T(8,128)S(1)}, f32[48,128]{1,0:T(8,128)S(1)}, u32[]{:S(2)}, u32[]{:S(2)}) collective-permute-start(f32[48,128]{1,0:T(8,128)S(1)} %get-tuple-element.85.sent_first), channel_id=1, source_target_pairs={{130,132},{132,130},{131,133},{133,131},{134,136},{136,134},{135,1... | collective-permute-start | bytes 73736 | tf_op jit(solution)/shard_map/ppermute | solution.py:519
  68.6 2.1 %collective-permute-start.15 = (f32[48,128]{1,0:T(8,128)S(1)}, f32[48,128]{1,0:T(8,128)S(1)}, u32[]{:S(2)}, u32[]{:S(2)}) collective-permute-start(f32[48,128]{1,0:T(8,128)S(1)} %get-tuple-element.86.sent_second), channel_id=1, source_target_pairs={{128,130},{130,128},{129,131},{131,129},{132,134},{134,132},{133,1... | collective-permute-start | bytes 73736 | tf_op jit(solution)/shard_map/ppermute | solution.py:519
  70.7 2.1 %shard_map.103 = (f32[256,512]{1,0:T(8,128)S(1)}, f32[256,512]{1,0:T(8,128)S(1)}, f32[48,256]{1,0:T(8,128)S(1)}) custom-call(f32[256,512]{1,0:T(8,128)S(1)} %get-tuple-element.87.state, f32[256,512]{1,0:T(8,128)S(1)} %get-tuple-element.88.carry, f32[192,512]{1,0:T(8,128)S(1)} %get-tuple-element.82.force, bf16[576,256]{1,0:T(8,128)(2,1)S(1)} %get-tuple-element.89.stacks, ...), custom_call_target="tpu_custom_call" | custom-call | flops 1048576 | bytes 5775360 | tf_op jit(solution)/shard_map/pallas_call | solution.py:494
  73.1 1.2 %collective-permute-done.15.second = f32[48,128]{1,0:T(8,128)S(1)} collective-permute-done((f32[48,128]{1,0:T(8,128)S(1)}, f32[48,128]{1,0:T(8,128)S(1)}, u32[]{:S(2)}, u32[]{:S(2)}) %collective-permute-start.15) | collective-permute-done | bytes 24608 | tf_op jit(solution)/shard_map/ppermute | solution.py:519
  74.9 4.7 %collective-permute-start.16 = (f32[48,128]{1,0:T(8,128)S(1)}, f32[48,128]{1,0:T(8,128)S(1)}, u32[]{:S(2)}, u32[]{:S(2)}) collective-permute-start(f32[48,128]{1,0:T(8,128)S(1)} %get-tuple-element.91.sent_first), channel_id=1, source_target_pairs={{130,132},{132,130},{131,133},{133,131},{134,136},{136,134},{135,1... | collective-permute-start | bytes 73736 | tf_op jit(solution)/shard_map/ppermute | solution.py:519
  79.6 1.9 %collective-permute-start.17 = (f32[48,128]{1,0:T(8,128)S(1)}, f32[48,128]{1,0:T(8,128)S(1)}, u32[]{:S(2)}, u32[]{:S(2)}) collective-permute-start(f32[48,128]{1,0:T(8,128)S(1)} %get-tuple-element.92.sent_second), channel_id=1, source_target_pairs={{128,130},{130,128},{129,131},{131,129},{132,134},{134,132},{133,1... | collective-permute-start | bytes 73736 | tf_op jit(solution)/shard_map/ppermute | solution.py:519
  81.5 1.7 %shard_map.105.ahead = f32[256,256]{1,0:T(8,128)S(1)} custom-call(f32[256,512]{1,0:T(8,128)S(1)} %get-tuple-element.94.state, f32[256,512]{1,0:T(8,128)S(1)} %get-tuple-element.95.carry, f32[192,512]{1,0:T(8,128)S(1)} %get-tuple-element.82.force, bf16[576,256]{1,0:T(8,128)(2,1)S(1)} %get-tuple-element.96.stacks, ...), custom_call_target="tpu_custom_call" | custom-call | flops 1048576 | bytes 4669440 | tf_op jit(solution)/shard_map/pallas_call | solution.py:494
  83.9 1.4 %collective-permute-done.17.second = f32[48,128]{1,0:T(8,128)S(1)} collective-permute-done((f32[48,128]{1,0:T(8,128)S(1)}, f32[48,128]{1,0:T(8,128)S(1)}, u32[]{:S(2)}, u32[]{:S(2)}) %collective-permute-start.17) | collective-permute-done | bytes 24608 | tf_op jit(solution)/shard_map/ppermute | solution.py:519
  85.3 1.2 %shard_map.106 = f32[256,256]{1,0:T(8,128)} custom-call(f32[48,128]{1,0:T(8,128)S(1)} %collective-permute-done.16.first, f32[48,128]{1,0:T(8,128)S(1)} %collective-permute-done.17.second, f32[48,128]{1,0:T(8,128)S(1)} %get-tuple-element.91.sent_first, f32[48,128]{1,0:T(8,128)S(1)} %get-tuple-element.92.sent_second, f32[8,256]{1,0:T(8,128)S(1)} %get-tuple-element.63.kinds, ...), custom_call_target="tpu_custom_call" | custom-call | flops 1048576 | bytes 1056768 | tf_op jit(solution)/shard_map/pallas_call | solution.py:494
  (29 shorter events, 7.7 us)
Async XLA Ops:
  0.0 26.5 %copy-start.2 = (bf16[288,256]{1,0:T(8,128)(2,1)S(1)}, bf16[288,256]{1,0:T(8,128)(2,1)}, u32[]{:S(2)}) copy-start(bf16[288,256]{1,0:T(8,128)(2,1)} %constant.13.clone.trace) | copy-start | bytes 442372
  1.4 5.3 %collective-permute-start.6 = (f32[192,256]{1,0:T(8,128)S(1)}, f32[192,256]{1,0:T(8,128)S(1)}, u32[]{:S(2)}, u32[]{:S(2)}) collective-permute-start(f32[192,256]{1,0:T(8,128)S(1)} %shard_map.93), channel_id=1, source_target_pairs={{0,384},{1,385},{2,386},{3,387},{4,388},{5,389},{6,390},{7,391},{8... | collective-permute-start | bytes 589832 | tf_op jit(solution)/shard_map/ppermute | solution.py:554
  2.1 4.6 %collective-permute-start.5 = (f32[192,256]{1,0:T(8,128)S(1)}, f32[192,256]{1,0:T(8,128)S(1)}, u32[]{:S(2)}, u32[]{:S(2)}) collective-permute-start(f32[192,256]{1,0:T(8,128)S(1)} %shard_map.93), channel_id=1, source_target_pairs={{0,256},{1,257},{2,258},{3,259},{4,260},{5,261},{6,262},{7,263},{8... | collective-permute-start | bytes 589832 | tf_op jit(solution)/shard_map/ppermute | solution.py:554
  2.7 14.0 %collective-permute-start.4 = (f32[192,256]{1,0:T(8,128)S(1)}, f32[192,256]{1,0:T(8,128)S(1)}, u32[]{:S(2)}, u32[]{:S(2)}) collective-permute-start(f32[192,256]{1,0:T(8,128)S(1)} %shard_map.93), channel_id=1, source_target_pairs={{0,128},{1,129},{2,130},{3,131},{4,132},{5,133},{6,134},{7,135},{8... | collective-permute-start | bytes 589832 | tf_op jit(solution)/shard_map/ppermute | solution.py:554
  4.0 14.8 %collective-permute-start.1 = (f32[264,256]{1,0:T(8,128)S(1)}, f32[264,256]{1,0:T(8,128)S(1)}, u32[]{:S(2)}, u32[]{:S(2)}) collective-permute-start(f32[264,256]{1,0:T(8,128)S(1)} %pad_add_fusion.mine.packed), channel_id=1, source_target_pairs={{0,1},{1,0},{2,3},{3,2},{4,5},{5,4},{6,7},{7,6},{8,9},{9,8},{10,11... | collective-permute-start | bytes 811016 | tf_op jit(solution)/shard_map/ppermute | solution.py:526
  4.7 14.2 %collective-permute-start = (f32[264,256]{1,0:T(8,128)S(1)}, f32[264,256]{1,0:T(8,128)S(1)}, u32[]{:S(2)}, u32[]{:S(2)}) collective-permute-start(f32[264,256]{1,0:T(8,128)S(1)} %pad_add_fusion.mine.packed), channel_id=1, source_target_pairs={{128,129},{129,128},{130,131},{131,130},{132,133},{133,132},{134,1... | collective-permute-start | bytes 811016 | tf_op jit(solution)/shard_map/ppermute | solution.py:526
  16.9 13.1 %collective-permute-start.7 = (f32[192,256]{1,0:T(8,128)S(1)}, f32[192,256]{1,0:T(8,128)S(1)}, u32[]{:S(2)}, u32[]{:S(2)}) collective-permute-start(f32[192,256]{1,0:T(8,128)S(1)} %shard_map.94.force_mine), channel_id=1, source_target_pairs={{128,129},{129,128},{130,131},{131,130},{132,133},{133,132},{134,1... | collective-permute-start | bytes 589832 | tf_op jit(solution)/shard_map/ppermute | solution.py:526
  19.4 18.8 %copy-start = (bf16[256,576]{1,0:T(8,128)(2,1)S(1)}, bf16[256,576]{1,0:T(8,128)(2,1)}, u32[]{:S(2)}) copy-start(bf16[256,576]{1,0:T(8,128)(2,1)} %constant.14.clone.lift_two) | copy-start | bytes 884740
  19.4 18.8 %copy-start.1 = (bf16[256,768]{1,0:T(8,128)(2,1)S(1)}, bf16[256,768]{1,0:T(8,128)(2,1)}, u32[]{:S(2)}) copy-start(bf16[256,768]{1,0:T(8,128)(2,1)} %constant.12.clone.interior) | copy-start | bytes 1179652
  19.4 9.5 %collective-permute-start.2 = (f32[48,256]{1,0:T(8,128)S(1)}, f32[48,256]{1,0:T(8,128)S(1)}, u32[]{:S(2)}, u32[]{:S(2)}) collective-permute-start(f32[48,256]{1,0:T(8,128)S(1)} %get-tuple-element.51), channel_id=1, source_target_pairs={{2,4},{4,2},{3,5},{5,3},{6,8},{8,6},{7,9},{9,7},{10,12},{12,10},{1... | collective-permute-start | bytes 147464 | tf_op jit(solution)/shard_map/ppermute | solution.py:519
  24.0 6.0 %collective-permute-start.3 = (f32[48,256]{1,0:T(8,128)S(1)}, f32[48,256]{1,0:T(8,128)S(1)}, u32[]{:S(2)}, u32[]{:S(2)}) collective-permute-start(f32[48,256]{1,0:T(8,128)S(1)} %get-tuple-element.52), channel_id=1, source_target_pairs={{0,2},{2,0},{1,3},{3,1},{4,6},{6,4},{5,7},{7,5},{8,10},{10,8},{9,1... | collective-permute-start | bytes 147464 | tf_op jit(solution)/shard_map/ppermute | solution.py:519
  30.6 9.7 %collective-permute-start.8 = (f32[48,384]{1,0:T(8,128)S(1)}, f32[48,384]{1,0:T(8,128)S(1)}, u32[]{:S(2)}, u32[]{:S(2)}) collective-permute-start(f32[48,384]{1,0:T(8,128)S(1)} %get-tuple-element.58), channel_id=1, source_target_pairs={{130,132},{132,130},{131,133},{133,131},{134,136},{136,134},{135,1... | collective-permute-start | bytes 221192 | tf_op jit(solution)/shard_map/ppermute | solution.py:519
  35.3 6.2 %collective-permute-start.9 = (f32[48,384]{1,0:T(8,128)S(1)}, f32[48,384]{1,0:T(8,128)S(1)}, u32[]{:S(2)}, u32[]{:S(2)}) collective-permute-start(f32[48,384]{1,0:T(8,128)S(1)} %get-tuple-element.59), channel_id=1, source_target_pairs={{128,130},{130,128},{129,131},{131,129},{132,134},{134,132},{133,1... | collective-permute-start | bytes 221192 | tf_op jit(solution)/shard_map/ppermute | solution.py:519
  38.2 3.4 %copy-start.3 = (bf16[288,576]{1,0:T(8,128)(2,1)S(1)}, bf16[288,576]{1,0:T(8,128)(2,1)}, u32[]{:S(2)}) copy-start(bf16[288,576]{1,0:T(8,128)(2,1)} %constant.15.clone.reach) | copy-start | bytes 995332
  42.4 9.0 %collective-permute-start.10 = (f32[48,128]{1,0:T(8,128)S(1)}, f32[48,128]{1,0:T(8,128)S(1)}, u32[]{:S(2)}, u32[]{:S(2)}) collective-permute-start(f32[48,128]{1,0:T(8,128)S(1)} %get-tuple-element.70.sent_first), channel_id=1, source_target_pairs={{130,132},{132,130},{131,133},{133,131},{134,136},{136,134},{135,1... | collective-permute-start | bytes 73736 | tf_op jit(solution)/shard_map/ppermute | solution.py:519
  46.8 5.7 %collective-permute-start.11 = (f32[48,128]{1,0:T(8,128)S(1)}, f32[48,128]{1,0:T(8,128)S(1)}, u32[]{:S(2)}, u32[]{:S(2)}) collective-permute-start(f32[48,128]{1,0:T(8,128)S(1)} %get-tuple-element.71.sent_second), channel_id=1, source_target_pairs={{128,130},{130,128},{129,131},{131,129},{132,134},{134,132},{133,1... | collective-permute-start | bytes 73736 | tf_op jit(solution)/shard_map/ppermute | solution.py:519
  53.1 9.0 %collective-permute-start.12 = (f32[48,128]{1,0:T(8,128)S(1)}, f32[48,128]{1,0:T(8,128)S(1)}, u32[]{:S(2)}, u32[]{:S(2)}) collective-permute-start(f32[48,128]{1,0:T(8,128)S(1)} %get-tuple-element.78.sent_first), channel_id=1, source_target_pairs={{130,132},{132,130},{131,133},{133,131},{134,136},{136,134},{135,1... | collective-permute-start | bytes 73736 | tf_op jit(solution)/shard_map/ppermute | solution.py:519
  57.8 5.7 %collective-permute-start.13 = (f32[48,128]{1,0:T(8,128)S(1)}, f32[48,128]{1,0:T(8,128)S(1)}, u32[]{:S(2)}, u32[]{:S(2)}) collective-permute-start(f32[48,128]{1,0:T(8,128)S(1)} %get-tuple-element.79.sent_second), channel_id=1, source_target_pairs={{128,130},{130,128},{129,131},{131,129},{132,134},{134,132},{133,1... | collective-permute-start | bytes 73736 | tf_op jit(solution)/shard_map/ppermute | solution.py:519
  64.1 9.0 %collective-permute-start.14 = (f32[48,128]{1,0:T(8,128)S(1)}, f32[48,128]{1,0:T(8,128)S(1)}, u32[]{:S(2)}, u32[]{:S(2)}) collective-permute-start(f32[48,128]{1,0:T(8,128)S(1)} %get-tuple-element.85.sent_first), channel_id=1, source_target_pairs={{130,132},{132,130},{131,133},{133,131},{134,136},{136,134},{135,1... | collective-permute-start | bytes 73736 | tf_op jit(solution)/shard_map/ppermute | solution.py:519
  68.6 5.7 %collective-permute-start.15 = (f32[48,128]{1,0:T(8,128)S(1)}, f32[48,128]{1,0:T(8,128)S(1)}, u32[]{:S(2)}, u32[]{:S(2)}) collective-permute-start(f32[48,128]{1,0:T(8,128)S(1)} %get-tuple-element.86.sent_second), channel_id=1, source_target_pairs={{128,130},{130,128},{129,131},{131,129},{132,134},{134,132},{133,1... | collective-permute-start | bytes 73736 | tf_op jit(solution)/shard_map/ppermute | solution.py:519
  74.9 9.0 %collective-permute-start.16 = (f32[48,128]{1,0:T(8,128)S(1)}, f32[48,128]{1,0:T(8,128)S(1)}, u32[]{:S(2)}, u32[]{:S(2)}) collective-permute-start(f32[48,128]{1,0:T(8,128)S(1)} %get-tuple-element.91.sent_first), channel_id=1, source_target_pairs={{130,132},{132,130},{131,133},{133,131},{134,136},{136,134},{135,1... | collective-permute-start | bytes 73736 | tf_op jit(solution)/shard_map/ppermute | solution.py:519
  79.6 5.7 %collective-permute-start.17 = (f32[48,128]{1,0:T(8,128)S(1)}, f32[48,128]{1,0:T(8,128)S(1)}, u32[]{:S(2)}, u32[]{:S(2)}) collective-permute-start(f32[48,128]{1,0:T(8,128)S(1)} %get-tuple-element.92.sent_second), channel_id=1, source_target_pairs={{128,130},{130,128},{129,131},{131,129},{132,134},{134,132},{133,1... | collective-permute-start | bytes 73736 | tf_op jit(solution)/shard_map/ppermute | solution.py:519

commit v5 on v4

--- a/solution.py
+++ b/solution.py
@@ -418,20 +418,17 @@
 
 
 def first_outer_kernel(
-    first, second, sent_first, sent_second, kinds, meet, reach, send_kinds, base, trace, arrive_pick,
+    first, second, sent_first, sent_second, kinds, meet, reach_force, send_kinds, base, arrive_pick,
     stacks_out, first_out, second_out,
 ):
     stacks = by_kind(
         (first[:, 256:384], second[:, 256:384]), (sent_first[...], sent_second[...]), kinds[...]
     )
     stacks_out[...] = stacks
-    shown = LIFT * mm(reach[...], mm(stacks, meet[...]).astype(BF))
-    chosen = [
-        jnp.concatenate([jnp.zeros((64, 256), BF), mm(term[0:192], arrive_pick[...]).astype(BF)], axis=0)
-        for term in came_columns(first[:, 0:256], second[:, 0:256])
-    ]
-    pushed = mm(trace[...], jnp.concatenate(chosen, axis=1))
-    shown = shown + (pushed[:, :256] + pushed[:, 256:])
+    parts = [mm(stacks, meet[...]).astype(BF)]
+    for term in came_columns(first[:, 0:256], second[:, 0:256]):
+        parts.append(mm(term[0:192], arrive_pick[...]).astype(BF))
+    shown = mm(reach_force[...], jnp.concatenate(parts, axis=0))
     sent = base[...] + (weight_of(0) * F32(TIME_STEP)) * of_kind(shown, send_kinds[...])
     first_out[...], second_out[...] = sides(sent[:, :LANES], sent[:, LANES:])
 
@@ -532,7 +529,10 @@
     interior = jnp.asarray(np.concatenate([high, high, low], axis=1))
     trace = jnp.asarray(trace_matrix().astype(BF))
     lift_two = jnp.asarray(np.concatenate([lift_matrix()] * 2, axis=1).astype(BF))
-    reach = jnp.asarray(np.concatenate([trace_matrix() @ lift_matrix()] * 2, axis=1).astype(BF))
+    across = np.concatenate([trace_matrix() @ lift_matrix()] * 2, axis=1)
+    reach = jnp.asarray(across.astype(BF))
+    pushed = [trace_matrix()[:, 64:256]] * 2
+    reach_force = jnp.asarray(np.concatenate([LIFT * across, *pushed], axis=1).astype(BF))
     every = range(lax.axis_size("sec"))
     acoustic = every[1:]
     piece, whole = arr(TRACE_ROWS, LANES), arr(256, 512)
@@ -607,7 +607,7 @@
     stacks, *later = call(
         first_outer_kernel,
         sending,
-        *came, *sent, kinds, meet, reach, send_kinds, base, trace, arrive_pick,
+        *came, *sent, kinds, meet, reach_force, send_kinds, base, arrive_pick,
     )
     extra = [*came, arrive]
     for segment in range(1, 5):

time: 87.2 us -> 86.9 us (level)
  the two profiles are of different devices: /device:TPU:258 before, /device:TPU:250 now
where the time goes in v5:
time: 86.9 us; the launch traced here: 86.4 us
  starting transfers between devices  46.3 us (53%)
  waiting for transfers between devices  21.3 us (25%)
  Pallas kernels  17.4 us (20%)
  other arithmetic  1.04 us (1%)
    ppermute x12, starting transfers between devices, trade(): came.append(lax.ppermute(value, ('sec', 'dom'), pairs))  39.1 us
    pallas_call x16, Pallas kernels, call(): pl.pallas_call(kernel, out_shape=list(outs), in_specs=[vmem] * len(args),...  17.4 us
    ppermute x12, waiting for transfers between devices, trade(): came.append(lax.ppermute(value, ('sec', 'dom'), pairs))  11.2 us
    ppermute x3, waiting for transfers between devices, step(): lamb_parts.append(lax.ppermute(lamb, 'sec', [(0, section)]))  10 us
    ppermute x3, starting transfers between devices, swap(): return lax.ppermute(value, ('sec', 'dom'), pairs)  4.52 us
    ppermute x3, starting transfers between devices, step(): lamb_parts.append(lax.ppermute(lamb, 'sec', [(0, section)]))  2.64 us
  transfers between devices with their start and end apart: 18, of which 13 were waited for; matrix products, arithmetic and copies ran while one was open for 0% of the time, Pallas kernels for 15%

profile of v5, /device:TPU:250, one launch (start us, length us, event | category | flops | bytes accessed | tf_op | source)
XLA Modules:
  0.0 86.4 jit_solution(6366589906103826340)
XLA Ops:
  0.0 1.0 %pad_add_fusion.mine.packed = f32[264,256]{1,0:T(8,128)S(1)} fusion(f32[256,256]{1,0:T(8,128)} %bitcast.5, s32[1,96]{1,0:T(1,128)} %bitcast.7, s32[1,64]{1,0:T(1,128)} %bitcast.8, s32[1,256]{1,0:T(1,128)} %bitcast.6, s32[6,256]{1,0:T(8,128)} %param.14), kind=kLoop, calls=%fused_computation | loop fusion | flops 337920 | bytes 540288 | tf_op jit(solution)/shard_map/add | solution.py:550
  2.7 1.3 %collective-permute-start.4 = (f32[192,256]{1,0:T(8,128)S(1)}, f32[192,256]{1,0:T(8,128)S(1)}, u32[]{:S(2)}, u32[]{:S(2)}) collective-permute-start(f32[192,256]{1,0:T(8,128)S(1)} %shard_map.102), channel_id=1, source_target_pairs={{0,128},{1,129},{2,130},{3,131},{4,132},{5,133},{6,134},{7,135},{8... | collective-permute-start | bytes 589832 | tf_op jit(solution)/shard_map/ppermute | solution.py:554
  4.7 1.9 %collective-permute-start = (f32[264,256]{1,0:T(8,128)S(1)}, f32[264,256]{1,0:T(8,128)S(1)}, u32[]{:S(2)}, u32[]{:S(2)}) collective-permute-start(f32[264,256]{1,0:T(8,128)S(1)} %pad_add_fusion.mine.packed), channel_id=1, source_target_pairs={{128,129},{129,128},{130,131},{131,130},{132,133},{133,132},{134,1... | collective-permute-start | bytes 811016 | tf_op jit(solution)/shard_map/ppermute | solution.py:523
  6.7 10.0 %collective-permute-done.4.first = f32[192,256]{1,0:T(8,128)S(1)} collective-permute-done((f32[192,256]{1,0:T(8,128)S(1)}, f32[192,256]{1,0:T(8,128)S(1)}, u32[]{:S(2)}, u32[]{:S(2)}) %collective-permute-start.4) | collective-permute-done | bytes 196640 | tf_op jit(solution)/shard_map/ppermute | solution.py:554
  16.9 1.9 %collective-permute-start.7 = (f32[192,256]{1,0:T(8,128)S(1)}, f32[192,256]{1,0:T(8,128)S(1)}, u32[]{:S(2)}, u32[]{:S(2)}) collective-permute-start(f32[192,256]{1,0:T(8,128)S(1)} %shard_map.103.force_mine), channel_id=1, source_target_pairs={{128,129},{129,128},{130,131},{131,130},{132,133},{133,132},{134,1... | collective-permute-start | bytes 589832 | tf_op jit(solution)/shard_map/ppermute | solution.py:523
  19.4 4.8 %collective-permute-start.2 = (f32[48,256]{1,0:T(8,128)S(1)}, f32[48,256]{1,0:T(8,128)S(1)}, u32[]{:S(2)}, u32[]{:S(2)}) collective-permute-start(f32[48,256]{1,0:T(8,128)S(1)} %get-tuple-element.51), channel_id=1, source_target_pairs={{2,4},{4,2},{3,5},{5,3},{6,8},{8,6},{7,9},{9,7},{10,12},{12,10},{1... | collective-permute-start | bytes 147464 | tf_op jit(solution)/shard_map/ppermute | solution.py:516
  24.2 1.9 %collective-permute-start.3 = (f32[48,256]{1,0:T(8,128)S(1)}, f32[48,256]{1,0:T(8,128)S(1)}, u32[]{:S(2)}, u32[]{:S(2)}) collective-permute-start(f32[48,256]{1,0:T(8,128)S(1)} %get-tuple-element.52), channel_id=1, source_target_pairs={{0,2},{2,0},{1,3},{3,1},{4,6},{6,4},{5,7},{7,5},{8,10},{10,8},{9,1... | collective-permute-start | bytes 147464 | tf_op jit(solution)/shard_map/ppermute | solution.py:516
  26.2 1.1 %shard_map.101 = (f32[256,512]{1,0:T(8,128)S(1)}, bf16[512,512]{1,0:T(8,128)(2,1)S(1)}, bf16[96,512]{1,0:T(8,128)(2,1)S(1)}, bf16[512,256]{1,0:T(8,128)(2,1)S(1)...) custom-call(f32[264,256]{1,0:T(8,128)S(1)} %pad_add_fusion.mine.packed, ...), custom_call_target="tpu_custom_call" | custom-call | flops 1048576 | bytes 2506752 | tf_op jit(solution)/shard_map/pallas_call | solution.py:491
  27.3 1.6 %collective-permute-done.2.first = f32[48,256]{1,0:T(8,128)S(1)} collective-permute-done((f32[48,256]{1,0:T(8,128)S(1)}, f32[48,256]{1,0:T(8,128)S(1)}, u32[]{:S(2)}, u32[]{:S(2)}) %collective-permute-start.2) | collective-permute-done | bytes 49184 | tf_op jit(solution)/shard_map/ppermute | solution.py:516
  28.9 1.3 %collective-permute-done.3.second = f32[48,256]{1,0:T(8,128)S(1)} collective-permute-done((f32[48,256]{1,0:T(8,128)S(1)}, f32[48,256]{1,0:T(8,128)S(1)}, u32[]{:S(2)}, u32[]{:S(2)}) %collective-permute-start.3) | collective-permute-done | bytes 49184 | tf_op jit(solution)/shard_map/ppermute | solution.py:516
  30.8 4.5 %collective-permute-start.8 = (f32[48,384]{1,0:T(8,128)S(1)}, f32[48,384]{1,0:T(8,128)S(1)}, u32[]{:S(2)}, u32[]{:S(2)}) collective-permute-start(f32[48,384]{1,0:T(8,128)S(1)} %get-tuple-element.58), channel_id=1, source_target_pairs={{130,132},{132,130},{131,133},{133,131},{134,136},{136,134},{135,1... | collective-permute-start | bytes 221192 | tf_op jit(solution)/shard_map/ppermute | solution.py:516
  35.3 1.9 %collective-permute-start.9 = (f32[48,384]{1,0:T(8,128)S(1)}, f32[48,384]{1,0:T(8,128)S(1)}, u32[]{:S(2)}, u32[]{:S(2)}) collective-permute-start(f32[48,384]{1,0:T(8,128)S(1)} %get-tuple-element.59), channel_id=1, source_target_pairs={{128,130},{130,128},{129,131},{131,129},{132,134},{134,132},{133,1... | collective-permute-start | bytes 221192 | tf_op jit(solution)/shard_map/ppermute | solution.py:516
  38.0 2.1 %shard_map.106 = (f32[256,512]{1,0:T(8,128)S(1)}, f32[256,512]{1,0:T(8,128)S(1)}, f32[192,512]{1,0:T(8,128)S(1)}, f32[48,256]{1,0:T(8,128)S(1)}) custom-call(f32[48,256]{1,0:T(8,128)S(1)} %collective-permute-done.2.first, f32[48,256]{1,0:T(8,128)S(1)} %collective-permute-done.3.second, f32[256,512]{1,0:T(8,128)S(1)} %get-tuple-element.65.kept, ...), custom_call_target="tpu_custom_call" | custom-call | flops 1048576 | bytes 5808128 | tf_op jit(solution)/shard_map/pallas_call | solution.py:491
  40.4 1.2 %collective-permute-done.9.second.refs_1_ = f32[48,384]{1,0:T(8,128)S(1)} collective-permute-done((f32[48,384]{1,0:T(8,128)S(1)}, f32[48,384]{1,0:T(8,128)S(1)}, u32[]{:S(2)}, u32[]{:S(2)}) %collective-permute-start.9) | collective-permute-done | bytes 73760 | tf_op jit(solution)/shard_map/ppermute | solution.py:516
  42.2 4.7 %collective-permute-start.10 = (f32[48,128]{1,0:T(8,128)S(1)}, f32[48,128]{1,0:T(8,128)S(1)}, u32[]{:S(2)}, u32[]{:S(2)}) collective-permute-start(f32[48,128]{1,0:T(8,128)S(1)} %get-tuple-element.70.sent_first), channel_id=1, source_target_pairs={{130,132},{132,130},{131,133},{133,131},{134,136},{136,134},{135,1... | collective-permute-start | bytes 73736 | tf_op jit(solution)/shard_map/ppermute | solution.py:516
  46.9 1.9 %collective-permute-start.11 = (f32[48,128]{1,0:T(8,128)S(1)}, f32[48,128]{1,0:T(8,128)S(1)}, u32[]{:S(2)}, u32[]{:S(2)}) collective-permute-start(f32[48,128]{1,0:T(8,128)S(1)} %get-tuple-element.71.sent_second), channel_id=1, source_target_pairs={{128,130},{130,128},{129,131},{131,129},{132,134},{134,132},{133,1... | collective-permute-start | bytes 73736 | tf_op jit(solution)/shard_map/ppermute | solution.py:516
  48.8 2.3 %shard_map.108 = (f32[256,512]{1,0:T(8,128)S(1)}, f32[256,512]{1,0:T(8,128)S(1)}, f32[48,256]{1,0:T(8,128)S(1)}, f32[192,512]{1,0:T(8,128)S(1)}) custom-call(f32[256,512]{1,0:T(8,128)S(1)} %get-tuple-element.72.state, f32[256,512]{1,0:T(8,128)S(1)} %get-tuple-element.73.carry, f32[192,512]{1,0:T(8,128)S(1)} %get-tuple-element.74.force, ...), custom_call_target="tpu_custom_call" | custom-call | flops 1048576 | bytes 6414336 | tf_op jit(solution)/shard_map/pallas_call | solution.py:491
  51.2 1.4 %collective-permute-done.11.second = f32[48,128]{1,0:T(8,128)S(1)} collective-permute-done((f32[48,128]{1,0:T(8,128)S(1)}, f32[48,128]{1,0:T(8,128)S(1)}, u32[]{:S(2)}, u32[]{:S(2)}) %collective-permute-start.11) | collective-permute-done | bytes 24608 | tf_op jit(solution)/shard_map/ppermute | solution.py:516
  53.2 4.5 %collective-permute-start.12 = (f32[48,128]{1,0:T(8,128)S(1)}, f32[48,128]{1,0:T(8,128)S(1)}, u32[]{:S(2)}, u32[]{:S(2)}) collective-permute-start(f32[48,128]{1,0:T(8,128)S(1)} %get-tuple-element.78.sent_first), channel_id=1, source_target_pairs={{130,132},{132,130},{131,133},{133,131},{134,136},{136,134},{135,1... | collective-permute-start | bytes 73736 | tf_op jit(solution)/shard_map/ppermute | solution.py:516
  57.7 1.9 %collective-permute-start.13 = (f32[48,128]{1,0:T(8,128)S(1)}, f32[48,128]{1,0:T(8,128)S(1)}, u32[]{:S(2)}, u32[]{:S(2)}) collective-permute-start(f32[48,128]{1,0:T(8,128)S(1)} %get-tuple-element.79.sent_second), channel_id=1, source_target_pairs={{128,130},{130,128},{129,131},{131,129},{132,134},{134,132},{133,1... | collective-permute-start | bytes 73736 | tf_op jit(solution)/shard_map/ppermute | solution.py:516
  59.6 2.1 %shard_map.110 = (f32[256,512]{1,0:T(8,128)S(1)}, f32[256,512]{1,0:T(8,128)S(1)}, f32[48,256]{1,0:T(8,128)S(1)}) custom-call(f32[256,512]{1,0:T(8,128)S(1)} %get-tuple-element.80.state, f32[256,512]{1,0:T(8,128)S(1)} %get-tuple-element.81.carry, f32[192,512]{1,0:T(8,128)S(1)} %get-tuple-element.82.force, bf16[576,256]{1,0:T(8,128)(2,1)S(1)} %get-tuple-element.83.stacks, ...), custom_call_target="tpu_custom_call" | custom-call | flops 1048576 | bytes 5775360 | tf_op jit(solution)/shard_map/pallas_call | solution.py:491
  62.2 1.2 %collective-permute-done.13.second = f32[48,128]{1,0:T(8,128)S(1)} collective-permute-done((f32[48,128]{1,0:T(8,128)S(1)}, f32[48,128]{1,0:T(8,128)S(1)}, u32[]{:S(2)}, u32[]{:S(2)}) %collective-permute-start.13) | collective-permute-done | bytes 24608 | tf_op jit(solution)/shard_map/ppermute | solution.py:516
  63.9 4.7 %collective-permute-start.14 = (f32[48,128]{1,0:T(8,128)S(1)}, f32[48,128]{1,0:T(8,128)S(1)}, u32[]{:S(2)}, u32[]{:S(2)}) collective-permute-start(f32[48,128]{1,0:T(8,128)S(1)} %get-tuple-element.85.sent_first), channel_id=1, source_target_pairs={{130,132},{132,130},{131,133},{133,131},{134,136},{136,134},{135,1... | collective-permute-start | bytes 73736 | tf_op jit(solution)/shard_map/ppermute | solution.py:516
  68.7 1.9 %collective-permute-start.15 = (f32[48,128]{1,0:T(8,128)S(1)}, f32[48,128]{1,0:T(8,128)S(1)}, u32[]{:S(2)}, u32[]{:S(2)}) collective-permute-start(f32[48,128]{1,0:T(8,128)S(1)} %get-tuple-element.86.sent_second), channel_id=1, source_target_pairs={{128,130},{130,128},{129,131},{131,129},{132,134},{134,132},{133,1... | collective-permute-start | bytes 73736 | tf_op jit(solution)/shard_map/ppermute | solution.py:516
  70.6 2.1 %shard_map.112 = (f32[256,512]{1,0:T(8,128)S(1)}, f32[256,512]{1,0:T(8,128)S(1)}, f32[48,256]{1,0:T(8,128)S(1)}) custom-call(f32[256,512]{1,0:T(8,128)S(1)} %get-tuple-element.87.state, f32[256,512]{1,0:T(8,128)S(1)} %get-tuple-element.88.carry, f32[192,512]{1,0:T(8,128)S(1)} %get-tuple-element.82.force, bf16[576,256]{1,0:T(8,128)(2,1)S(1)} %get-tuple-element.89.stacks, ...), custom_call_target="tpu_custom_call" | custom-call | flops 1048576 | bytes 5775360 | tf_op jit(solution)/shard_map/pallas_call | solution.py:491
  73.0 1.4 %collective-permute-done.15.second = f32[48,128]{1,0:T(8,128)S(1)} collective-permute-done((f32[48,128]{1,0:T(8,128)S(1)}, f32[48,128]{1,0:T(8,128)S(1)}, u32[]{:S(2)}, u32[]{:S(2)}) %collective-permute-start.15) | collective-permute-done | bytes 24608 | tf_op jit(solution)/shard_map/ppermute | solution.py:516
  74.9 4.5 %collective-permute-start.16 = (f32[48,128]{1,0:T(8,128)S(1)}, f32[48,128]{1,0:T(8,128)S(1)}, u32[]{:S(2)}, u32[]{:S(2)}) collective-permute-start(f32[48,128]{1,0:T(8,128)S(1)} %get-tuple-element.91.sent_first), channel_id=1, source_target_pairs={{130,132},{132,130},{131,133},{133,131},{134,136},{136,134},{135,1... | collective-permute-start | bytes 73736 | tf_op jit(solution)/shard_map/ppermute | solution.py:516
  79.4 1.9 %collective-permute-start.17 = (f32[48,128]{1,0:T(8,128)S(1)}, f32[48,128]{1,0:T(8,128)S(1)}, u32[]{:S(2)}, u32[]{:S(2)}) collective-permute-start(f32[48,128]{1,0:T(8,128)S(1)} %get-tuple-element.92.sent_second), channel_id=1, source_target_pairs={{128,130},{130,128},{129,131},{131,129},{132,134},{134,132},{133,1... | collective-permute-start | bytes 73736 | tf_op jit(solution)/shard_map/ppermute | solution.py:516
  81.3 1.7 %shard_map.114.ahead = f32[256,256]{1,0:T(8,128)S(1)} custom-call(f32[256,512]{1,0:T(8,128)S(1)} %get-tuple-element.94.state, f32[256,512]{1,0:T(8,128)S(1)} %get-tuple-element.95.carry, f32[192,512]{1,0:T(8,128)S(1)} %get-tuple-element.82.force, bf16[576,256]{1,0:T(8,128)(2,1)S(1)} %get-tuple-element.96.stacks, ...), custom_call_target="tpu_custom_call" | custom-call | flops 1048576 | bytes 4669440 | tf_op jit(solution)/shard_map/pallas_call | solution.py:491
  83.1 0.9 %collective-permute-done.16.first = f32[48,128]{1,0:T(8,128)S(1)} collective-permute-done((f32[48,128]{1,0:T(8,128)S(1)}, f32[48,128]{1,0:T(8,128)S(1)}, u32[]{:S(2)}, u32[]{:S(2)}) %collective-permute-start.16) | collective-permute-done | bytes 24608 | tf_op jit(solution)/shard_map/ppermute | solution.py:516
  84.0 1.2 %collective-permute-done.17.second = f32[48,128]{1,0:T(8,128)S(1)} collective-permute-done((f32[48,128]{1,0:T(8,128)S(1)}, f32[48,128]{1,0:T(8,128)S(1)}, u32[]{:S(2)}, u32[]{:S(2)}) %collective-permute-start.17) | collective-permute-done | bytes 24608 | tf_op jit(solution)/shard_map/ppermute | solution.py:516
  85.1 1.2 %shard_map.115 = f32[256,256]{1,0:T(8,128)} custom-call(f32[48,128]{1,0:T(8,128)S(1)} %collective-permute-done.16.first, f32[48,128]{1,0:T(8,128)S(1)} %collective-permute-done.17.second, f32[48,128]{1,0:T(8,128)S(1)} %get-tuple-element.91.sent_first, f32[48,128]{1,0:T(8,128)S(1)} %get-tuple-element.92.sent_second, f32[8,256]{1,0:T(8,128)S(1)} %get-tuple-element.63.kinds, ...), custom_call_target="tpu_custom_call" | custom-call | flops 1048576 | bytes 1056768 | tf_op jit(solution)/shard_map/pallas_call | solution.py:491
  (31 shorter events, 7.9 us)
Async XLA Ops:
  0.0 26.2 %copy-start.2 = (bf16[288,256]{1,0:T(8,128)(2,1)S(1)}, bf16[288,256]{1,0:T(8,128)(2,1)}, u32[]{:S(2)}) copy-start(bf16[288,256]{1,0:T(8,128)(2,1)} %constant.15.clone.trace) | copy-start | bytes 442372
  1.4 5.3 %collective-permute-start.6 = (f32[192,256]{1,0:T(8,128)S(1)}, f32[192,256]{1,0:T(8,128)S(1)}, u32[]{:S(2)}, u32[]{:S(2)}) collective-permute-start(f32[192,256]{1,0:T(8,128)S(1)} %shard_map.102), channel_id=1, source_target_pairs={{0,384},{1,385},{2,386},{3,387},{4,388},{5,389},{6,390},{7,391},{8... | collective-permute-start | bytes 589832 | tf_op jit(solution)/shard_map/ppermute | solution.py:554
  2.1 4.6 %collective-permute-start.5 = (f32[192,256]{1,0:T(8,128)S(1)}, f32[192,256]{1,0:T(8,128)S(1)}, u32[]{:S(2)}, u32[]{:S(2)}) collective-permute-start(f32[192,256]{1,0:T(8,128)S(1)} %shard_map.102), channel_id=1, source_target_pairs={{0,256},{1,257},{2,258},{3,259},{4,260},{5,261},{6,262},{7,263},{8... | collective-permute-start | bytes 589832 | tf_op jit(solution)/shard_map/ppermute | solution.py:554
  2.7 14.0 %collective-permute-start.4 = (f32[192,256]{1,0:T(8,128)S(1)}, f32[192,256]{1,0:T(8,128)S(1)}, u32[]{:S(2)}, u32[]{:S(2)}) collective-permute-start(f32[192,256]{1,0:T(8,128)S(1)} %shard_map.102), channel_id=1, source_target_pairs={{0,128},{1,129},{2,130},{3,131},{4,132},{5,133},{6,134},{7,135},{8... | collective-permute-start | bytes 589832 | tf_op jit(solution)/shard_map/ppermute | solution.py:554
  4.0 14.8 %collective-permute-start.1 = (f32[264,256]{1,0:T(8,128)S(1)}, f32[264,256]{1,0:T(8,128)S(1)}, u32[]{:S(2)}, u32[]{:S(2)}) collective-permute-start(f32[264,256]{1,0:T(8,128)S(1)} %pad_add_fusion.mine.packed), channel_id=1, source_target_pairs={{0,1},{1,0},{2,3},{3,2},{4,5},{5,4},{6,7},{7,6},{8,9},{9,8},{10,11... | collective-permute-start | bytes 811016 | tf_op jit(solution)/shard_map/ppermute | solution.py:523
  4.7 14.2 %collective-permute-start = (f32[264,256]{1,0:T(8,128)S(1)}, f32[264,256]{1,0:T(8,128)S(1)}, u32[]{:S(2)}, u32[]{:S(2)}) collective-permute-start(f32[264,256]{1,0:T(8,128)S(1)} %pad_add_fusion.mine.packed), channel_id=1, source_target_pairs={{128,129},{129,128},{130,131},{131,130},{132,133},{133,132},{134,1... | collective-permute-start | bytes 811016 | tf_op jit(solution)/shard_map/ppermute | solution.py:523
  16.9 13.3 %collective-permute-start.7 = (f32[192,256]{1,0:T(8,128)S(1)}, f32[192,256]{1,0:T(8,128)S(1)}, u32[]{:S(2)}, u32[]{:S(2)}) collective-permute-start(f32[192,256]{1,0:T(8,128)S(1)} %shard_map.103.force_mine), channel_id=1, source_target_pairs={{128,129},{129,128},{130,131},{131,130},{132,133},{133,132},{134,1... | collective-permute-start | bytes 589832 | tf_op jit(solution)/shard_map/ppermute | solution.py:523
  19.4 18.6 %copy-start = (bf16[256,576]{1,0:T(8,128)(2,1)S(1)}, bf16[256,576]{1,0:T(8,128)(2,1)}, u32[]{:S(2)}) copy-start(bf16[256,576]{1,0:T(8,128)(2,1)} %constant.16.clone.lift_two) | copy-start | bytes 884740
  19.4 18.6 %copy-start.1 = (bf16[256,768]{1,0:T(8,128)(2,1)S(1)}, bf16[256,768]{1,0:T(8,128)(2,1)}, u32[]{:S(2)}) copy-start(bf16[256,768]{1,0:T(8,128)(2,1)} %constant.14.clone.interior) | copy-start | bytes 1179652
  19.4 9.5 %collective-permute-start.2 = (f32[48,256]{1,0:T(8,128)S(1)}, f32[48,256]{1,0:T(8,128)S(1)}, u32[]{:S(2)}, u32[]{:S(2)}) collective-permute-start(f32[48,256]{1,0:T(8,128)S(1)} %get-tuple-element.51), channel_id=1, source_target_pairs={{2,4},{4,2},{3,5},{5,3},{6,8},{8,6},{7,9},{9,7},{10,12},{12,10},{1... | collective-permute-start | bytes 147464 | tf_op jit(solution)/shard_map/ppermute | solution.py:516
  24.2 6.0 %collective-permute-start.3 = (f32[48,256]{1,0:T(8,128)S(1)}, f32[48,256]{1,0:T(8,128)S(1)}, u32[]{:S(2)}, u32[]{:S(2)}) collective-permute-start(f32[48,256]{1,0:T(8,128)S(1)} %get-tuple-element.52), channel_id=1, source_target_pairs={{0,2},{2,0},{1,3},{3,1},{4,6},{6,4},{5,7},{7,5},{8,10},{10,8},{9,1... | collective-permute-start | bytes 147464 | tf_op jit(solution)/shard_map/ppermute | solution.py:516
  30.8 9.6 %collective-permute-start.8 = (f32[48,384]{1,0:T(8,128)S(1)}, f32[48,384]{1,0:T(8,128)S(1)}, u32[]{:S(2)}, u32[]{:S(2)}) collective-permute-start(f32[48,384]{1,0:T(8,128)S(1)} %get-tuple-element.58), channel_id=1, source_target_pairs={{130,132},{132,130},{131,133},{133,131},{134,136},{136,134},{135,1... | collective-permute-start | bytes 221192 | tf_op jit(solution)/shard_map/ppermute | solution.py:516
  35.3 6.2 %collective-permute-start.9 = (f32[48,384]{1,0:T(8,128)S(1)}, f32[48,384]{1,0:T(8,128)S(1)}, u32[]{:S(2)}, u32[]{:S(2)}) collective-permute-start(f32[48,384]{1,0:T(8,128)S(1)} %get-tuple-element.59), channel_id=1, source_target_pairs={{128,130},{130,128},{129,131},{131,129},{132,134},{134,132},{133,1... | collective-permute-start | bytes 221192 | tf_op jit(solution)/shard_map/ppermute | solution.py:516
  38.0 3.5 %copy-start.4 = (bf16[288,960]{1,0:T(8,128)(2,1)S(1)}, bf16[288,960]{1,0:T(8,128)(2,1)}, u32[]{:S(2)}) copy-start(bf16[288,960]{1,0:T(8,128)(2,1)} %constant.18.clone.reach_force) | copy-start | bytes 1658884
  42.2 9.0 %collective-permute-start.10 = (f32[48,128]{1,0:T(8,128)S(1)}, f32[48,128]{1,0:T(8,128)S(1)}, u32[]{:S(2)}, u32[]{:S(2)}) collective-permute-start(f32[48,128]{1,0:T(8,128)S(1)} %get-tuple-element.70.sent_first), channel_id=1, source_target_pairs={{130,132},{132,130},{131,133},{133,131},{134,136},{136,134},{135,1... | collective-permute-start | bytes 73736 | tf_op jit(solution)/shard_map/ppermute | solution.py:516
  46.9 5.7 %collective-permute-start.11 = (f32[48,128]{1,0:T(8,128)S(1)}, f32[48,128]{1,0:T(8,128)S(1)}, u32[]{:S(2)}, u32[]{:S(2)}) collective-permute-start(f32[48,128]{1,0:T(8,128)S(1)} %get-tuple-element.71.sent_second), channel_id=1, source_target_pairs={{128,130},{130,128},{129,131},{131,129},{132,134},{134,132},{133,1... | collective-permute-start | bytes 73736 | tf_op jit(solution)/shard_map/ppermute | solution.py:516
  48.8 3.8 %copy-start.3 = (bf16[288,576]{1,0:T(8,128)(2,1)S(1)}, bf16[288,576]{1,0:T(8,128)(2,1)}, u32[]{:S(2)}) copy-start(bf16[288,576]{1,0:T(8,128)(2,1)} %constant.17.clone.reach) | copy-start | bytes 995332
  53.2 9.0 %collective-permute-start.12 = (f32[48,128]{1,0:T(8,128)S(1)}, f32[48,128]{1,0:T(8,128)S(1)}, u32[]{:S(2)}, u32[]{:S(2)}) collective-permute-start(f32[48,128]{1,0:T(8,128)S(1)} %get-tuple-element.78.sent_first), channel_id=1, source_target_pairs={{130,132},{132,130},{131,133},{133,131},{134,136},{136,134},{135,1... | collective-permute-start | bytes 73736 | tf_op jit(solution)/shard_map/ppermute | solution.py:516
  57.7 5.7 %collective-permute-start.13 = (f32[48,128]{1,0:T(8,128)S(1)}, f32[48,128]{1,0:T(8,128)S(1)}, u32[]{:S(2)}, u32[]{:S(2)}) collective-permute-start(f32[48,128]{1,0:T(8,128)S(1)} %get-tuple-element.79.sent_second), channel_id=1, source_target_pairs={{128,130},{130,128},{129,131},{131,129},{132,134},{134,132},{133,1... | collective-permute-start | bytes 73736 | tf_op jit(solution)/shard_map/ppermute | solution.py:516
  63.9 9.0 %collective-permute-start.14 = (f32[48,128]{1,0:T(8,128)S(1)}, f32[48,128]{1,0:T(8,128)S(1)}, u32[]{:S(2)}, u32[]{:S(2)}) collective-permute-start(f32[48,128]{1,0:T(8,128)S(1)} %get-tuple-element.85.sent_first), channel_id=1, source_target_pairs={{130,132},{132,130},{131,133},{133,131},{134,136},{136,134},{135,1... | collective-permute-start | bytes 73736 | tf_op jit(solution)/shard_map/ppermute | solution.py:516
  68.7 5.7 %collective-permute-start.15 = (f32[48,128]{1,0:T(8,128)S(1)}, f32[48,128]{1,0:T(8,128)S(1)}, u32[]{:S(2)}, u32[]{:S(2)}) collective-permute-start(f32[48,128]{1,0:T(8,128)S(1)} %get-tuple-element.86.sent_second), channel_id=1, source_target_pairs={{128,130},{130,128},{129,131},{131,129},{132,134},{134,132},{133,1... | collective-permute-start | bytes 73736 | tf_op jit(solution)/shard_map/ppermute | solution.py:516
  74.9 9.0 %collective-permute-start.16 = (f32[48,128]{1,0:T(8,128)S(1)}, f32[48,128]{1,0:T(8,128)S(1)}, u32[]{:S(2)}, u32[]{:S(2)}) collective-permute-start(f32[48,128]{1,0:T(8,128)S(1)} %get-tuple-element.91.sent_first), channel_id=1, source_target_pairs={{130,132},{132,130},{131,133},{133,131},{134,136},{136,134},{135,1... | collective-permute-start | bytes 73736 | tf_op jit(solution)/shard_map/ppermute | solution.py:516
  79.4 5.7 %collective-permute-start.17 = (f32[48,128]{1,0:T(8,128)S(1)}, f32[48,128]{1,0:T(8,128)S(1)}, u32[]{:S(2)}, u32[]{:S(2)}) collective-permute-start(f32[48,128]{1,0:T(8,128)S(1)} %get-tuple-element.92.sent_second), channel_id=1, source_target_pairs={{128,130},{130,128},{129,131},{131,129},{132,134},{134,132},{133,1... | collective-permute-start | bytes 73736 | tf_op jit(solution)/shard_map/ppermute | solution.py:516
